TPU v7x, 32 devices: a whole 2x2x4 slice. The times are simulated.
32 devices in a mesh: seq: 8 (over z, y), tp: 4 (over x, core).
Axes of the slice: x: 2, y: 2, z: 4, core: 2. Of those that a mesh axis runs over, the one named last changes fastest.
Arguments:
- glob_out: bfloat16 [3072, 8192], P('seq', 'tp'), may hold values from -6 to 6
- byte_ids: int32 [3072, 8], P(('seq', 'tp')), may hold values from 0 to 255
- out_grad: bfloat16 [24576, 1024], P(('seq', 'tp')), may hold values from -6 to 6
- embed: bfloat16 [256, 1024], replicated, may hold values from -6 to 6
- w_proj: bfloat16 [1024, 1024], replicated, may hold values from -0.1875 to 0.1875
- norm_gain: float32 [1024], replicated, may hold values from 0.5 to 1.5
- w_qkv: bfloat16 [1024, 3072], replicated, may hold values from -0.40625 to 0.40625
- w_out: bfloat16 [1024, 1024], replicated, may hold values from -0.1875 to 0.1875
Outputs:
- glob_grad: bfloat16 [3072, 8192], P('seq', 'tp')
- grad_embed: float32 [256, 1024], P(('seq', 'tp'))
- grad_proj: float32 [1024, 1024], P(('seq', 'tp'))
- grad_gain: float32 [1024], P(('seq', 'tp'))
- grad_qkv: float32 [1024, 3072], P(('seq', 'tp'))
- grad_out: float32 [1024, 1024], P(('seq', 'tp'))
All inputs are finite; a program needn't handle non-finite values.
Results may differ from a plain program's by a relative error of at most 0.0075.
The roundings to bfloat16 on the way count: a program that leaves them out, or rounds other values in their place, can miss the bound.
Values may be sent and summed in bfloat16 or wider, within the bound.
No kernel may reach another device: no remote copies, remote signals or barrier semaphores. Data moves between devices by JAX's collectives and lax.ppermute only.
A program may use at most 192 MiB of HBM per device.

v0:
```python
import functools

import jax
import jax.numpy as jnp
from jax import lax
from jax.experimental import pallas as pl
from jax.experimental.pallas import tpu as pltpu
from jax.sharding import PartitionSpec as P

HEADS = 16
HEAD = 64
PATCH = 8
PAIR = 2 * HEAD
GROUP = 16
AXES = ("seq", "tp")
F32 = jnp.float32
BF16 = jnp.bfloat16
NN = (((1,), (0,)), ((), ()))
NT = (((1,), (1,)), ((), ()))
TN = (((0,), (0,)), ((), ()))


def dot(a, b, dims=NN):
    return lax.dot_general(a, b, dims, preferred_element_type=F32)


def cost(flops, nbytes, transcendentals=0):
    return pl.CostEstimate(
        flops=int(flops), bytes_accessed=int(nbytes), transcendentals=int(transcendentals)
    )


def bit_masks(mesh):
    seq, tp = mesh.shape["seq"], mesh.shape["tp"]
    tp_bits = [1 << b for b in range(tp.bit_length() - 1)]
    seq_bits = [tp << b for b in range(seq.bit_length() - 1)]
    return tp_bits, seq_bits


def spans(bits):
    masks = [0]
    for bit in bits:
        masks = masks + [m ^ bit for m in masks]
    return masks


def scatter_order(stages):
    order = [0]
    for bits in reversed(stages):
        order = [m ^ q for m in spans(bits) for q in order]
    return order


def exchange(block, mask, devices):
    return lax.ppermute(block, AXES, [(d, d ^ mask) for d in range(devices)])


def finish_scatter(parts, stages, devices, wire=BF16):
    for n, bits in enumerate(stages):
        masks = spans(bits)
        got = [parts[0]]
        for part, mask in zip(parts[1:], masks[1:]):
            got.append(exchange(part, mask, devices))
        last = n + 1 == len(stages)
        pieces = 1 if last else len(spans(stages[n + 1]))
        size = parts[0].shape[0] // pieces
        parts = []
        for k in reversed(range(pieces)):
            total = got[0][k * size : (k + 1) * size].astype(F32)
            for other in got[1:]:
                total = total + other[k * size : (k + 1) * size].astype(F32)
            parts.append(total if last else total.astype(wire))
        parts = parts[::-1]
    return parts[0]


def split_scatter(blocks, stages, devices, wire=BF16):
    pieces = len(spans(stages[0]))
    size = blocks.shape[0] // pieces
    parts = [blocks[k * size : (k + 1) * size] for k in range(pieces)]
    return finish_scatter(parts, stages, devices, wire)


def project_kernel(
    place, a_ref, b_ref, onehot_ref, embed_ref, w_proj_ref, gain_ref, w_qkv_ref, *rest, alias
):
    if alias:
        rest = rest[5:]
    slices_ref, normed_ref, inv_ref, act_ref, qkv_ref, x_ref = rest
    step = pl.program_id(0)
    half, width = slices_ref.shape[1], slices_ref.shape[2]
    rows = 4 * half

    @pl.when(step == 0)
    def _():
        for k, src in enumerate((a_ref, b_ref)):
            at = 2 * (place[1] ^ k)
            for h in range(2):
                slices_ref[at + h] = src[:, h * width : (h + 1) * width]
        slices = slices_ref[...].reshape(rows, width)
        onehot = onehot_ref[...].reshape(rows, onehot_ref.shape[2])
        for n in range(0, width, 256):
            x_ref[:, n : n + 256] = dot(onehot, embed_ref[:, n : n + 256]) + dot(
                slices, w_proj_ref[:, n : n + 256]
            )
        for r in range(0, rows, half):
            x = x_ref[r : r + half, :]
            inv = lax.rsqrt(jnp.mean(x * x, axis=1, keepdims=True) + 1e-05)
            normed = x * inv
            normed_ref[r // half] = normed
            inv_ref[r // half] = jnp.broadcast_to(inv, (half, 128))
            act_ref[r // half] = (normed * gain_ref[...]).astype(BF16)

    act = act_ref[...].reshape(rows, width)
    qkv_ref[...] = dot(act, w_qkv_ref[...]).astype(BF16).reshape(4, half, w_qkv_ref.shape[1])


def project(place, first, second, onehot, embed, w_proj, gain, w_qkv, earlier):
    half = onehot.shape[1]
    width = w_proj.shape[0]
    vocab = embed.shape[0]
    outs = [
        jax.ShapeDtypeStruct((PATCH, half, width), BF16),
        jax.ShapeDtypeStruct((PATCH, half, width), F32),
        jax.ShapeDtypeStruct((PATCH, half, 128), F32),
        jax.ShapeDtypeStruct((PATCH, half, width), BF16),
        jax.ShapeDtypeStruct((PATCH, half, 3 * width), BF16),
    ]
    block = 512
    if earlier is None:
        first_spec = pl.BlockSpec((half, 2 * width), lambda n, s: (s[2], 0))
    else:
        first_spec = pl.BlockSpec((half, 2 * width), lambda n, s: (0, 0))
    in_specs = [
        first_spec,
        pl.BlockSpec((half, 2 * width), lambda n, s: (0, 0)),
        pl.BlockSpec((4, half, vocab), lambda n, s: (s[0], 0, 0)),
        pl.BlockSpec((vocab, width), lambda n, s: (0, 0)),
        pl.BlockSpec((width, width), lambda n, s: (0, 0)),
        pl.BlockSpec((1, width), lambda n, s: (0, 0)),
        pl.BlockSpec((width, block), lambda n, s: (0, n)),
    ]
    args = [place, first, second, onehot, embed, w_proj, gain, w_qkv]
    aliases = {}
    if earlier is not None:
        in_specs += [pl.BlockSpec(memory_space=pl.ANY)] * 5
        args += list(earlier)
        aliases = {8 + i: i for i in range(5)}
    out_specs = [
        pl.BlockSpec((4, half, width), lambda n, s: (s[0], 0, 0)),
        pl.BlockSpec((4, half, width), lambda n, s: (s[0], 0, 0)),
        pl.BlockSpec((4, half, 128), lambda n, s: (s[0], 0, 0)),
        pl.BlockSpec((4, half, width), lambda n, s: (s[0], 0, 0)),
        pl.BlockSpec((4, half, block), lambda n, s: (s[0], 0, n)),
    ]
    return pl.pallas_call(
        functools.partial(project_kernel, alias=earlier is not None),
        grid_spec=pltpu.PrefetchScalarGridSpec(
            num_scalar_prefetch=1,
            grid=(3 * width // block,),
            in_specs=in_specs,
            out_specs=out_specs,
            scratch_shapes=[pltpu.VMEM((4 * half, width), F32)],
        ),
        out_shape=outs,
        input_output_aliases=aliases,
        cost_estimate=cost(2 * 4 * half * width * (4 * width + vocab), 16e6),
        name="project",
    )(*args)


def attention_kernel(mask_ref, q_ref, k_ref, v_ref, d_ref, context_ref, d_qkv_ref):
    scale = HEAD ** (-0.5)
    mask = mask_ref[...] > 0.5
    lane = lax.broadcasted_iota(jnp.int32, (PATCH * GROUP, PAIR), 1)
    low = lane < HEAD
    rows = PATCH * GROUP

    def block(ref, g):
        return ref[:, g * GROUP : (g + 1) * GROUP, :].reshape(rows, PAIR)

    def stack(value):
        zero = jnp.zeros_like(value)
        return jnp.concatenate([jnp.where(low, value, zero), jnp.where(low, zero, value)], axis=0)

    def merge(value):
        return jnp.where(low, value[:rows], value[rows:]).astype(BF16).reshape(PATCH, GROUP, PAIR)

    for g in range(q_ref.shape[1] // GROUP):
        at = slice(g * GROUP, (g + 1) * GROUP)
        q, k, v, d = block(q_ref, g), block(k_ref, g), block(v_ref, g), block(d_ref, g)
        q2, d2 = stack(q), stack(d)
        scores = jnp.where(mask, dot(q2, k, NT) * scale, -1e30)
        expo = jnp.exp(scores - jnp.max(scores, axis=1, keepdims=True))
        probs = expo * (1.0 / jnp.sum(expo, axis=1, keepdims=True))
        d_probs = dot(d2, v, NT)
        weighted = probs * d_probs
        d_scores = (weighted - probs * jnp.sum(weighted, axis=1, keepdims=True)) * scale
        d_scores = d_scores.astype(BF16)
        probs = probs.astype(BF16)
        context_ref[:, at, :] = merge(dot(probs, v))
        d_qkv_ref[0, :, at, :] = merge(dot(d_scores, k))
        d_qkv_ref[1, :, at, :] = dot(d_scores, q2, TN).astype(BF16).reshape(PATCH, GROUP, PAIR)
        d_qkv_ref[2, :, at, :] = dot(probs, d2, TN).astype(BF16).reshape(PATCH, GROUP, PAIR)


def attention(mask, qkv, d_context, first, count):
    half, width = d_context.shape[1], d_context.shape[2]
    pairs = width // PAIR
    spec = lambda part: pl.BlockSpec((PATCH, half, PAIR), lambda n: (0, 0, part * pairs + first + n))
    return pl.pallas_call(
        attention_kernel,
        grid=(count,),
        in_specs=[
            pl.BlockSpec(mask.shape, lambda n: (0, 0)),
            spec(0),
            spec(1),
            spec(2),
            spec(0),
        ],
        out_specs=[
            pl.BlockSpec((PATCH, half, PAIR), lambda n: (0, 0, n)),
            pl.BlockSpec((3, PATCH, half, PAIR), lambda n: (0, 0, 0, n)),
        ],
        out_shape=[
            jax.ShapeDtypeStruct((PATCH, half, count * PAIR), BF16),
            jax.ShapeDtypeStruct((3, PATCH, half, count * PAIR), BF16),
        ],
        cost_estimate=cost(count * half / GROUP * 6 * 2 * 256 * 256 * 256, count * 1.6e6),
        name="attention",
    )(mask, qkv, qkv, qkv, d_context)


def grad_kernel(place, *refs, counts, height):
    lhs, (rhs_ref, keep_ref, send_ref, acc_ref) = refs[: len(counts)], refs[len(counts) :]
    rhs = rhs_ref[...].reshape(-1, rhs_ref.shape[-1])
    base = 0
    for ref in lhs:
        tokens, cols = rhs.shape[0], ref.shape[-1]
        left = ref[...].reshape(tokens, cols)
        for m in range(0, cols, 256):
            tile = dot(left[:, m : m + 256], rhs, TN)
            for b in range(0, 256, height):
                at = pl.multiple_of(place[(base + m + b) // height] * height, height)
                acc_ref[pl.ds(at, height), :] = tile[b : b + height]
        base += cols
    half = acc_ref.shape[0] // 2
    keep_ref[...] = acc_ref[:half].astype(BF16)
    send_ref[...] = acc_ref[half:].astype(BF16)


def grad_rows(place, lhs, rhs, devices):
    rows = sum(a.shape[-1] for a in lhs)
    cols = rhs.shape[-1]
    stacked = rhs.ndim == 4
    planes = rhs.shape[0] if stacked else 1
    block = 256
    per = cols // block
    whole = lambda a: pl.BlockSpec(a.shape, lambda n, s: (0,) * a.ndim)
    if stacked:
        rhs_spec = pl.BlockSpec((1,) + rhs.shape[1:3] + (block,), lambda n, s: (n // per, 0, 0, n % per))
    else:
        rhs_spec = pl.BlockSpec(rhs.shape[:-1] + (block,), lambda n, s: (0,) * (rhs.ndim - 1) + (n,))
    tokens = rhs.shape[-2] * rhs.shape[-3]
    out = jax.ShapeDtypeStruct((rows // 2, planes * cols), BF16)
    return pl.pallas_call(
        functools.partial(grad_kernel, counts=[a.shape[-1] for a in lhs], height=rows // devices),
        grid_spec=pltpu.PrefetchScalarGridSpec(
            num_scalar_prefetch=1,
            grid=(planes * per,),
            in_specs=[whole(a) for a in lhs] + [rhs_spec],
            out_specs=[pl.BlockSpec((rows // 2, block), lambda n, s: (0, n))] * 2,
            scratch_shapes=[pltpu.VMEM((rows, block), F32)],
        ),
        out_shape=[out, out],
        cost_estimate=cost(2 * tokens * rows * planes * cols, 2 * rows * planes * cols + 4e6),
        name="grad_rows",
    )(place, *lhs, rhs)


def input_grad_kernel(*refs, chunks):
    d_refs, w_refs = refs[:chunks], refs[chunks : 2 * chunks]
    normed_ref, inv_ref, gain_ref, out_grad_ref, d_x_ref, grad_gain_ref, acc_ref = refs[2 * chunks :]
    step = pl.program_id(0)
    half, width = normed_ref.shape[1], normed_ref.shape[2]
    rows = PATCH * half
    for n in range(0, width, 256):
        total = None
        for d_ref, w_ref in zip(d_refs, w_refs):
            term = dot(d_ref[...].reshape(rows, d_ref.shape[-1]), w_ref[n : n + 256, :], NT)
            total = term if total is None else total + term

        @pl.when(step == 0)
        def _():
            acc_ref[:, n : n + 256] = total

        @pl.when(step > 0)
        def _():
            acc_ref[:, n : n + 256] += total

    @pl.when(step == pl.num_programs(0) - 1)
    def _():
        gain_total = jnp.zeros((1, width), F32)
        for j in range(PATCH):
            d_act = acc_ref[j * half : (j + 1) * half, :]
            normed = normed_ref[j]
            inv = inv_ref[j][:, :1]
            gain_total = gain_total + jnp.sum(d_act * normed, axis=0, keepdims=True)
            d_normed = d_act * gain_ref[...]
            mean = jnp.mean(d_normed * normed, axis=1, keepdims=True)
            d_x = out_grad_ref[j].astype(F32) + inv * (d_normed - normed * mean)
            d_x_ref[j] = d_x.astype(BF16)
        grad_gain_ref[...] = gain_total


def input_grad(d_qkvs, w_qkv, normed, inv, gain, out_grad):
    half, width = normed.shape[1], normed.shape[2]
    chunks = len(d_qkvs)
    cols = [d.shape[-1] for d in d_qkvs]
    d_specs, w_specs, at = [], [], 0
    for c in cols:
        d_specs.append(pl.BlockSpec((1, PATCH, half, c), lambda n: (n, 0, 0, 0)))
        w_specs.append(
            pl.BlockSpec((width, c), lambda n, c=c, at=at: (0, n * (width // c) + at // c))
        )
        at += c
    whole = lambda a: pl.BlockSpec(a.shape, lambda n: (0,) * a.ndim)
    return pl.pallas_call(
        functools.partial(input_grad_kernel, chunks=chunks),
        grid=(3,),
        in_specs=d_specs + w_specs + [whole(normed), whole(inv), whole(gain), whole(out_grad)],
        out_specs=[
            pl.BlockSpec((PATCH, half, width), lambda n: (0, 0, 0)),
            pl.BlockSpec((1, width), lambda n: (0, 0)),
        ],
        out_shape=[
            jax.ShapeDtypeStruct((PATCH, half, width), BF16),
            jax.ShapeDtypeStruct((1, width), F32),
        ],
        scratch_shapes=[pltpu.VMEM((PATCH * half, width), F32)],
        cost_estimate=cost(2 * PATCH * half * width * 3 * width, 20e6),
        name="input_grad",
    )(*d_qkvs, *([w_qkv] * chunks), normed, inv, gain, out_grad)


def back_kernel(place, d_x_ref, w_ref, *outs):
    half, width = d_x_ref.shape[1], d_x_ref.shape[2]
    for k, out in enumerate(outs):
        at = 2 * (place[2] ^ k)
        left = d_x_ref[pl.ds(at, 2)].reshape(2 * half, width)
        for n in range(0, width, 256):
            got = dot(left, w_ref[n : n + 256, :], NT).astype(BF16)
            out[:, n : n + 256] = got[:half]
            out[:, width + n : width + n + 256] = got[half:]


def back(place, d_x, w_proj, tp):
    half, width = d_x.shape[1], d_x.shape[2]
    whole = lambda a: pl.BlockSpec(a.shape, lambda n, s: (0,) * a.ndim)
    out = jax.ShapeDtypeStruct((half, 2 * width), BF16)
    return pl.pallas_call(
        back_kernel,
        grid_spec=pltpu.PrefetchScalarGridSpec(
            num_scalar_prefetch=1,
            grid=(1,),
            in_specs=[whole(d_x), whole(w_proj)],
            out_specs=[whole(out)] * tp,
        ),
        out_shape=[out] * tp,
        cost_estimate=cost(2 * PATCH * half * width * width, 6e6),
        name="back",
    )(place, d_x, w_proj)


def on_device(mesh, glob_out, byte_ids, out_grad, embed, w_proj, norm_gain, w_qkv, w_out):
    vocab, width = embed.shape
    tp, devices = mesh.shape["tp"], mesh.size
    half = byte_ids.shape[0]
    t = lax.axis_index("tp").astype(jnp.int32)
    me = lax.axis_index("seq").astype(jnp.int32) * tp + t
    tp_bits, seq_bits = bit_masks(mesh)
    core, wide = tp_bits[:1], tp_bits[1:]
    xy = [core, wide, seq_bits[:1], seq_bits[1:]]
    yx = [core, seq_bits[:1], wide, seq_bits[1:]]

    arrived = {}
    for k in range(1, tp):
        block = lax.dynamic_slice(glob_out, ((t ^ k) * half, 0), (half, glob_out.shape[1]))
        arrived[k] = exchange(block, k, devices)

    onehot = (byte_ids.T[:, :, None] == jnp.arange(vocab, dtype=jnp.int32)).astype(BF16)
    grads = out_grad.reshape(half, PATCH, width).transpose(1, 0, 2)
    d_context = lax.dot_general(
        grads, w_out, (((2,), (1,)), ((), ())), preferred_element_type=F32
    ).astype(BF16)
    gain = norm_gain.reshape(1, width)

    place = jnp.stack([t >> 1, t & 1, t])
    early = project(place, glob_out, arrived[1], onehot, embed, w_proj, gain, w_qkv, None)
    place = jnp.stack([(t >> 1) ^ 1, t & 1, t])
    slices, normed, inv, act, qkv = project(
        place, arrived[2], arrived[3], onehot, embed, w_proj, gain, w_qkv, early
    )

    row = jnp.arange(2 * PATCH * GROUP)[:, None] % (PATCH * GROUP)
    col = jnp.arange(PATCH * GROUP)[None, :]
    mask = ((row % GROUP == col % GROUP) & (row // GROUP >= col // GROUP)).astype(F32)

    def positions(stages):
        order = scatter_order(stages)
        where = [0] * devices
        for p, q in enumerate(order):
            where[q] = p
        table = jnp.array(where, dtype=jnp.int32)
        return table[jnp.arange(devices, dtype=jnp.int32) ^ me]

    at_xy, at_yx = positions(xy), positions(yx)

    pairs = width // PAIR
    splits = 2
    contexts, d_qkvs, qkv_parts = [], [], []
    for c in range(splits):
        count = pairs // splits
        context, d_qkv = attention(mask, qkv, d_context, c * count, count)
        contexts.append(context)
        d_qkvs.append(d_qkv)
        stages, at = ((xy, at_xy), (yx, at_yx))[c % 2]
        pieces = grad_rows(at, [act], d_qkv, devices)
        qkv_parts.append(finish_scatter(list(pieces), stages, devices))
    grad_out = finish_scatter(list(grad_rows(at_xy, contexts, grads, devices)), xy, devices)

    d_x, grad_gain = input_grad(d_qkvs, w_qkv, normed, inv, gain, grads)
    grad_proj = finish_scatter(list(grad_rows(at_yx, [slices], d_x, devices)), yx, devices)

    own = jnp.stack([t >> 1, t & 1, t])
    rows = back(own, d_x, w_proj, tp)
    glob_grad = jnp.zeros((tp * half, 2 * width), BF16)
    for k in range(tp):
        piece = rows[k] if k == 0 else exchange(rows[k], k, devices)
        glob_grad = lax.dynamic_update_slice(glob_grad, piece, ((t ^ k) * half, 0))

    height = vocab // devices
    owner = (byte_ids.T // height) ^ me
    spot = jnp.zeros_like(owner)
    order = scatter_order(yx)
    for bit in range(devices.bit_length() - 1):
        spot = spot + ((owner >> bit) & 1) * order.index(1 << bit)
    spot = spot * height + byte_ids.T % height
    marks = (spot[:, :, None] == jnp.arange(vocab, dtype=jnp.int32)).astype(BF16)
    grad_embed = lax.dot_general(
        marks, d_x, (((0, 1), (0, 1)), ((), ())), preferred_element_type=F32
    ).astype(BF16)
    grad_embed = split_scatter(grad_embed, yx, devices)

    blocks = grad_gain.reshape(devices, width // devices)
    blocks = blocks[jnp.array(scatter_order(yx), dtype=jnp.int32) ^ me]
    grad_gain = split_scatter(blocks, yx, devices, F32).reshape(-1)

    third = width // splits
    grad_qkv = jnp.concatenate(
        [part[:, n * third : (n + 1) * third] for n in range(3) for part in qkv_parts], axis=1
    )
    return (glob_grad, grad_embed, grad_proj, grad_gain, grad_qkv, grad_out)


def solution(mesh):
    return jax.shard_map(
        functools.partial(on_device, mesh),
        mesh=mesh,
        in_specs=(
            P("seq", "tp"),
            P(AXES, None),
            P(AXES, None),
            P(),
            P(),
            P(),
            P(),
            P(),
        ),
        out_specs=(
            P("seq", "tp"),
            P(AXES, None),
            P(AXES, None),
            P(AXES),
            P(AXES, None),
            P(AXES, None),
        ),
        check_vma=False,
    )
```

profile of v0, /device:TPU:0, one launch (start us, length us, event | category | flops | bytes accessed | tf_op | source)
XLA Modules:
  0.0 245.5 jit_solution(16688680778001120823)
XLA Ops:
  5.4 4.9 %fusion.2.d_ref = bf16[8,96,1024]{2,1,0:T(8,128)(2,1)} fusion(bf16[1024,1024]{1,0:T(8,128)(2,1)S(1)} %copy-done, bf16[96,8,1024]{2,1,0:T(8,128)(2,1)} %bitcast.28), kind=kOutput, calls=%fused_computation.5 | convolution fusion | flops 1611399168 | bytes 5242880 | tf_op jit(solution)/shard_map/dot_general | solution.py:393
  11.7 3.4 %copy.25 = bf16[96,8,1024]{2,0,1:T(8,128)(2,1)} copy(bf16[96,8,1024]{2,1,0:T(8,128)(2,1)} %bitcast.29) | data formatting | bytes 3145728 | tf_op jit(solution)/shard_map/reshape | solution.py:392
  19.1 11.5 %project.2 = (bf16[8,96,1024]{2,1,0:T(8,128)(2,1)}, f32[8,96,1024]{2,1,0:T(8,128)}, f32[8,96,128]{2,1,0:T(8,128)}, bf16[8,96,1024]{2,1,0:T(8,128)(2,1)}, bf16[8,96,3072]{2,1,0:T(8,128)(2,1)}) custom-call(s32[3]{0:T(128)} %add_add_fusion.place, bf16[384,2048]{1,0:T(8,128)(2,1)} %a_ref.1, bf16[96,2048]{1,0:T(8,128)(2,1)} %collective-permute-done.2.b_ref, ...), custom_call_target="tpu_custom_call" | custom-call | flops 3422552064 | bytes 16000000 | tf_op jit(solution)/shard_map/project/pallas_call | solution.py:156
  30.7 11.1 %project.3 = (bf16[8,96,1024]{2,1,0:T(8,128)(2,1)}, f32[8,96,1024]{2,1,0:T(8,128)}, f32[8,96,128]{2,1,0:T(8,128)}, bf16[8,96,1024]{2,1,0:T(8,128)(2,1)}, bf16[8,96,3072]{2,1,0:T(8,128)(2,1)}) custom-call(s32[3]{0:T(128)} %add_add_fusion.1.place, ...), custom_call_target="tpu_custom_call", output_to_operand_aliasing={{0}: (8, {}), {1}: (9, {}), {2}: (10, {}), {3}: (11, {}), {... | custom-call | flops 3422552064 | bytes 16000000 | tf_op jit(solution)/shard_map/project/pallas_call | solution.py:156
  41.8 14.4 %attention.3 = (bf16[8,96,512]{2,1,0:T(8,128)(2,1)}, bf16[3,8,96,512]{3,2,1,0:T(8,128)(2,1)}) custom-call(f32[256,128]{1,0:T(8,128)} %and_convert_fusion.mask_ref, bf16[8,96,3072]{2,1,0:T(8,128)(2,1)} %get-tuple-element.39.q_ref.k_ref.v_ref, bf16[8,96,3072]{2,1,0:T(8,128)(2,1)} %get-tuple-element.39.q_ref.k_ref.v_ref, ...), custom_call_target="tpu_custom_call" | custom-call | flops 4831838208 | bytes 6400000 | tf_op jit(solution)/shard_map/attention/pallas_call | solution.py:211
  56.2 14.4 %attention.2 = (bf16[8,96,512]{2,1,0:T(8,128)(2,1)}, bf16[3,8,96,512]{3,2,1,0:T(8,128)(2,1)}) custom-call(f32[256,128]{1,0:T(8,128)} %and_convert_fusion.mask_ref, bf16[8,96,3072]{2,1,0:T(8,128)(2,1)} %get-tuple-element.39.q_ref.k_ref.v_ref, bf16[8,96,3072]{2,1,0:T(8,128)(2,1)} %get-tuple-element.39.q_ref.k_ref.v_ref, ...), custom_call_target="tpu_custom_call" | custom-call | flops 4831838208 | bytes 6400000 | tf_op jit(solution)/shard_map/attention/pallas_call | solution.py:211
  70.6 6.2 %grad_rows.7 = (bf16[512,1024]{1,0:T(8,128)(2,1)}, bf16[512,1024]{1,0:T(8,128)(2,1)}) custom-call(s32[32]{0:T(128)} %gather_fusion.2, bf16[8,96,512]{2,1,0:T(8,128)(2,1)} %get-tuple-element.58.refs_0_, bf16[8,96,512]{2,1,0:T(8,128)(2,1)} %get-tuple-element.59.refs_1_, bf16[8,96,1024]{2,1,0:T(8,128)(2,1)} %bitcast.26), custom_call_target="tpu_custom_call" | custom-call | flops 1610612736 | bytes 6097152 | tf_op jit(solution)/shard_map/grad_rows/pallas_call | solution.py:266
  77.0 8.2 %grad_rows.6 = (bf16[512,1536]{1,0:T(8,128)(2,1)}, bf16[512,1536]{1,0:T(8,128)(2,1)}) custom-call(s32[32]{0:T(128)} %gather_fusion, bf16[8,96,1024]{2,1,0:T(8,128)(2,1)} %get-tuple-element.53.refs_0_, bf16[3,8,96,512]{3,2,1,0:T(8,128)(2,1)} %get-tuple-element.41.refs_1_), custom_call_target="tpu_custom_call" | custom-call | flops 2415919104 | bytes 7145728 | tf_op jit(solution)/shard_map/grad_rows/pallas_call | solution.py:266
  85.5 19.4 %input_grad.1 = (bf16[8,96,1024]{2,1,0:T(8,128)(2,1)}, f32[1,1024]{1,0:T(1,128)}) custom-call(bf16[3,8,96,512]{3,2,1,0:T(8,128)(2,1)} %get-tuple-element.40.refs_0_.refs_1_, bf16[3,8,96,512]{3,2,1,0:T(8,128)(2,1)} %get-tuple-element.41.refs_1_, bf16[1024,3072]{1,0:T(8,128)(2,1)} %refs_3_.1, bf16[1024,3072]{1,0:T(8,128)(2,1)} %refs_3_.1, ...), custom_call_target="tpu_custom_call" | custom-call | flops 4831838208 | bytes 20000000 | tf_op jit(solution)/shard_map/input_grad/pallas_call | solution.py:328
  107.6 6.4 %back.1 = (bf16[96,2048]{1,0:T(8,128)(2,1)}, bf16[96,2048]{1,0:T(8,128)(2,1)}, bf16[96,2048]{1,0:T(8,128)(2,1)}, bf16[96,2048]{1,0:T(8,128)(2,1)}) custom-call(s32[3]{0:T(128)} %add_add_fusion.place, bf16[8,96,1024]{2,1,0:T(8,128)(2,1)} %get-tuple-element.44.d_x_ref.refs_1_, bf16[1024,1024]{1,0:T(8,128)(2,1)} %w_ref.1), custom_call_target="tpu_custom_call" | custom-call | flops 1610612736 | bytes 6000000 | tf_op jit(solution)/shard_map/back/pallas_call | solution.py:361
  114.0 6.3 %grad_rows.4 = (bf16[512,1024]{1,0:T(8,128)(2,1)}, bf16[512,1024]{1,0:T(8,128)(2,1)}) custom-call(s32[32]{0:T(128)} %gather_fusion, bf16[8,96,1024]{2,1,0:T(8,128)(2,1)} %get-tuple-element.49.refs_0_, bf16[8,96,1024]{2,1,0:T(8,128)(2,1)} %get-tuple-element.44.d_x_ref.refs_1_), custom_call_target="tpu_custom_call" | custom-call | flops 1610612736 | bytes 6097152 | tf_op jit(solution)/shard_map/grad_rows/pallas_call | solution.py:266
  129.3 8.2 %grad_rows.5 = (bf16[512,1536]{1,0:T(8,128)(2,1)}, bf16[512,1536]{1,0:T(8,128)(2,1)}) custom-call(s32[32]{0:T(128)} %gather_fusion.2, bf16[8,96,1024]{2,1,0:T(8,128)(2,1)} %get-tuple-element.53.refs_0_, bf16[3,8,96,512]{3,2,1,0:T(8,128)(2,1)} %get-tuple-element.40.refs_0_.refs_1_), custom_call_target="tpu_custom_call" | custom-call | flops 2415919104 | bytes 7145728 | tf_op jit(solution)/shard_map/grad_rows/pallas_call | solution.py:266
  141.8 2.9 %collective-permute-start.23 = (f32[1,32]{1,0:T(1,128)S(1)}, f32[1,32]{1,0:T(1,128)S(1)}, u32[]{:S(2)}, u32[]{:S(2)}) collective-permute-start(f32[1,32]{1,0:T(1,128)S(1)} %get-tuple-element.105), channel_id=1, source_target_pairs={{0,24},{1,25},{2,26},{3,27},{4,28},{5,29},{6,30},{7,31},{8,16},{9,... | collective-permute-start | bytes 392 | tf_op jit(solution)/shard_map/ppermute | solution.py:55
  149.3 2.9 %collective-permute-done.7 = bf16[64,1024]{1,0:T(8,128)(2,1)S(1)} collective-permute-done((bf16[64,1024]{1,0:T(8,128)(2,1)S(1)}, bf16[64,1024]{1,0:T(8,128)(2,1)S(1)}, u32[]{:S(2)}, u32[]{:S(2)}) %collective-permute-start.7) | collective-permute-done | bytes 131104 | tf_op jit(solution)/shard_map/ppermute | solution.py:55
  153.0 8.1 %collective-permute-done.4 = bf16[96,2048]{1,0:T(8,128)(2,1)S(1)} collective-permute-done((bf16[96,2048]{1,0:T(8,128)(2,1)}, bf16[96,2048]{1,0:T(8,128)(2,1)S(1)}, u32[]{:S(2)}, u32[]{:S(2)}) %collective-permute-start.4) | collective-permute-done | bytes 393248 | tf_op jit(solution)/shard_map/ppermute | solution.py:55
  161.6 3.7 %collective-permute-done.8 = bf16[32,1024]{1,0:T(8,128)(2,1)S(1)} collective-permute-done((bf16[32,1024]{1,0:T(8,128)(2,1)S(1)}, bf16[32,1024]{1,0:T(8,128)(2,1)S(1)}, u32[]{:S(2)}, u32[]{:S(2)}) %collective-permute-start.8) | collective-permute-done | bytes 65568 | tf_op jit(solution)/shard_map/ppermute | solution.py:55
  166.6 9.3 %collective-permute-done.5 = bf16[96,2048]{1,0:T(8,128)(2,1)S(1)} collective-permute-done((bf16[96,2048]{1,0:T(8,128)(2,1)S(1)}, bf16[96,2048]{1,0:T(8,128)(2,1)S(1)}, u32[]{:S(2)}, u32[]{:S(2)}) %collective-permute-start.5) | collective-permute-done | bytes 393248 | tf_op jit(solution)/shard_map/ppermute | solution.py:55
  175.8 2.8 %collective-permute-start.11 = (bf16[8,1024]{1,0:T(8,128)(2,1)S(1)}, bf16[8,1024]{1,0:T(8,128)(2,1)S(1)}, u32[]{:S(2)}, u32[]{:S(2)}) collective-permute-start(bf16[8,1024]{1,0:T(8,128)(2,1)S(1)} %get-tuple-element.98), channel_id=1, source_target_pairs={{0,24},{1,25},{2,26},{3,27},{4,28},{5,29},{6,30},{7,31},{8,16},{9,... | collective-permute-start | bytes 49160 | tf_op jit(solution)/shard_map/ppermute | solution.py:55
  186.0 5.9 %collective-permute-done.37 = bf16[256,1024]{1,0:T(8,128)(2,1)S(1)} collective-permute-done((bf16[256,1024]{1,0:T(8,128)(2,1)S(1)}, bf16[256,1024]{1,0:T(8,128)(2,1)S(1)}, u32[]{:S(2)}, u32[]{:S(2)}) %collective-permute-start.37) | collective-permute-done | bytes 524320 | tf_op jit(solution)/shard_map/ppermute | solution.py:55
  193.7 2.8 %collective-permute-done.13 = bf16[256,1024]{1,0:T(8,128)(2,1)S(1)} collective-permute-done((bf16[256,1024]{1,0:T(8,128)(2,1)S(1)}, bf16[256,1024]{1,0:T(8,128)(2,1)S(1)}, u32[]{:S(2)}, u32[]{:S(2)}) %collective-permute-start.13) | collective-permute-done | bytes 524320 | tf_op jit(solution)/shard_map/ppermute | solution.py:55
  209.1 3.5 %collective-permute-done.40 = bf16[32,1024]{1,0:T(8,128)(2,1)S(1)} collective-permute-done((bf16[32,1024]{1,0:T(8,128)(2,1)S(1)}, bf16[32,1024]{1,0:T(8,128)(2,1)S(1)}, u32[]{:S(2)}, u32[]{:S(2)}) %collective-permute-start.40) | collective-permute-done | bytes 65568 | tf_op jit(solution)/shard_map/ppermute | solution.py:55
  214.6 3.2 %collective-permute-done.16 = bf16[32,1024]{1,0:T(8,128)(2,1)S(1)} collective-permute-done((bf16[32,1024]{1,0:T(8,128)(2,1)S(1)}, bf16[32,1024]{1,0:T(8,128)(2,1)S(1)}, u32[]{:S(2)}, u32[]{:S(2)}) %collective-permute-start.16) | collective-permute-done | bytes 65568 | tf_op jit(solution)/shard_map/ppermute | solution.py:55
  222.2 6.4 %collective-permute-done.26 = bf16[128,1536]{1,0:T(8,128)(2,1)S(1)} collective-permute-done((bf16[128,1536]{1,0:T(8,128)(2,1)S(1)}, bf16[128,1536]{1,0:T(8,128)(2,1)S(1)}, u32[]{:S(2)}, u32[]{:S(2)}) %collective-permute-start.26) | collective-permute-done | bytes 393248 | tf_op jit(solution)/shard_map/ppermute | solution.py:55
  237.7 4.8 %collective-permute-done.28 = bf16[32,1536]{1,0:T(8,128)(2,1)S(1)} collective-permute-done((bf16[32,1536]{1,0:T(8,128)(2,1)S(1)}, bf16[32,1536]{1,0:T(8,128)(2,1)S(1)}, u32[]{:S(2)}, u32[]{:S(2)}) %collective-permute-start.28) | collective-permute-done | bytes 98336 | tf_op jit(solution)/shard_map/ppermute | solution.py:55
  (156 shorter events, 73.7 us)
Async XLA Ops:
  2.2 17.0 %collective-permute-start.2 = (bf16[96,2048]{1,0:T(8,128)(2,1)S(1)}, bf16[96,2048]{1,0:T(8,128)(2,1)}, u32[]{:S(2)}, u32[]{:S(2)}) collective-permute-start(bf16[96,2048]{1,0:T(8,128)(2,1)S(1)} %get-tuple-element.74), channel_id=1, source_target_pairs={{0,1},{1,0},{2,3},{3,2},{4,5},{5,4},{6,7},{7,6},{8,9},{9,8},{10,11... | collective-permute-start | bytes 1179656 | tf_op jit(solution)/shard_map/ppermute | solution.py:55
  2.7 28.0 %collective-permute-start = (bf16[96,2048]{1,0:T(8,128)(2,1)S(1)}, bf16[96,2048]{1,0:T(8,128)(2,1)}, u32[]{:S(2)}, u32[]{:S(2)}) collective-permute-start(bf16[96,2048]{1,0:T(8,128)(2,1)S(1)} %get-tuple-element.76), channel_id=1, source_target_pairs={{0,2},{1,3},{2,0},{3,1},{4,6},{5,7},{6,4},{7,5},{8,10},{9,11},{10,... | collective-permute-start | bytes 1179656 | tf_op jit(solution)/shard_map/ppermute | solution.py:55
  5.3 25.4 %collective-permute-start.1 = (bf16[96,2048]{1,0:T(8,128)(2,1)S(1)}, bf16[96,2048]{1,0:T(8,128)(2,1)}, u32[]{:S(2)}, u32[]{:S(2)}) collective-permute-start(bf16[96,2048]{1,0:T(8,128)(2,1)S(1)} %get-tuple-element.75), channel_id=1, source_target_pairs={{0,3},{1,2},{2,1},{3,0},{4,7},{5,6},{6,5},{7,4},{8,11},{9,10},{10,... | collective-permute-start | bytes 1179656 | tf_op jit(solution)/shard_map/ppermute | solution.py:55
  76.8 88.5 %collective-permute-start.36 = (bf16[512,1024]{1,0:T(8,128)(2,1)}, bf16[512,1024]{1,0:T(8,128)(2,1)S(1)}, u32[]{:S(2)}, u32[]{:S(2)}) collective-permute-start(bf16[512,1024]{1,0:T(8,128)(2,1)} %get-tuple-element.61), channel_id=1, source_target_pairs={{0,1},{1,0},{2,3},{3,2},{4,5},{5,4},{6,7},{7,6},{8,9},{9,8},{10,11... | collective-permute-start | bytes 3145736 | tf_op jit(solution)/shard_map/ppermute | solution.py:55
  85.2 111.6 %collective-permute-start.30 = (bf16[512,1536]{1,0:T(8,128)(2,1)}, bf16[512,1536]{1,0:T(8,128)(2,1)}, u32[]{:S(2)}, u32[]{:S(2)}) collective-permute-start(bf16[512,1536]{1,0:T(8,128)(2,1)} %get-tuple-element.57), channel_id=1, source_target_pairs={{0,1},{1,0},{2,3},{3,2},{4,5},{5,4},{6,7},{7,6},{8,9},{9,8},{10,11... | collective-permute-start | bytes 4718600 | tf_op jit(solution)/shard_map/ppermute | solution.py:55
  107.4 16.3 %collective-permute-start.18 = (f32[16,32]{1,0:T(8,128)S(1)}, f32[16,32]{1,0:T(8,128)S(1)}, u32[]{:S(2)}, u32[]{:S(2)}) collective-permute-start(f32[16,32]{1,0:T(8,128)S(1)} %slice.460), channel_id=1, source_target_pairs={{0,1},{1,0},{2,3},{3,2},{4,5},{5,4},{6,7},{7,6},{8,9},{9,8},{10,11... | collective-permute-start | bytes 6152 | tf_op jit(solution)/shard_map/ppermute | solution.py:55
  120.3 58.2 %collective-permute-start.12 = (bf16[512,1024]{1,0:T(8,128)(2,1)}, bf16[512,1024]{1,0:T(8,128)(2,1)}, u32[]{:S(2)}, u32[]{:S(2)}) collective-permute-start(bf16[512,1024]{1,0:T(8,128)(2,1)} %get-tuple-element.51), channel_id=1, source_target_pairs={{0,1},{1,0},{2,3},{3,2},{4,5},{5,4},{6,7},{7,6},{8,9},{9,8},{10,11... | collective-permute-start | bytes 3145736 | tf_op jit(solution)/shard_map/ppermute | solution.py:55
  123.6 15.6 %collective-permute-start.6 = (bf16[128,1024]{1,0:T(8,128)(2,1)}, bf16[128,1024]{1,0:T(8,128)(2,1)S(1)}, u32[]{:S(2)}, u32[]{:S(2)}) collective-permute-start(bf16[128,1024]{1,0:T(8,128)(2,1)} %slice.429), channel_id=1, source_target_pairs={{0,1},{1,0},{2,3},{3,2},{4,5},{5,4},{6,7},{7,6},{8,9},{9,8},{10,11... | collective-permute-start | bytes 786440 | tf_op jit(solution)/shard_map/ppermute | solution.py:55
  127.4 10.1 %collective-permute-start.20 = (f32[4,32]{1,0:T(4,128)S(1)}, f32[4,32]{1,0:T(4,128)S(1)}, u32[]{:S(2)}, u32[]{:S(2)}) collective-permute-start(f32[4,32]{1,0:T(4,128)S(1)} %get-tuple-element.103), channel_id=1, source_target_pairs={{0,2},{1,3},{2,0},{3,1},{4,6},{5,7},{6,4},{7,5},{8,10},{9,11},{10,... | collective-permute-start | bytes 1544 | tf_op jit(solution)/shard_map/ppermute | solution.py:55
  152.8 47.4 %collective-permute-start.24 = (bf16[512,1536]{1,0:T(8,128)(2,1)}, bf16[512,1536]{1,0:T(8,128)(2,1)S(1)}, u32[]{:S(2)}, u32[]{:S(2)}) collective-permute-start(bf16[512,1536]{1,0:T(8,128)(2,1)} %get-tuple-element.55), channel_id=1, source_target_pairs={{0,1},{1,0},{2,3},{3,2},{4,5},{5,4},{6,7},{7,6},{8,9},{9,8},{10,11... | collective-permute-start | bytes 4718600 | tf_op jit(solution)/shard_map/ppermute | solution.py:55
  165.3 10.5 %collective-permute-start.5 = (bf16[96,2048]{1,0:T(8,128)(2,1)S(1)}, bf16[96,2048]{1,0:T(8,128)(2,1)S(1)}, u32[]{:S(2)}, u32[]{:S(2)}) collective-permute-start(bf16[96,2048]{1,0:T(8,128)(2,1)S(1)} %copy-done.12), channel_id=1, source_target_pairs={{0,3},{1,2},{2,1},{3,0},{4,7},{5,6},{6,5},{7,4},{8,11},{9,10},{10,... | collective-permute-start | bytes 1179656 | tf_op jit(solution)/shard_map/ppermute | solution.py:55
  165.3 16.2 %collective-permute-start.10 = (bf16[8,1024]{1,0:T(8,128)(2,1)S(1)}, bf16[8,1024]{1,0:T(8,128)(2,1)S(1)}, u32[]{:S(2)}, u32[]{:S(2)}) collective-permute-start(bf16[8,1024]{1,0:T(8,128)(2,1)S(1)} %get-tuple-element.99), channel_id=1, source_target_pairs={{0,16},{1,17},{2,18},{3,19},{4,20},{5,21},{6,22},{7,23},{8,24},{9,... | collective-permute-start | bytes 49160 | tf_op jit(solution)/shard_map/ppermute | solution.py:55
  178.6 13.3 %collective-permute-start.37 = (bf16[256,1024]{1,0:T(8,128)(2,1)S(1)}, bf16[256,1024]{1,0:T(8,128)(2,1)S(1)}, u32[]{:S(2)}, u32[]{:S(2)}) collective-permute-start(bf16[256,1024]{1,0:T(8,128)(2,1)S(1)} %get-tuple-element.67), channel_id=1, source_target_pairs={{0,2},{1,3},{2,0},{3,1},{4,6},{5,7},{6,4},{7,5},{8,10},{9,11},{10,... | collective-permute-start | bytes 1572872 | tf_op jit(solution)/shard_map/ppermute | solution.py:55
  181.6 14.9 %collective-permute-start.13 = (bf16[256,1024]{1,0:T(8,128)(2,1)S(1)}, bf16[256,1024]{1,0:T(8,128)(2,1)S(1)}, u32[]{:S(2)}, u32[]{:S(2)}) collective-permute-start(bf16[256,1024]{1,0:T(8,128)(2,1)S(1)} %get-tuple-element.69), channel_id=1, source_target_pairs={{0,4},{1,5},{2,6},{3,7},{4,0},{5,1},{6,2},{7,3},{8,12},{9,13},{10,... | collective-permute-start | bytes 1572872 | tf_op jit(solution)/shard_map/ppermute | solution.py:55
  192.1 10.6 %collective-permute-start.38 = (bf16[128,1024]{1,0:T(8,128)(2,1)S(1)}, bf16[128,1024]{1,0:T(8,128)(2,1)S(1)}, u32[]{:S(2)}, u32[]{:S(2)}) collective-permute-start(bf16[128,1024]{1,0:T(8,128)(2,1)S(1)} %get-tuple-element.78), channel_id=1, source_target_pairs={{0,4},{1,5},{2,6},{3,7},{4,0},{5,1},{6,2},{7,3},{8,12},{9,13},{10,... | collective-permute-start | bytes 786440 | tf_op jit(solution)/shard_map/ppermute | solution.py:55
  196.7 9.2 %collective-permute-start.14 = (bf16[128,1024]{1,0:T(8,128)(2,1)S(1)}, bf16[128,1024]{1,0:T(8,128)(2,1)S(1)}, u32[]{:S(2)}, u32[]{:S(2)}) collective-permute-start(bf16[128,1024]{1,0:T(8,128)(2,1)S(1)} %get-tuple-element.80), channel_id=1, source_target_pairs={{0,2},{1,3},{2,0},{3,1},{4,6},{5,7},{6,4},{7,5},{8,10},{9,11},{10,... | collective-permute-start | bytes 786440 | tf_op jit(solution)/shard_map/ppermute | solution.py:55
  198.7 22.4 %collective-permute-start.31 = (bf16[256,1536]{1,0:T(8,128)(2,1)S(1)}, bf16[256,1536]{1,0:T(8,128)(2,1)S(1)}, u32[]{:S(2)}, u32[]{:S(2)}) collective-permute-start(bf16[256,1536]{1,0:T(8,128)(2,1)S(1)} %get-tuple-element.63), channel_id=1, source_target_pairs={{0,4},{1,5},{2,6},{3,7},{4,0},{5,1},{6,2},{7,3},{8,12},{9,13},{10,... | collective-permute-start | bytes 2359304 | tf_op jit(solution)/shard_map/ppermute | solution.py:55
  200.7 19.3 %collective-permute-start.25 = (bf16[256,1536]{1,0:T(8,128)(2,1)S(1)}, bf16[256,1536]{1,0:T(8,128)(2,1)S(1)}, u32[]{:S(2)}, u32[]{:S(2)}) collective-permute-start(bf16[256,1536]{1,0:T(8,128)(2,1)S(1)} %get-tuple-element.65), channel_id=1, source_target_pairs={{0,2},{1,3},{2,0},{3,1},{4,6},{5,7},{6,4},{7,5},{8,10},{9,11},{10,... | collective-permute-start | bytes 2359304 | tf_op jit(solution)/shard_map/ppermute | solution.py:55
  221.3 11.8 %collective-permute-start.32 = (bf16[128,1536]{1,0:T(8,128)(2,1)S(1)}, bf16[128,1536]{1,0:T(8,128)(2,1)S(1)}, u32[]{:S(2)}, u32[]{:S(2)}) collective-permute-start(bf16[128,1536]{1,0:T(8,128)(2,1)S(1)} %get-tuple-element.71), channel_id=1, source_target_pairs={{0,2},{1,3},{2,0},{3,1},{4,6},{5,7},{6,4},{7,5},{8,10},{9,11},{10,... | collective-permute-start | bytes 1179656 | tf_op jit(solution)/shard_map/ppermute | solution.py:55
  229.6 12.9 %collective-permute-start.28 = (bf16[32,1536]{1,0:T(8,128)(2,1)S(1)}, bf16[32,1536]{1,0:T(8,128)(2,1)S(1)}, u32[]{:S(2)}, u32[]{:S(2)}) collective-permute-start(bf16[32,1536]{1,0:T(8,128)(2,1)S(1)} %get-tuple-element.86), channel_id=1, source_target_pairs={{0,16},{1,17},{2,18},{3,19},{4,20},{5,21},{6,22},{7,23},{8,24},{9,... | collective-permute-start | bytes 294920 | tf_op jit(solution)/shard_map/ppermute | solution.py:55
  230.5 11.9 %collective-permute-start.29 = (bf16[32,1536]{1,0:T(8,128)(2,1)S(1)}, bf16[32,1536]{1,0:T(8,128)(2,1)S(1)}, u32[]{:S(2)}, u32[]{:S(2)}) collective-permute-start(bf16[32,1536]{1,0:T(8,128)(2,1)S(1)} %get-tuple-element.85), channel_id=1, source_target_pairs={{0,24},{1,25},{2,26},{3,27},{4,28},{5,29},{6,30},{7,31},{8,16},{9,... | collective-permute-start | bytes 294920 | tf_op jit(solution)/shard_map/ppermute | solution.py:55
  233.2 9.3 %collective-permute-start.33 = (bf16[32,1536]{1,0:T(8,128)(2,1)S(1)}, bf16[32,1536]{1,0:T(8,128)(2,1)S(1)}, u32[]{:S(2)}, u32[]{:S(2)}) collective-permute-start(bf16[32,1536]{1,0:T(8,128)(2,1)S(1)} %get-tuple-element.81), channel_id=1, source_target_pairs={{0,8},{1,9},{2,10},{3,11},{4,12},{5,13},{6,14},{7,15},{8,0},{9,1},... | collective-permute-start | bytes 294920 | tf_op jit(solution)/shard_map/ppermute | solution.py:55
  233.3 11.3 %collective-permute-start.34 = (bf16[32,1536]{1,0:T(8,128)(2,1)S(1)}, bf16[32,1536]{1,0:T(8,128)(2,1)S(1)}, u32[]{:S(2)}, u32[]{:S(2)}) collective-permute-start(bf16[32,1536]{1,0:T(8,128)(2,1)S(1)} %get-tuple-element.83), channel_id=1, source_target_pairs={{0,16},{1,17},{2,18},{3,19},{4,20},{5,21},{6,22},{7,23},{8,24},{9,... | collective-permute-start | bytes 294920 | tf_op jit(solution)/shard_map/ppermute | solution.py:55
  235.3 9.3 %collective-permute-start.35 = (bf16[32,1536]{1,0:T(8,128)(2,1)S(1)}, bf16[32,1536]{1,0:T(8,128)(2,1)S(1)}, u32[]{:S(2)}, u32[]{:S(2)}) collective-permute-start(bf16[32,1536]{1,0:T(8,128)(2,1)S(1)} %get-tuple-element.82), channel_id=1, source_target_pairs={{0,24},{1,25},{2,26},{3,27},{4,28},{5,29},{6,30},{7,31},{8,16},{9,... | collective-permute-start | bytes 294920 | tf_op jit(solution)/shard_map/ppermute | solution.py:55
  (32 other events, 233.6 us)
where the time goes:
time: 247 us; the launch traced here: 246 us
  Pallas kernels  106 us (43%)
  waiting for transfers between devices  61 us (25%)
  starting transfers between devices  46.7 us (19%)
  other arithmetic  12.3 us (5%)
  local copies, waits for them, and re-layouts  11.2 us (5%)
  matrix products  7.08 us (3%)
    ppermute x42, waiting for transfers between devices, exchange(): return lax.ppermute(block, AXES, [(d, d ^ mask) for d in range(devices)])  61 us
    ppermute x42, starting transfers between devices, exchange(): return lax.ppermute(block, AXES, [(d, d ^ mask) for d in range(devices)])  46.7 us
    pallas_call x4, Pallas kernels, grad_rows(): pl.pallas_call(functools.partial(grad_kernel, counts=[a.shape[-1] for a i...  28.9 us
    pallas_call x2, Pallas kernels, attention(): pl.pallas_call(attention_kernel, grid=(count,), in_specs=[pl.BlockSpec(ma...  28.8 us
    pallas_call x2, Pallas kernels, project(): pl.pallas_call(functools.partial(project_kernel, alias=earlier is not Non...  22.6 us
    pallas_call x1, Pallas kernels, input_grad(): pl.pallas_call(functools.partial(input_grad_kernel, chunks=chunks), grid=...  19.4 us
    pallas_call x1, Pallas kernels, back(): pl.pallas_call(back_kernel, grid_spec=pltpu.PrefetchScalarGridSpec(num_sc...  6.37 us
    convert_element_type x15, other arithmetic, finish_scatter(): parts.append(total if last else total.astype(wire))  5.4 us
  transfers between devices with their start and end apart: 42, of which 19 were waited for; matrix products, arithmetic and copies ran while one was open for 11% of the time, Pallas kernels for 24%

commit v1 on v0

v1 whole, which is shorter than its diff:
```python
import functools

import jax
import jax.numpy as jnp
from jax import lax
from jax.experimental import pallas as pl
from jax.experimental.pallas import tpu as pltpu
from jax.sharding import PartitionSpec as P


HEAD = 64
PATCH = 8
PAIR = 2 * HEAD
GROUP = 16
AXES = ("seq", "tp")
F32 = jnp.float32
BF16 = jnp.bfloat16
NN = (((1,), (0,)), ((), ()))
NT = (((1,), (1,)), ((), ()))
TN = (((0,), (0,)), ((), ()))


def dot(a, b, dims=NN):
    return lax.dot_general(a, b, dims, preferred_element_type=F32)


def cost(flops, nbytes, transcendentals=0):
    return pl.CostEstimate(
        flops=int(flops), bytes_accessed=int(nbytes), transcendentals=int(transcendentals)
    )


def bit_masks(mesh):
    seq, tp = mesh.shape["seq"], mesh.shape["tp"]
    tp_bits = [1 << b for b in range(tp.bit_length() - 1)]
    seq_bits = [tp << b for b in range(seq.bit_length() - 1)]
    return tp_bits, seq_bits


def spans(bits):
    masks = [0]
    for bit in bits:
        masks = masks + [m ^ bit for m in masks]
    return masks


def scatter_order(stages):
    order = [0]
    for bits in reversed(stages):
        order = [m ^ q for m in spans(bits) for q in order]
    return order


def exchange(block, mask, devices):
    return lax.ppermute(block, AXES, [(d, d ^ mask) for d in range(devices)])


def finish_scatter(keep, send, bits, devices):
    for n, bit in enumerate(bits):
        got = exchange(send, bit, devices)
        total = keep.astype(F32) + got.astype(F32)
        if n + 1 == len(bits):
            return total
        total = total.astype(keep.dtype)
        half = keep.shape[0] // 2
        keep, send = total[:half], total[half:]


def combine(pairs, mode="split"):
    if mode == "last":
        return [keep.astype(F32) + got.astype(F32) for keep, got in pairs]
    half = pairs[0][0].shape[0] // 2
    halves = []
    for part in (slice(0, half), slice(half, None)):
        sums = [(k[part].astype(F32) + g[part].astype(F32)).astype(BF16) for k, g in pairs]
        halves.append([jnp.concatenate(sums, axis=1)] if mode == "merge" else sums)
    return list(zip(*halves))


def split_scatter(blocks, bits, devices):
    half = blocks.shape[0] // 2
    return finish_scatter(blocks[:half], blocks[half:], bits, devices)


def project_kernel(
    place, a_ref, b_ref, onehot_ref, embed_ref, w_proj_ref, gain_ref, w_qkv_ref, *rest, alias
):
    if alias:
        rest = rest[5:]
    slices_ref, normed_ref, inv_ref, act_ref, qkv_ref, x_ref = rest
    step = pl.program_id(0)
    groups, four, _, width = slices_ref.shape
    tile = four * GROUP
    rows = groups * tile

    @pl.when(step == 0)
    def _():
        for k, src in enumerate((a_ref, b_ref)):
            at = 2 * (place[1] ^ k)
            for g in range(groups):
                for h in range(2):
                    slices_ref[g, at + h] = src[
                        g * GROUP : (g + 1) * GROUP, h * width : (h + 1) * width
                    ]
        slices = slices_ref[...].reshape(rows, width)
        onehot = onehot_ref[...].reshape(rows, onehot_ref.shape[-1])
        for n in range(0, width, 256):
            x_ref[:, n : n + 256] = dot(onehot, embed_ref[:, n : n + 256]) + dot(
                slices, w_proj_ref[:, n : n + 256]
            )
        for g in range(groups):
            for p in range(four):
                at = g * tile + p * GROUP
                x = x_ref[at : at + GROUP, :]
                inv = lax.rsqrt(jnp.mean(x * x, axis=1, keepdims=True) + 1e-05)
                normed = x * inv
                normed_ref[g, p] = normed
                inv_ref[g, p] = jnp.broadcast_to(inv, (GROUP, 128))
                act_ref[g, p] = (normed * gain_ref[...]).astype(BF16)

    act = act_ref[...].reshape(rows, width)
    qkv_ref[...] = dot(act, w_qkv_ref[...]).astype(BF16).reshape(qkv_ref.shape)


def project(place, first, second, onehot, embed, w_proj, gain, w_qkv, earlier):
    groups = onehot.shape[0]
    half = groups * GROUP
    width = w_proj.shape[0]
    vocab = embed.shape[0]
    four = PATCH // 2
    shape = lambda cols, kind: jax.ShapeDtypeStruct((groups, PATCH, GROUP, cols), kind)
    outs = [
        shape(width, BF16),
        shape(width, F32),
        shape(128, F32),
        shape(width, BF16),
        shape(3 * width, BF16),
    ]
    block = 512
    flip = 0 if earlier is None else 1
    part = lambda cols: pl.BlockSpec(
        (groups, four, GROUP, cols), lambda n, s: (0, s[0] ^ flip, 0, 0)
    )
    first_spec = pl.BlockSpec((half, 2 * width), lambda n, s: (0 if flip else s[2], 0))
    in_specs = [
        first_spec,
        pl.BlockSpec((half, 2 * width), lambda n, s: (0, 0)),
        part(vocab),
        pl.BlockSpec((vocab, width), lambda n, s: (0, 0)),
        pl.BlockSpec((width, width), lambda n, s: (0, 0)),
        pl.BlockSpec((1, width), lambda n, s: (0, 0)),
        pl.BlockSpec((width, block), lambda n, s: (0, n)),
    ]
    args = [place, first, second, onehot, embed, w_proj, gain, w_qkv]
    aliases = {}
    if earlier is not None:
        in_specs += [pl.BlockSpec(memory_space=pl.ANY)] * 5
        args += list(earlier)
        aliases = {8 + i: i for i in range(5)}
    out_specs = [
        part(width),
        part(width),
        part(128),
        part(width),
        pl.BlockSpec((groups, four, GROUP, block), lambda n, s: (0, s[0] ^ flip, 0, n)),
    ]
    return pl.pallas_call(
        functools.partial(project_kernel, alias=earlier is not None),
        grid_spec=pltpu.PrefetchScalarGridSpec(
            num_scalar_prefetch=1,
            grid=(3 * width // block,),
            in_specs=in_specs,
            out_specs=out_specs,
            scratch_shapes=[pltpu.VMEM((four * half, width), F32)],
        ),
        out_shape=outs,
        input_output_aliases=aliases,
        cost_estimate=cost(2 * four * half * width * (4 * width + vocab), 16e6),
        name="project",
    )(*args)


def attention_kernel(q_ref, k_ref, v_ref, d_ref, *rest):
    context_ref, d_qkv_ref, mask_ref = rest[-3:]
    rows = PATCH * GROUP
    scale = HEAD ** (-0.5)

    @pl.when(pl.program_id(0) == 0)
    def _():
        key = lax.broadcasted_iota(jnp.int32, (rows, 2 * rows), 0)
        query = lax.broadcasted_iota(jnp.int32, (rows, 2 * rows), 1) % rows
        seen = (key % GROUP == query % GROUP) & (key // GROUP <= query // GROUP)
        mask_ref[...] = seen.astype(F32)

    low = lax.broadcasted_iota(jnp.int32, (rows, PAIR), 1) < HEAD
    own = mask_ref[:GROUP, :] > 0.5

    def stack(value):
        zero = jnp.zeros_like(value)
        return jnp.concatenate([jnp.where(low, value, zero), jnp.where(low, zero, value)], axis=0)

    split = lambda value: value.reshape(PATCH, GROUP, 2 * rows)
    join = lambda value: value.astype(BF16).reshape(rows, 2 * rows)
    for g in range(q_ref.shape[0]):
        q, k, v, d = (ref[g].reshape(rows, PAIR) for ref in (q_ref, k_ref, v_ref, d_ref))
        q2, d2 = stack(q * jnp.asarray(scale, BF16)), stack(d)
        scores = split(jnp.where(mask_ref[...] > 0.5, dot(k, q2, NT), -1e30))
        expo = jnp.exp(scores - jnp.max(scores, axis=0, keepdims=True))
        total = jnp.sum(expo, axis=0, keepdims=True)
        probs = expo * jnp.where(own, 1.0 / total, 0.0)
        d_probs = split(dot(v, d2, NT))
        d_scores = probs * (d_probs - jnp.sum(probs * d_probs, axis=0, keepdims=True))
        probs, d_scores = join(probs), join(d_scores)
        context = dot(v.T, probs).astype(BF16)
        at = slice(g * rows, (g + 1) * rows)
        context_ref[:HEAD, at] = context[:HEAD, :rows]
        context_ref[HEAD:, at] = context[HEAD:, rows:]
        d_query = dot(d_scores, k * jnp.asarray(scale, BF16), TN)
        d_query = jnp.where(low, d_query[:rows], d_query[rows:])
        for n, grad in enumerate((d_query, dot(d_scores, q2), dot(probs, d2))):
            d_qkv_ref[n, g] = grad.astype(BF16).reshape(PATCH, GROUP, PAIR)


def attention(qkv, d_context, first, count, after=()):
    groups, _, _, width = d_context.shape
    pairs = width // PAIR
    tokens = groups * PATCH * GROUP
    spec = lambda part: pl.BlockSpec(
        (groups, PATCH, GROUP, PAIR), lambda n: (0, 0, 0, part * pairs + first + n)
    )
    return pl.pallas_call(
        attention_kernel,
        grid=(count,),
        in_specs=[spec(0), spec(1), spec(2), spec(0)]
        + [pl.BlockSpec(memory_space=pl.ANY)] * len(after),
        out_specs=[
            pl.BlockSpec((PAIR, tokens), lambda n: (n, 0)),
            pl.BlockSpec((3, groups, PATCH, GROUP, PAIR), lambda n: (0, 0, 0, 0, n)),
        ],
        out_shape=[
            jax.ShapeDtypeStruct((count * PAIR, tokens), BF16),
            jax.ShapeDtypeStruct((3, groups, PATCH, GROUP, count * PAIR), BF16),
        ],
        scratch_shapes=[pltpu.VMEM((PATCH * GROUP, 2 * PATCH * GROUP), F32)],
        cost_estimate=cost(count * groups * 6 * 2 * 256 * 256 * 128, count * 1.6e6),
        name="attention",
    )(qkv, qkv, qkv, d_context, *after)


def turn_rows(lhs, left_ref, orders, place, height):
    tokens = left_ref.shape[2]
    base = 0
    for ref in lhs:
        major = ref.ndim == 2
        cols = ref.shape[0] if major else ref.shape[-1]
        for m in range(0, cols, 256):
            if major:
                turned = ref[m : m + 256, :]
            else:
                turned = ref[..., m : m + 256].reshape(tokens, 256).T
            turned = turned.astype(left_ref.dtype)
            for n, (which, order) in enumerate(orders):
                for b in range(0, 256, height):
                    at = order[(base + m + b) // height] ^ place[which]
                    left_ref[n, pl.ds(pl.multiple_of(at * height, height), height), :] = turned[
                        b : b + height
                    ]
        base += cols


def grad_kernel(place, *refs, sources, orders, height, extra):
    lhs, rhs_ref, rest = refs[:sources], refs[sources], refs[sources + 1 :]
    if extra:
        marks_ref, gain_ref = rest[:2]
        marked_ref, column_ref = rest[-2:]
        rest = rest[:-2]
    left_ref, outs = rest[-1], rest[-1 - 2 * len(orders) : -1]
    _, rows, tokens = left_ref.shape
    step = pl.program_id(0)
    steps = pl.num_programs(0)

    @pl.when(step == 0)
    def _():
        turn_rows(lhs, left_ref, orders, place, height)

    def emit(n, rhs):
        keep_ref, send_ref = outs[2 * n], outs[2 * n + 1]
        for m in range(0, rows, 256):
            tile = dot(left_ref[n, m : m + 256, :].astype(BF16), rhs).astype(BF16)
            if m < rows // 2:
                keep_ref[m : m + 256, :] = tile
            else:
                send_ref[m - rows // 2 : m - rows // 2 + 256, :] = tile

    for n in range(len(orders)):
        blocks = steps // len(orders)
        last = 4 if extra else steps

        @pl.when((step >= n * blocks) & (step < jnp.minimum((n + 1) * blocks, last)))
        def _(n=n):
            emit(n, rhs_ref[...].reshape(tokens, rhs_ref.shape[-1]))

    if extra:
        keep_ref, send_ref = outs[-2:]
        half = rows // 2
        per = marks_ref.shape[-1] * height // rows

        @pl.when(step < 4)
        def _():
            marks = marks_ref[...].reshape(tokens, marks_ref.shape[-1])
            got = dot(marks, rhs_ref[...].reshape(tokens, rhs_ref.shape[-1]), TN)
            for p in range(rows // height):
                at = pl.multiple_of(p * height + step * per, per)
                marked_ref[pl.ds(at, per), :] = got[p * per : (p + 1) * per]

        @pl.when(step == 4)
        def _():
            keep_ref[...] = marked_ref[:half].astype(BF16)
            send_ref[...] = marked_ref[half:].astype(BF16)

        @pl.when(step == 5)
        def _():
            column = jnp.sum(gain_ref[...].T, axis=1, keepdims=True)
            which, order = orders[-1]
            for b in range(0, rows, height):
                at = pl.multiple_of((order[b // height] ^ place[which]) * height, height)
                column_ref[pl.ds(at, height), :] = jnp.broadcast_to(
                    column[b : b + height], (height, 256)
                )
            keep_ref[...] = column_ref[:half].astype(BF16)
            send_ref[...] = column_ref[half:].astype(BF16)


def grad_rows(place, kinds, lhs, rhs, devices, after=(), extra=()):
    rows = sum(a.shape[0] if a.ndim == 2 else a.shape[-1] for a in lhs)
    cols = rhs.shape[-1]
    stacked = rhs.ndim == 5
    planes = rhs.shape[0] if stacked else 1
    block = 256
    per = cols // block
    height = rows // devices
    steps = planes * per + (2 if extra else 0)
    whole = lambda a: pl.BlockSpec(a.shape, lambda n, s: (0,) * a.ndim)
    if stacked:
        rhs_spec = pl.BlockSpec(
            (1,) + rhs.shape[1:4] + (block,), lambda n, s: (n // per, 0, 0, 0, n % per)
        )
    else:
        rhs_spec = pl.BlockSpec(
            rhs.shape[:-1] + (block,), lambda n, s: (0, 0, 0, jnp.minimum(n, per - 1))
        )
    tokens = rhs.shape[-2] * rhs.shape[-3] * rhs.shape[-4]
    each = steps // len(kinds)
    out = jax.ShapeDtypeStruct((rows // 2, each * block), BF16)
    out_specs = []
    for n in range(len(kinds)):
        spec = pl.BlockSpec(
            (rows // 2, block), lambda i, s, n=n: (0, jnp.clip(i - n * each, 0, each - 1))
        )
        out_specs += [spec, spec]
    scratch = [pltpu.VMEM((len(kinds), rows, tokens), F32 if height % 16 else BF16)]
    if extra:
        scratch += [pltpu.VMEM((rows, block), F32), pltpu.VMEM((rows, block), F32)]
    got = pl.pallas_call(
        functools.partial(
            grad_kernel,
            sources=len(lhs),
            orders=[(which, spots(stages, devices)) for which, stages in kinds],
            height=height,
            extra=bool(extra),
        ),
        grid_spec=pltpu.PrefetchScalarGridSpec(
            num_scalar_prefetch=1,
            grid=(steps,),
            in_specs=[whole(a) for a in lhs]
            + [rhs_spec]
            + [whole(a) for a in extra]
            + [pl.BlockSpec(memory_space=pl.ANY)] * len(after),
            out_specs=out_specs,
            scratch_shapes=scratch,
        ),
        out_shape=[out] * (2 * len(kinds)),
        cost_estimate=cost(2 * tokens * rows * steps * block, 2 * rows * steps * block + 4e6),
        name="grad_rows",
    )(place, *lhs, rhs, *extra, *after)
    return [(got[n], got[n + 1]) for n in range(0, len(got), 2)]


def input_grad_kernel(*refs, chunks):
    d_refs, w_refs = refs[:chunks], refs[chunks : 2 * chunks]
    normed_ref, inv_ref, gain_ref, out_grad_ref = refs[2 * chunks : 2 * chunks + 4]
    d_x_ref, grad_gain_ref, acc_ref = refs[-3:]
    step = pl.program_id(0)
    groups, _, _, width = normed_ref.shape
    rows = groups * PATCH * GROUP
    for n in range(0, width, 256):
        total = None
        for d_ref, w_ref in zip(d_refs, w_refs):
            term = dot(d_ref[...].reshape(rows, d_ref.shape[-1]), w_ref[n : n + 256, :], NT)
            total = term if total is None else total + term

        @pl.when(step == 0)
        def _():
            acc_ref[:, n : n + 256] = total

        @pl.when(step > 0)
        def _():
            acc_ref[:, n : n + 256] += total

    @pl.when(step == pl.num_programs(0) - 1)
    def _():
        grad_gain_ref[...] = jnp.zeros_like(grad_gain_ref)

        @pl.loop(0, groups)
        def _(g):
          for p in range(PATCH):
            n = g * PATCH + p
            d_act = acc_ref[pl.ds(pl.multiple_of(n * GROUP, GROUP), GROUP), :]
            normed = normed_ref[g, p]
            inv = inv_ref[g, p][:, :1]
            part = d_act * normed
            grad_gain_ref[...] += part[:8] + part[8:]
            d_normed = d_act * gain_ref[...]
            mean = jnp.mean(part * gain_ref[...], axis=1, keepdims=True)
            d_x = out_grad_ref[g, p].astype(F32) + inv * (d_normed - normed * mean)
            d_x_ref[g, p] = d_x.astype(BF16)


def input_grad(d_qkvs, w_qkv, normed, inv, gain, out_grad, after=()):
    groups, _, _, width = normed.shape
    tokens = groups * PATCH * GROUP
    chunks = len(d_qkvs)
    cols = [d.shape[-1] for d in d_qkvs]
    d_specs, w_specs, at = [], [], 0
    for c in cols:
        d_specs.append(pl.BlockSpec((1, groups, PATCH, GROUP, c), lambda n: (n, 0, 0, 0, 0)))
        w_specs.append(
            pl.BlockSpec((width, c), lambda n, c=c, at=at: (0, n * (width // c) + at // c))
        )
        at += c
    whole = lambda a: pl.BlockSpec(a.shape, lambda n: (0,) * a.ndim)
    return pl.pallas_call(
        functools.partial(input_grad_kernel, chunks=chunks),
        grid=(3,),
        in_specs=d_specs
        + w_specs
        + [whole(normed), whole(inv), whole(gain), whole(out_grad)]
        + [pl.BlockSpec(memory_space=pl.ANY)] * len(after),
        out_specs=[
            pl.BlockSpec(normed.shape, lambda n: (0, 0, 0, 0)),
            pl.BlockSpec((8, width), lambda n: (0, 0)),
        ],
        out_shape=[
            jax.ShapeDtypeStruct(normed.shape, BF16),
            jax.ShapeDtypeStruct((8, width), F32),
        ],
        scratch_shapes=[pltpu.VMEM((tokens, width), F32)],
        cost_estimate=cost(2 * tokens * width * 3 * width, 20e6),
        name="input_grad",
    )(*d_qkvs, *([w_qkv] * chunks), normed, inv, gain, out_grad, *after)


def back_kernel(place, d_x_ref, w_ref, *refs, count):
    outs, moved_ref = refs[-count - 1 : -1], refs[-1]
    groups, _, _, width = d_x_ref.shape
    rows = groups * PATCH * GROUP
    left = d_x_ref[...].reshape(rows, width)
    for n in range(0, width, 256):
        got = dot(left, w_ref[n : n + 256, :], NT).astype(BF16)
        got = got.reshape(groups, PATCH, GROUP, 256)
        for g in range(groups):
            for j in range(PATCH):
                moved_ref[j, g * GROUP : (g + 1) * GROUP, n : n + 256] = got[g, j]
    for k, out in enumerate(outs):
        for h in range(2):
            out[:, h * width : (h + 1) * width] = moved_ref[2 * (place[2] ^ k) + h]


def back(place, d_x, w_proj, tp, after=()):
    groups, _, _, width = d_x.shape
    half = groups * GROUP
    whole = lambda a: pl.BlockSpec(a.shape, lambda n, s: (0,) * a.ndim)
    out = jax.ShapeDtypeStruct((half, 2 * width), BF16)
    return pl.pallas_call(
        functools.partial(back_kernel, count=tp),
        grid_spec=pltpu.PrefetchScalarGridSpec(
            num_scalar_prefetch=1,
            grid=(1,),
            in_specs=[whole(d_x), whole(w_proj)]
            + [pl.BlockSpec(memory_space=pl.ANY)] * len(after),
            out_specs=[whole(out)] * tp,
            scratch_shapes=[pltpu.VMEM((PATCH, half, width), BF16)],
        ),
        out_shape=[out] * tp,
        cost_estimate=cost(2 * PATCH * half * width * width, 6e6),
        name="back",
    )(place, d_x, w_proj, *after)


def spots(stages, devices):
    order = scatter_order(stages)
    where = [0] * devices
    for p, q in enumerate(order):
        where[q] = p
    return where


def spot_of(value, stages, devices):
    where = spots(stages, devices)
    total = jnp.zeros_like(value)
    for bit in range(devices.bit_length() - 1):
        total = total + ((value >> bit) & 1) * where[1 << bit]
    return total


def on_device(mesh, glob_out, byte_ids, out_grad, embed, w_proj, norm_gain, w_qkv, w_out):
    vocab, width = embed.shape
    tp, devices = mesh.shape["tp"], mesh.size
    half = byte_ids.shape[0]
    groups = half // GROUP
    t = lax.axis_index("tp").astype(jnp.int32)
    me = lax.axis_index("seq").astype(jnp.int32) * tp + t
    tp_bits, seq_bits = bit_masks(mesh)
    core, wide = tp_bits[:1], tp_bits[1:]
    xy = [core, wide] + [[bit] for bit in seq_bits]
    yx = [core, seq_bits[:1], wide] + [[bit] for bit in seq_bits[1:]]
    place = jnp.stack(
        [t >> 1, t & 1, t, spot_of(me, xy, devices), spot_of(me, yx, devices)]
    )
    XY, YX = (3, xy), (4, yx)

    arrived = {}
    for k in (2, 3, 1)[: tp - 1]:
        block = lax.dynamic_slice(glob_out, ((t ^ k) * half, 0), (half, glob_out.shape[1]))
        arrived[k] = exchange(block, k, devices)

    ids = byte_ids.reshape(groups, GROUP, PATCH).transpose(0, 2, 1)
    onehot = (ids[..., None] == jnp.arange(vocab, dtype=jnp.int32)).astype(BF16)
    grads = out_grad.reshape(groups, GROUP, PATCH, width).transpose(0, 2, 1, 3)
    d_context = lax.dot_general(
        grads, w_out, (((3,), (1,)), ((), ())), preferred_element_type=F32
    ).astype(BF16)
    gain = norm_gain.reshape(1, width)

    early = project(place, glob_out, arrived[1], onehot, embed, w_proj, gain, w_qkv, None)
    slices, normed, inv, act, qkv = project(
        place, arrived[2], arrived[3], onehot, embed, w_proj, gain, w_qkv, early
    )

    def hop(pairs, masks, mode="split"):
        arrived = []
        for (keep, send), mask in zip(pairs, masks):
            arrived.append((keep, exchange(send, mask, devices)))
        return combine(arrived, mode)

    flat = lambda pairs: [a for pair in pairs for a in pair]
    first, second = core[0], (wide[0], seq_bits[0])
    rest = seq_bits[1:]

    def finish(pairs, n=0):
        for bit in rest[n:-1]:
            pairs = hop(pairs, [bit])
            n += 1
        return hop(pairs, [rest[-1]], "last")[0]

    pairs = width // PAIR
    count = pairs // 2
    context_a, d_qkv_a = attention(qkv, d_context, 0, count)
    one = grad_rows(place, (XY, YX), [act], d_qkv_a, devices)
    context_b, d_qkv_b = attention(qkv, d_context, count, count, flat(one)[:1])
    one = hop(one, (first, first))
    two = grad_rows(place, (XY,), [act], d_qkv_b, devices)
    two = two + grad_rows(place, (YX,), [context_a, context_b], grads, devices, flat(two)[:1])
    one = hop(one, second)
    two = hop(two, (first, first))

    d_x, grad_gain = input_grad((d_qkv_a, d_qkv_b), w_qkv, normed, inv, gain, grads)
    one = hop(one, second[::-1], "merge")
    two = hop(two, second)

    height = vocab // devices
    spot = spot_of((ids // height) ^ me, yx, devices) * height + ids % height
    marks = (spot[..., None] == jnp.arange(vocab, dtype=jnp.int32)).astype(BF16)
    fits = height % 8 == 0 and width == 4 * vocab
    extra = (marks, grad_gain) if fits else ()
    three = grad_rows(place, (XY, YX), [slices], d_x, devices, (), extra)

    rows = back(place, d_x, w_proj, tp, flat(three)[:1])
    glob_grad = jnp.zeros((tp * half, 2 * width), BF16)
    for k in range(tp):
        piece = rows[0]
        if k:
            piece = exchange(rows[k], k, devices)
        glob_grad = lax.dynamic_update_slice(glob_grad, piece, ((t ^ k) * half, 0))

    two = hop(two, second[::-1], "merge")
    three = hop(three, (first, first))
    three = hop(three, second)
    three = hop(three, second[::-1], "merge")
    one, two, three = finish(one), finish(two), finish(three)

    each = width // devices
    if fits:
        grad_proj = three[:, :width]
        marked = three[:, width : width + 256].reshape(4, height, 256)
        grad_embed = marked.transpose(1, 0, 2).reshape(height, width)
        grad_gain = three[:, width + 256]
    else:
        grad_proj = three
        grad_embed = lax.dot_general(
            marks, d_x, (((0, 1, 2), (0, 1, 2)), ((), ())), preferred_element_type=F32
        ).astype(BF16)
        flips = [first, second[1], second[0]] + rest
        grad_embed = split_scatter(grad_embed, flips, devices)
        blocks = jnp.sum(grad_gain, axis=0).reshape(devices, each)
        blocks = blocks[jnp.array(scatter_order(yx), dtype=jnp.int32) ^ me]
        grad_gain = split_scatter(blocks, flips, devices).reshape(-1)

    span = count * PAIR
    grad_out = two[:, 3 * span :]
    grad_qkv = jnp.concatenate(
        [part[:, n * span : (n + 1) * span] for n in range(3) for part in (one, two)], axis=1
    )
    return (glob_grad, grad_embed, grad_proj, grad_gain, grad_qkv, grad_out)


def solution(mesh):
    def body(*args):
        return on_device(mesh, *args)

    return shard(body, mesh)


def shard(body, mesh):
    return jax.shard_map(
        body,
        mesh=mesh,
        in_specs=(
            P("seq", "tp"),
            P(AXES, None),
            P(AXES, None),
            P(),
            P(),
            P(),
            P(),
            P(),
        ),
        out_specs=(
            P("seq", "tp"),
            P(AXES, None),
            P(AXES, None),
            P(AXES),
            P(AXES, None),
            P(AXES, None),
        ),
        check_vma=False,
    )
```

time: 247 us -> 229 us (0.927)
  starting transfers between devices: 46.7 us -> 31.2 us
  waiting for transfers between devices: 61 us -> 70.4 us
  Pallas kernels: 106 us -> 101 us
  other arithmetic: 12.3 us -> 7.4 us
    ppermute x42 -> x30, starting transfers between devices: 46.7 us -> 31.2 us  [exchange(): return lax.ppermute(block, AXES, [(d, d ^ mask) for d in range(devices)])]
    ppermute x42 -> x30, waiting for transfers between devices: 61 us -> 70.4 us  [exchange(): return lax.ppermute(block, AXES, [(d, d ^ mask) for d in range(devices)])]
    pallas_call x7, Pallas kernels: 64.1 us -> 57.8 us  [the longest x4 32.6 us: grad_rows(): pl.pallas_call(functools.partial(grad_kernel, sources=len(lhs), orders=[(...]
    gather x3 -> x0, local copies, waits for them, and re-layouts: 3.07 us -> none  [the longest x2 2.49 us: positions(): return table[jnp.arange(devices, dtype=jnp.int32) ^ me]]
    dot_general x2 -> x1, matrix products: 7.08 us -> 4.62 us  [on_device(): lax.dot_general(grads, w_out, (((3,), (1,)), ((), ())), preferred_element...]
    convert_element_type x17 -> x23, other arithmetic: 7.11 us -> 7.16 us  [the longest x21 5.33 us: combine(): (k[part].astype(F32) + g[part].astype(F32)).astype(BF16)]
  transfers between devices with their start and end apart: 42 -> 30, of which waited for: 19 -> 11; matrix products, arithmetic and copies ran while one was open for 11% -> 9% of each run, Pallas kernels for 24% -> 12%
where the time goes in v1:
time: 229 us; the launch traced here: 228 us
  Pallas kernels  101 us (44%)
  waiting for transfers between devices  70.4 us (31%)
  starting transfers between devices  31.2 us (14%)
  local copies, waits for them, and re-layouts  12.7 us (6%)
  other arithmetic  7.4 us (3%)
  matrix products  4.62 us (2%)
    ppermute x30, waiting for transfers between devices, exchange(): return lax.ppermute(block, AXES, [(d, d ^ mask) for d in range(devices)])  70.4 us
    pallas_call x4, Pallas kernels, grad_rows(): pl.pallas_call(functools.partial(grad_kernel, sources=len(lhs), orders=[(...  32.6 us
    ppermute x30, starting transfers between devices, exchange(): return lax.ppermute(block, AXES, [(d, d ^ mask) for d in range(devices)])  31.2 us
    pallas_call x2, Pallas kernels, project(): pl.pallas_call(functools.partial(project_kernel, alias=earlier is not Non...  23.7 us
    pallas_call x1, Pallas kernels, input_grad(): pl.pallas_call(functools.partial(input_grad_kernel, chunks=chunks), grid=...  19.6 us
    pallas_call x2, Pallas kernels, attention(): pl.pallas_call(attention_kernel, grid=(count,), in_specs=[spec(0), spec(1...  19.6 us
    pallas_call x1, Pallas kernels, back(): pl.pallas_call(functools.partial(back_kernel, count=tp), grid_spec=pltpu....  5.73 us
    convert_element_type x21, other arithmetic, combine(): (k[part].astype(F32) + g[part].astype(F32)).astype(BF16)  5.33 us
  transfers between devices with their start and end apart: 30, of which 11 were waited for; matrix products, arithmetic and copies ran while one was open for 9% of the time, Pallas kernels for 12%

profile of v1, /device:TPU:0, one launch (start us, length us, event | category | flops | bytes accessed | tf_op | source)
XLA Modules:
  0.0 228.5 jit_solution(7511948655951924672)
XLA Ops:
  2.7 2.6 %collective-permute-start = (bf16[96,2048]{1,0:T(8,128)(2,1)S(1)}, bf16[96,2048]{1,0:T(8,128)(2,1)}, u32[]{:S(2)}, u32[]{:S(2)}) collective-permute-start(bf16[96,2048]{1,0:T(8,128)(2,1)S(1)} %get-tuple-element.86), channel_id=1, source_target_pairs={{0,2},{1,3},{2,0},{3,1},{4,6},{5,7},{6,4},{7,5},{8,10},{9,11},{10,... | collective-permute-start | bytes 1179656 | tf_op jit(solution)/shard_map/ppermute | solution.py:55
  5.5 4.6 %fusion.2.d_ref = bf16[6,8,16,1024]{3,2,1,0:T(8,128)(2,1)} fusion(bf16[1024,1024]{1,0:T(8,128)(2,1)S(1)} %copy-done, bf16[6,16,8,1024]{3,2,1,0:T(8,128)(2,1)} %bitcast.29), kind=kOutput, calls=%fused_computation.2 | convolution fusion | flops 1611399168 | bytes 5242880 | tf_op jit(solution)/shard_map/dot_general | solution.py:540
  11.9 3.4 %copy.26 = bf16[6,16,8,1024]{3,1,2,0:T(8,128)(2,1)} copy(bf16[6,16,8,1024]{3,2,1,0:T(8,128)(2,1)} %bitcast.30) | data formatting | bytes 3145728 | tf_op jit(solution)/shard_map/reshape | solution.py:539
  16.0 11.9 %project.2 = (bf16[6,8,16,1024]{3,2,1,0:T(8,128)(2,1)}, f32[6,8,16,1024]{3,2,1,0:T(8,128)}, f32[6,8,16,128]{3,2,1,0:T(8,128)}, bf16[6,8,16,1024]{3,2,1,0:T(8,128)(2,1)}, bf16[6,8,16,3072]{3,2,1,0:T(8,128)(2,1)}) custom-call(s32[5]{0:T(128)} %stack.23.place, bf16[384,2048]{1,0:T(8,128)(2,1)} %a_ref.1, bf16[96,2048]{1,0:T(8,128)(2,1)} %collective-permute-done.2.b_ref, ...), custom_call_target="tpu_custom_call" | custom-call | flops 3422552064 | bytes 16000000 | tf_op jit(solution)/shard_map/project/pallas_call | solution.py:167
  28.0 11.7 %project.3 = (bf16[6,8,16,1024]{3,2,1,0:T(8,128)(2,1)}, f32[6,8,16,1024]{3,2,1,0:T(8,128)}, f32[6,8,16,128]{3,2,1,0:T(8,128)}, bf16[6,8,16,1024]{3,2,1,0:T(8,128)(2,1)}, bf16[6,8,16,3072]{3,2,1,0:T(8,128)(2,1)}) custom-call(s32[5]{0:T(128)} %stack.23.place, ...), custom_call_target="tpu_custom_call", output_to_operand_aliasing={{0}: (8, {}), {1}: (9, {}), {2}: (10, {}), {3}: (11, {}), {... | custom-call | flops 3422552064 | bytes 16000000 | tf_op jit(solution)/shard_map/project/pallas_call | solution.py:167
  39.7 9.8 %attention.2 = (bf16[512,768]{1,0:T(8,128)(2,1)}, bf16[3,6,8,16,512]{4,3,2,1,0:T(8,128)(2,1)}) custom-call(bf16[6,8,16,3072]{3,2,1,0:T(8,128)(2,1)} %get-tuple-element.43.q_ref.k_ref.v_ref, bf16[6,8,16,3072]{3,2,1,0:T(8,128)(2,1)} %get-tuple-element.43.q_ref.k_ref.v_ref, bf16[6,8,16,3072]{3,2,1,0:T(8,128)(2,1)} %get-tuple-element.43.q_ref.k_ref.v_ref, ...), custom_call_target="tpu_custom_call" | custom-call | flops 2415919104 | bytes 6400000 | tf_op jit(solution)/shard_map/attention/pallas_call | solution.py:231
  49.5 8.7 %grad_rows.4 = (bf16[512,768]{1,0:T(8,128)(2,1)}, bf16[512,768]{1,0:T(8,128)(2,1)}, bf16[512,768]{1,0:T(8,128)(2,1)}, bf16[512,768]{1,0:T(8,128)(2,1)}) custom-call(s32[5]{0:T(128)} %stack.23.place, bf16[6,8,16,1024]{3,2,1,0:T(8,128)(2,1)} %get-tuple-element.45.refs_0_, bf16[3,6,8,16,512]{4,3,2,1,0:T(8,128)(2,1)} %get-tuple-element.44.refs_1_.refs_0_), custom_call_target="tpu_custom_call" | custom-call | flops 2415919104 | bytes 7145728 | tf_op jit(solution)/shard_map/grad_rows/pallas_call | solution.py:364
  58.2 9.8 %attention.3 = (bf16[512,768]{1,0:T(8,128)(2,1)}, bf16[3,6,8,16,512]{4,3,2,1,0:T(8,128)(2,1)}) custom-call(bf16[6,8,16,3072]{3,2,1,0:T(8,128)(2,1)} %get-tuple-element.43.q_ref.k_ref.v_ref, bf16[6,8,16,3072]{3,2,1,0:T(8,128)(2,1)} %get-tuple-element.43.q_ref.k_ref.v_ref, bf16[6,8,16,3072]{3,2,1,0:T(8,128)(2,1)} %get-tuple-element.43.q_ref.k_ref.v_ref, ...), custom_call_target="tpu_custom_call" | custom-call | flops 2415919104 | bytes 6400000 | tf_op jit(solution)/shard_map/attention/pallas_call | solution.py:231
  68.0 19.6 %input_grad.1 = (bf16[6,8,16,1024]{3,2,1,0:T(8,128)(2,1)}, f32[8,1024]{1,0:T(8,128)}) custom-call(bf16[3,6,8,16,512]{4,3,2,1,0:T(8,128)(2,1)} %get-tuple-element.44.refs_1_.refs_0_, bf16[3,6,8,16,512]{4,3,2,1,0:T(8,128)(2,1)} %get-tuple-element.47.refs_1_, bf16[1024,3072]{1,0:T(8,128)(2,1)} %refs_3_.1, bf16[1024,3072]{1,0:T(8,128)(2,1)} %refs_3_.1, ...), custom_call_target="tpu_custom_call" | custom-call | flops 4831838208 | bytes 20000000 | tf_op jit(solution)/shard_map/input_grad/pallas_call | solution.py:442
  87.6 9.2 %grad_rows.5 = (bf16[512,768]{1,0:T(8,128)(2,1)}, bf16[512,768]{1,0:T(8,128)(2,1)}, bf16[512,768]{1,0:T(8,128)(2,1)}, bf16[512,768]{1,0:T(8,128)(2,1)}) custom-call(s32[5]{0:T(128)} %stack.23.place, bf16[6,8,16,1024]{3,2,1,0:T(8,128)(2,1)} %get-tuple-element.51.refs_0_, bf16[6,8,16,1024]{3,2,1,0:T(8,128)(2,1)} %get-tuple-element.50.refs_1_.d_x_ref, ...), custom_call_target="tpu_custom_call" | custom-call | flops 2415919104 | bytes 7145728 | tf_op jit(solution)/shard_map/grad_rows/pallas_call | solution.py:364
  96.8 5.7 %back.1 = (bf16[96,2048]{1,0:T(8,128)(2,1)}, bf16[96,2048]{1,0:T(8,128)(2,1)}, bf16[96,2048]{1,0:T(8,128)(2,1)}, bf16[96,2048]{1,0:T(8,128)(2,1)}) custom-call(s32[5]{0:T(128)} %stack.23.place, bf16[6,8,16,1024]{3,2,1,0:T(8,128)(2,1)} %get-tuple-element.50.refs_1_.d_x_ref, bf16[1024,1024]{1,0:T(8,128)(2,1)} %w_ref.1, bf16[512,768]{1,0:T(8,128)(2,1)} %get-tuple-element.53.refs_0_), custom_call_target="tpu_custom_call" | custom-call | flops 1610612736 | bytes 6000000 | tf_op jit(solution)/shard_map/back/pallas_call | solution.py:484
  102.7 8.4 %grad_rows.6 = (bf16[512,1536]{1,0:T(8,128)(2,1)}, bf16[512,1536]{1,0:T(8,128)(2,1)}) custom-call(s32[5]{0:T(128)} %stack.23.place, bf16[6,8,16,1024]{3,2,1,0:T(8,128)(2,1)} %get-tuple-element.45.refs_0_, bf16[3,6,8,16,512]{4,3,2,1,0:T(8,128)(2,1)} %get-tuple-element.47.refs_1_), custom_call_target="tpu_custom_call" | custom-call | flops 2415919104 | bytes 7145728 | tf_op jit(solution)/shard_map/grad_rows/pallas_call | solution.py:364
  115.1 6.2 %grad_rows.7 = (bf16[512,1024]{1,0:T(8,128)(2,1)}, bf16[512,1024]{1,0:T(8,128)(2,1)}) custom-call(s32[5]{0:T(128)} %stack.23.place, bf16[512,768]{1,0:T(8,128)(2,1)} %get-tuple-element.66.refs_0_, bf16[512,768]{1,0:T(8,128)(2,1)} %get-tuple-element.67.refs_1_, bf16[6,8,16,1024]{3,2,1,0:T(8,128)(2,1)} %bitcast.28, bf16[512,1536]{1,0:T(8,128)(2,1)} %get-tuple-element.64.refs_3_), custom_call_target="tpu_custom_call" | custom-call | flops 1610612736 | bytes 6097152 | tf_op jit(solution)/shard_map/grad_rows/pallas_call | solution.py:364
  124.4 8.4 %collective-permute-done.5 = bf16[96,2048]{1,0:T(8,128)(2,1)S(1)} collective-permute-done((bf16[96,2048]{1,0:T(8,128)(2,1)}, bf16[96,2048]{1,0:T(8,128)(2,1)S(1)}, u32[]{:S(2)}, u32[]{:S(2)}) %collective-permute-start.5) | collective-permute-done | bytes 393248 | tf_op jit(solution)/shard_map/ppermute | solution.py:55
  140.7 6.7 %collective-permute-done.15 = bf16[256,768]{1,0:T(8,128)(2,1)S(1)} collective-permute-done((bf16[256,768]{1,0:T(8,128)(2,1)S(1)}, bf16[256,768]{1,0:T(8,128)(2,1)S(1)}, u32[]{:S(2)}, u32[]{:S(2)}) %collective-permute-start.15) | collective-permute-done | bytes 393248 | tf_op jit(solution)/shard_map/ppermute | solution.py:55
  150.1 4.9 %collective-permute-done.7 = bf16[256,768]{1,0:T(8,128)(2,1)S(1)} collective-permute-done((bf16[256,768]{1,0:T(8,128)(2,1)S(1)}, bf16[256,768]{1,0:T(8,128)(2,1)S(1)}, u32[]{:S(2)}, u32[]{:S(2)}) %collective-permute-start.7) | collective-permute-done | bytes 393248 | tf_op jit(solution)/shard_map/ppermute | solution.py:55
  158.6 13.6 %collective-permute-done.16 = bf16[128,768]{1,0:T(8,128)(2,1)S(1)} collective-permute-done((bf16[128,768]{1,0:T(8,128)(2,1)S(1)}, bf16[128,768]{1,0:T(8,128)(2,1)S(1)}, u32[]{:S(2)}, u32[]{:S(2)}) %collective-permute-start.16) | collective-permute-done | bytes 196640 | tf_op jit(solution)/shard_map/ppermute | solution.py:55
  175.4 2.3 %collective-permute-done.11 = bf16[128,768]{1,0:T(8,128)(2,1)S(1)} collective-permute-done((bf16[128,768]{1,0:T(8,128)(2,1)S(1)}, bf16[128,768]{1,0:T(8,128)(2,1)S(1)}, u32[]{:S(2)}, u32[]{:S(2)}) %collective-permute-start.11) | collective-permute-done | bytes 196640 | tf_op jit(solution)/shard_map/ppermute | solution.py:55
  177.9 1.9 collective-permute-start.12
  183.9 2.7 %collective-permute-start.21 = (bf16[32,1536]{1,0:T(8,128)(2,1)S(1)}, bf16[32,1536]{1,0:T(8,128)(2,1)S(1)}, u32[]{:S(2)}, u32[]{:S(2)}) collective-permute-start(bf16[32,1536]{1,0:T(8,128)(2,1)S(1)} %add_convert_fusion.30), channel_id=1, source_target_pairs={{0,16},{1,17},{2,18},{3,19},{4,20},{5,21},{6,22},{7,23},{8,24},{9,... | collective-permute-start | bytes 294920 | tf_op jit(solution)/shard_map/ppermute | solution.py:55
  188.2 13.6 %collective-permute-done.23 = bf16[256,1536]{1,0:T(8,128)(2,1)S(1)} collective-permute-done((bf16[256,1536]{1,0:T(8,128)(2,1)S(1)}, bf16[256,1536]{1,0:T(8,128)(2,1)S(1)}, u32[]{:S(2)}, u32[]{:S(2)}) %collective-permute-start.23) | collective-permute-done | bytes 786464 | tf_op jit(solution)/shard_map/ppermute | solution.py:55
  203.7 6.1 %collective-permute-done.24 = bf16[128,1536]{1,0:T(8,128)(2,1)S(1)} collective-permute-done((bf16[128,1536]{1,0:T(8,128)(2,1)S(1)}, bf16[128,1536]{1,0:T(8,128)(2,1)S(1)}, u32[]{:S(2)}, u32[]{:S(2)}) %collective-permute-start.24) | collective-permute-done | bytes 393248 | tf_op jit(solution)/shard_map/ppermute | solution.py:55
  210.7 8.2 %collective-permute-done.28 = bf16[64,2560]{1,0:T(8,128)(2,1)S(1)} collective-permute-done((bf16[64,2560]{1,0:T(8,128)(2,1)S(1)}, bf16[64,2560]{1,0:T(8,128)(2,1)S(1)}, u32[]{:S(2)}, u32[]{:S(2)}) %collective-permute-start.28) | collective-permute-done | bytes 327712 | tf_op jit(solution)/shard_map/ppermute | solution.py:55
  222.5 4.4 %collective-permute-done.29 = bf16[32,2560]{1,0:T(8,128)(2,1)S(1)} collective-permute-done((bf16[32,2560]{1,0:T(8,128)(2,1)S(1)}, bf16[32,2560]{1,0:T(8,128)(2,1)S(1)}, u32[]{:S(2)}, u32[]{:S(2)}) %collective-permute-start.29) | collective-permute-done | bytes 163872 | tf_op jit(solution)/shard_map/ppermute | solution.py:55
  (124 shorter events, 43.0 us)
Async XLA Ops:
  2.1 13.9 %collective-permute-start.2 = (bf16[96,2048]{1,0:T(8,128)(2,1)S(1)}, bf16[96,2048]{1,0:T(8,128)(2,1)}, u32[]{:S(2)}, u32[]{:S(2)}) collective-permute-start(bf16[96,2048]{1,0:T(8,128)(2,1)S(1)} %get-tuple-element.84), channel_id=1, source_target_pairs={{0,1},{1,0},{2,3},{3,2},{4,5},{5,4},{6,7},{7,6},{8,9},{9,8},{10,11... | collective-permute-start | bytes 1179656 | tf_op jit(solution)/shard_map/ppermute | solution.py:55
  2.7 25.3 %collective-permute-start = (bf16[96,2048]{1,0:T(8,128)(2,1)S(1)}, bf16[96,2048]{1,0:T(8,128)(2,1)}, u32[]{:S(2)}, u32[]{:S(2)}) collective-permute-start(bf16[96,2048]{1,0:T(8,128)(2,1)S(1)} %get-tuple-element.86), channel_id=1, source_target_pairs={{0,2},{1,3},{2,0},{3,1},{4,6},{5,7},{6,4},{7,5},{8,10},{9,11},{10,... | collective-permute-start | bytes 1179656 | tf_op jit(solution)/shard_map/ppermute | solution.py:55
  5.3 22.7 %collective-permute-start.1 = (bf16[96,2048]{1,0:T(8,128)(2,1)S(1)}, bf16[96,2048]{1,0:T(8,128)(2,1)}, u32[]{:S(2)}, u32[]{:S(2)}) collective-permute-start(bf16[96,2048]{1,0:T(8,128)(2,1)S(1)} %get-tuple-element.85), channel_id=1, source_target_pairs={{0,3},{1,2},{2,1},{3,0},{4,7},{5,6},{6,5},{7,4},{8,11},{9,10},{10,... | collective-permute-start | bytes 1179656 | tf_op jit(solution)/shard_map/ppermute | solution.py:55
  102.6 18.7 %collective-permute-start.3 = (bf16[96,2048]{1,0:T(8,128)(2,1)}, bf16[96,2048]{1,0:T(8,128)(2,1)S(1)}, u32[]{:S(2)}, u32[]{:S(2)}) collective-permute-start(bf16[96,2048]{1,0:T(8,128)(2,1)} %get-tuple-element.55), channel_id=1, source_target_pairs={{0,1},{1,0},{2,3},{3,2},{4,5},{5,4},{6,7},{7,6},{8,9},{9,8},{10,11... | collective-permute-start | bytes 1179656 | tf_op jit(solution)/shard_map/ppermute | solution.py:55
  111.2 70.1 %collective-permute-start.22 = (bf16[512,1536]{1,0:T(8,128)(2,1)}, bf16[512,1536]{1,0:T(8,128)(2,1)}, u32[]{:S(2)}, u32[]{:S(2)}) collective-permute-start(bf16[512,1536]{1,0:T(8,128)(2,1)} %get-tuple-element.65), channel_id=1, source_target_pairs={{0,1},{1,0},{2,3},{3,2},{4,5},{5,4},{6,7},{7,6},{8,9},{9,8},{10,11... | collective-permute-start | bytes 4718600 | tf_op jit(solution)/shard_map/ppermute | solution.py:55
  111.5 22.1 %collective-permute-start.14 = (bf16[512,768]{1,0:T(8,128)(2,1)}, bf16[512,768]{1,0:T(8,128)(2,1)}, u32[]{:S(2)}, u32[]{:S(2)}) collective-permute-start(bf16[512,768]{1,0:T(8,128)(2,1)} %get-tuple-element.61), channel_id=1, source_target_pairs={{0,1},{1,0},{2,3},{3,2},{4,5},{5,4},{6,7},{7,6},{8,9},{9,8},{10,11... | collective-permute-start | bytes 2359304 | tf_op jit(solution)/shard_map/ppermute | solution.py:55
  111.7 23.7 %collective-permute-start.17 = (bf16[512,768]{1,0:T(8,128)(2,1)}, bf16[512,768]{1,0:T(8,128)(2,1)S(1)}, u32[]{:S(2)}, u32[]{:S(2)}) collective-permute-start(bf16[512,768]{1,0:T(8,128)(2,1)} %get-tuple-element.63), channel_id=1, source_target_pairs={{0,1},{1,0},{2,3},{3,2},{4,5},{5,4},{6,7},{7,6},{8,9},{9,8},{10,11... | collective-permute-start | bytes 2359304 | tf_op jit(solution)/shard_map/ppermute | solution.py:55
  112.0 11.6 %collective-permute-start.4 = (bf16[96,2048]{1,0:T(8,128)(2,1)}, bf16[96,2048]{1,0:T(8,128)(2,1)S(1)}, u32[]{:S(2)}, u32[]{:S(2)}) collective-permute-start(bf16[96,2048]{1,0:T(8,128)(2,1)} %get-tuple-element.56), channel_id=1, source_target_pairs={{0,2},{1,3},{2,0},{3,1},{4,6},{5,7},{6,4},{7,5},{8,10},{9,11},{10,... | collective-permute-start | bytes 1179656 | tf_op jit(solution)/shard_map/ppermute | solution.py:55
  121.3 11.4 %collective-permute-start.5 = (bf16[96,2048]{1,0:T(8,128)(2,1)}, bf16[96,2048]{1,0:T(8,128)(2,1)S(1)}, u32[]{:S(2)}, u32[]{:S(2)}) collective-permute-start(bf16[96,2048]{1,0:T(8,128)(2,1)} %get-tuple-element.57), channel_id=1, source_target_pairs={{0,3},{1,2},{2,1},{3,0},{4,7},{5,6},{6,5},{7,4},{8,11},{9,10},{10,... | collective-permute-start | bytes 1179656 | tf_op jit(solution)/shard_map/ppermute | solution.py:55
  123.6 12.6 %collective-permute-start.6 = (bf16[512,768]{1,0:T(8,128)(2,1)}, bf16[512,768]{1,0:T(8,128)(2,1)S(1)}, u32[]{:S(2)}, u32[]{:S(2)}) collective-permute-start(bf16[512,768]{1,0:T(8,128)(2,1)} %get-tuple-element.58), channel_id=1, source_target_pairs={{0,1},{1,0},{2,3},{3,2},{4,5},{5,4},{6,7},{7,6},{8,9},{9,8},{10,11... | collective-permute-start | bytes 2359304 | tf_op jit(solution)/shard_map/ppermute | solution.py:55
  135.4 12.1 %collective-permute-start.15 = (bf16[256,768]{1,0:T(8,128)(2,1)S(1)}, bf16[256,768]{1,0:T(8,128)(2,1)S(1)}, u32[]{:S(2)}, u32[]{:S(2)}) collective-permute-start(bf16[256,768]{1,0:T(8,128)(2,1)S(1)} %get-tuple-element.77), channel_id=1, source_target_pairs={{0,2},{1,3},{2,0},{3,1},{4,6},{5,7},{6,4},{7,5},{8,10},{9,11},{10,... | collective-permute-start | bytes 1179656 | tf_op jit(solution)/shard_map/ppermute | solution.py:55
  136.2 12.9 %collective-permute-start.18 = (bf16[256,768]{1,0:T(8,128)(2,1)S(1)}, bf16[256,768]{1,0:T(8,128)(2,1)S(1)}, u32[]{:S(2)}, u32[]{:S(2)}) collective-permute-start(bf16[256,768]{1,0:T(8,128)(2,1)S(1)} %get-tuple-element.79), channel_id=1, source_target_pairs={{0,4},{1,5},{2,6},{3,7},{4,0},{5,1},{6,2},{7,3},{8,12},{9,13},{10,... | collective-permute-start | bytes 1179656 | tf_op jit(solution)/shard_map/ppermute | solution.py:55
  138.3 16.7 %collective-permute-start.7 = (bf16[256,768]{1,0:T(8,128)(2,1)S(1)}, bf16[256,768]{1,0:T(8,128)(2,1)S(1)}, u32[]{:S(2)}, u32[]{:S(2)}) collective-permute-start(bf16[256,768]{1,0:T(8,128)(2,1)S(1)} %get-tuple-element.81), channel_id=1, source_target_pairs={{0,2},{1,3},{2,0},{3,1},{4,6},{5,7},{6,4},{7,5},{8,10},{9,11},{10,... | collective-permute-start | bytes 1179656 | tf_op jit(solution)/shard_map/ppermute | solution.py:55
  139.8 16.9 %collective-permute-start.10 = (bf16[256,768]{1,0:T(8,128)(2,1)S(1)}, bf16[256,768]{1,0:T(8,128)(2,1)S(1)}, u32[]{:S(2)}, u32[]{:S(2)}) collective-permute-start(bf16[256,768]{1,0:T(8,128)(2,1)S(1)} %get-tuple-element.83), channel_id=1, source_target_pairs={{0,4},{1,5},{2,6},{3,7},{4,0},{5,1},{6,2},{7,3},{8,12},{9,13},{10,... | collective-permute-start | bytes 1179656 | tf_op jit(solution)/shard_map/ppermute | solution.py:55
  147.4 32.3 %collective-permute-start.26 = (bf16[256,1024]{1,0:T(8,128)(2,1)S(1)}, bf16[256,1024]{1,0:T(8,128)(2,1)S(1)}, u32[]{:S(2)}, u32[]{:S(2)}) collective-permute-start(bf16[256,1024]{1,0:T(8,128)(2,1)S(1)} %get-tuple-element.73), channel_id=1, source_target_pairs={{0,4},{1,5},{2,6},{3,7},{4,0},{5,1},{6,2},{7,3},{8,12},{9,13},{10,... | collective-permute-start | bytes 1572872 | tf_op jit(solution)/shard_map/ppermute | solution.py:55
  149.0 23.1 %collective-permute-start.16 = (bf16[128,768]{1,0:T(8,128)(2,1)S(1)}, bf16[128,768]{1,0:T(8,128)(2,1)S(1)}, u32[]{:S(2)}, u32[]{:S(2)}) collective-permute-start(bf16[128,768]{1,0:T(8,128)(2,1)S(1)} %get-tuple-element.92), channel_id=1, source_target_pairs={{0,4},{1,5},{2,6},{3,7},{4,0},{5,1},{6,2},{7,3},{8,12},{9,13},{10,... | collective-permute-start | bytes 589832 | tf_op jit(solution)/shard_map/ppermute | solution.py:55
  155.0 18.7 %collective-permute-start.19 = (bf16[128,768]{1,0:T(8,128)(2,1)S(1)}, bf16[128,768]{1,0:T(8,128)(2,1)S(1)}, u32[]{:S(2)}, u32[]{:S(2)}) collective-permute-start(bf16[128,768]{1,0:T(8,128)(2,1)S(1)} %get-tuple-element.94), channel_id=1, source_target_pairs={{0,2},{1,3},{2,0},{3,1},{4,6},{5,7},{6,4},{7,5},{8,10},{9,11},{10,... | collective-permute-start | bytes 589832 | tf_op jit(solution)/shard_map/ppermute | solution.py:55
  156.7 18.7 %collective-permute-start.8 = (bf16[128,768]{1,0:T(8,128)(2,1)S(1)}, bf16[128,768]{1,0:T(8,128)(2,1)S(1)}, u32[]{:S(2)}, u32[]{:S(2)}) collective-permute-start(bf16[128,768]{1,0:T(8,128)(2,1)S(1)} %get-tuple-element.96), channel_id=1, source_target_pairs={{0,4},{1,5},{2,6},{3,7},{4,0},{5,1},{6,2},{7,3},{8,12},{9,13},{10,... | collective-permute-start | bytes 589832 | tf_op jit(solution)/shard_map/ppermute | solution.py:55
  173.7 10.1 %collective-permute-start.20 = (bf16[64,1536]{1,0:T(8,128)(2,1)S(1)}, bf16[64,1536]{1,0:T(8,128)(2,1)S(1)}, u32[]{:S(2)}, u32[]{:S(2)}) collective-permute-start(bf16[64,1536]{1,0:T(8,128)(2,1)S(1)} %pad_maximum_fusion.2), channel_id=1, source_target_pairs={{0,8},{1,9},{2,10},{3,11},{4,12},{5,13},{6,14},{7,15},{8,0},{9,1},... | collective-permute-start | bytes 589832 | tf_op jit(solution)/shard_map/ppermute | solution.py:55
  179.9 23.7 %collective-permute-start.27 = (bf16[128,1024]{1,0:T(8,128)(2,1)S(1)}, bf16[128,1024]{1,0:T(8,128)(2,1)S(1)}, u32[]{:S(2)}, u32[]{:S(2)}) collective-permute-start(bf16[128,1024]{1,0:T(8,128)(2,1)S(1)} %get-tuple-element.88), channel_id=1, source_target_pairs={{0,2},{1,3},{2,0},{3,1},{4,6},{5,7},{6,4},{7,5},{8,10},{9,11},{10,... | collective-permute-start | bytes 786440 | tf_op jit(solution)/shard_map/ppermute | solution.py:55
  183.0 18.8 %collective-permute-start.23 = (bf16[256,1536]{1,0:T(8,128)(2,1)S(1)}, bf16[256,1536]{1,0:T(8,128)(2,1)S(1)}, u32[]{:S(2)}, u32[]{:S(2)}) collective-permute-start(bf16[256,1536]{1,0:T(8,128)(2,1)S(1)} %get-tuple-element.71), channel_id=1, source_target_pairs={{0,2},{1,3},{2,0},{3,1},{4,6},{5,7},{6,4},{7,5},{8,10},{9,11},{10,... | collective-permute-start | bytes 2359304 | tf_op jit(solution)/shard_map/ppermute | solution.py:55
  183.9 19.7 %collective-permute-start.21 = (bf16[32,1536]{1,0:T(8,128)(2,1)S(1)}, bf16[32,1536]{1,0:T(8,128)(2,1)S(1)}, u32[]{:S(2)}, u32[]{:S(2)}) collective-permute-start(bf16[32,1536]{1,0:T(8,128)(2,1)S(1)} %add_convert_fusion.30), channel_id=1, source_target_pairs={{0,16},{1,17},{2,18},{3,19},{4,20},{5,21},{6,22},{7,23},{8,24},{9,... | collective-permute-start | bytes 294920 | tf_op jit(solution)/shard_map/ppermute | solution.py:55
  186.6 24.0 %collective-permute-start.13 = (bf16[32,1536]{1,0:T(8,128)(2,1)S(1)}, bf16[32,1536]{1,0:T(8,128)(2,1)S(1)}, u32[]{:S(2)}, u32[]{:S(2)}) collective-permute-start(bf16[32,1536]{1,0:T(8,128)(2,1)S(1)} %add_convert_fusion.36), channel_id=1, source_target_pairs={{0,16},{1,17},{2,18},{3,19},{4,20},{5,21},{6,22},{7,23},{8,24},{9,... | collective-permute-start | bytes 294920 | tf_op jit(solution)/shard_map/ppermute | solution.py:55
  210.0 8.9 %collective-permute-start.28 = (bf16[64,2560]{1,0:T(8,128)(2,1)S(1)}, bf16[64,2560]{1,0:T(8,128)(2,1)S(1)}, u32[]{:S(2)}, u32[]{:S(2)}) collective-permute-start(bf16[64,2560]{1,0:T(8,128)(2,1)S(1)} %pad_maximum_fusion), channel_id=1, source_target_pairs={{0,8},{1,9},{2,10},{3,11},{4,12},{5,13},{6,14},{7,15},{8,0},{9,1},... | collective-permute-start | bytes 983048 | tf_op jit(solution)/shard_map/ppermute | solution.py:55
  (19 other events, 116.1 us)

commit v2 on v1

--- a/solution.py
+++ b/solution.py
@@ -176,6 +176,7 @@
         out_shape=outs,
         input_output_aliases=aliases,
         cost_estimate=cost(2 * four * half * width * (4 * width + vocab), 16e6),
+        compiler_params=pltpu.CompilerParams(vmem_limit_bytes=24 << 20),
         name="project",
     )(*args)
 
@@ -243,6 +244,7 @@
         ],
         scratch_shapes=[pltpu.VMEM((PATCH * GROUP, 2 * PATCH * GROUP), F32)],
         cost_estimate=cost(count * groups * 6 * 2 * 256 * 256 * 128, count * 1.6e6),
+        compiler_params=pltpu.CompilerParams(vmem_limit_bytes=12 << 20),
         name="attention",
     )(qkv, qkv, qkv, d_context, *after)
 
@@ -381,6 +383,7 @@
         ),
         out_shape=[out] * (2 * len(kinds)),
         cost_estimate=cost(2 * tokens * rows * steps * block, 2 * rows * steps * block + 4e6),
+        compiler_params=pltpu.CompilerParams(vmem_limit_bytes=20 << 20),
         name="grad_rows",
     )(place, *lhs, rhs, *extra, *after)
     return [(got[n], got[n + 1]) for n in range(0, len(got), 2)]
@@ -456,6 +459,7 @@
         ],
         scratch_shapes=[pltpu.VMEM((tokens, width), F32)],
         cost_estimate=cost(2 * tokens * width * 3 * width, 20e6),
+        compiler_params=pltpu.CompilerParams(vmem_limit_bytes=28 << 20),
         name="input_grad",
     )(*d_qkvs, *([w_qkv] * chunks), normed, inv, gain, out_grad, *after)
 
@@ -493,6 +497,7 @@
         ),
         out_shape=[out] * tp,
         cost_estimate=cost(2 * PATCH * half * width * width, 6e6),
+        compiler_params=pltpu.CompilerParams(vmem_limit_bytes=16 << 20),
         name="back",
     )(place, d_x, w_proj, *after)
 

time: 229 us -> 204 us (0.89)
  Pallas kernels: 101 us -> 71.2 us
  other arithmetic: 7.4 us -> 3.41 us
  waiting for transfers between devices: 70.4 us -> 73.9 us
  local copies, waits for them, and re-layouts: 12.7 us -> 15.7 us
  starting transfers between devices: 31.2 us -> 34.1 us
    pallas_call x4, Pallas kernels: 32.6 us -> 20.4 us  [grad_rows(): pl.pallas_call(functools.partial(grad_kernel, sources=len(lhs), orders=[(...]
    pallas_call x2, Pallas kernels: 23.7 us -> 15.5 us  [project(): pl.pallas_call(functools.partial(project_kernel, alias=earlier is not Non...]
    unnamed x31 -> x37, local copies, waits for them, and re-layouts: 1.96 us -> 6.62 us
    pallas_call x1, Pallas kernels: 19.6 us -> 15.1 us  [input_grad(): pl.pallas_call(functools.partial(input_grad_kernel, chunks=chunks), grid=...]
    ppermute x30, waiting for transfers between devices: 70.4 us -> 73.9 us  [exchange(): return lax.ppermute(block, AXES, [(d, d ^ mask) for d in range(devices)])]
    pallas_call x1, Pallas kernels: 5.73 us -> 2.5 us  [back(): pl.pallas_call(functools.partial(back_kernel, count=tp), grid_spec=pltpu....]
    ppermute x30, starting transfers between devices: 31.2 us -> 34.1 us  [exchange(): return lax.ppermute(block, AXES, [(d, d ^ mask) for d in range(devices)])]
    convert_element_type x21, other arithmetic: 5.33 us -> 2.84 us  [combine(): (k[part].astype(F32) + g[part].astype(F32)).astype(BF16)]
  transfers between devices with their start and end apart: 30 -> 30, of which waited for: 11 -> 13; matrix products, arithmetic and copies ran while one was open for 9% -> 7% of each run, Pallas kernels for 12% -> 8%
where the time goes in v2:
time: 204 us
  waiting for transfers between devices  73.9 us (36%)
  Pallas kernels  71.2 us (35%)
  starting transfers between devices  34.1 us (17%)
  local copies, waits for them, and re-layouts  15.7 us (8%)
  matrix products  4.61 us (2%)
  other arithmetic  3.41 us (2%)
    ppermute x30, waiting for transfers between devices, exchange(): return lax.ppermute(block, AXES, [(d, d ^ mask) for d in range(devices)])  73.9 us
    ppermute x30, starting transfers between devices, exchange(): return lax.ppermute(block, AXES, [(d, d ^ mask) for d in range(devices)])  34.1 us
    pallas_call x4, Pallas kernels, grad_rows(): pl.pallas_call(functools.partial(grad_kernel, sources=len(lhs), orders=[(...  20.4 us
    pallas_call x2, Pallas kernels, attention(): pl.pallas_call(attention_kernel, grid=(count,), in_specs=[spec(0), spec(1...  17.7 us
    pallas_call x2, Pallas kernels, project(): pl.pallas_call(functools.partial(project_kernel, alias=earlier is not Non...  15.5 us
    pallas_call x1, Pallas kernels, input_grad(): pl.pallas_call(functools.partial(input_grad_kernel, chunks=chunks), grid=...  15.1 us
    unnamed x37, local copies, waits for them, and re-layouts  6.62 us
    dot_general x1, matrix products, on_device(): lax.dot_general(grads, w_out, (((3,), (1,)), ((), ())), preferred_element...  4.61 us
  transfers between devices with their start and end apart: 30, of which 13 were waited for; matrix products, arithmetic and copies ran while one was open for 7% of the time, Pallas kernels for 8%

profile of v2, /device:TPU:0, one launch (start us, length us, event | category | flops | bytes accessed | tf_op | source)
XLA Modules:
  0.0 204.2 jit_solution(768999064912439058)
XLA Ops:
  3.6 2.5 %collective-permute-start = (bf16[96,2048]{1,0:T(8,128)(2,1)}, bf16[96,2048]{1,0:T(8,128)(2,1)}, u32[]{:S(2)}, u32[]{:S(2)}) collective-permute-start(bf16[96,2048]{1,0:T(8,128)(2,1)} %get-tuple-element.86), channel_id=1, source_target_pairs={{0,2},{1,3},{2,0},{3,1},{4,6},{5,7},{6,4},{7,5},{8,10},{9,11},{10,... | collective-permute-start | bytes 1179656 | tf_op jit(solution)/shard_map/ppermute | solution.py:55
  6.3 4.6 %fusion.2.d_ref = bf16[6,8,16,1024]{3,2,1,0:T(8,128)(2,1)} fusion(bf16[1024,1024]{1,0:T(8,128)(2,1)S(1)} %copy-done, bf16[6,16,8,1024]{3,2,1,0:T(8,128)(2,1)} %bitcast.34), kind=kOutput, calls=%fused_computation.2 | convolution fusion | flops 1611399168 | bytes 5242880 | tf_op jit(solution)/shard_map/dot_general | solution.py:545
  11.3 3.6 %copy.26 = bf16[6,16,8,1024]{3,1,2,0:T(8,128)(2,1)} copy(bf16[6,16,8,1024]{3,2,1,0:T(8,128)(2,1)} %bitcast.35) | data formatting | bytes 3145728 | tf_op jit(solution)/shard_map/reshape | solution.py:544
  15.1 2.8 %copy-done.2 = bf16[1024,3072]{1,0:T(8,128)(2,1)S(1)} copy-done((bf16[1024,3072]{1,0:T(8,128)(2,1)S(1)}, bf16[1024,3072]{1,0:T(8,128)(2,1)}, u32[]{:S(2)}) %copy-start.2) | copy-done | bytes 6291480
  20.9 8.0 %project.2 = (bf16[6,8,16,1024]{3,2,1,0:T(8,128)(2,1)S(1)}, f32[6,8,16,1024]{3,2,1,0:T(8,128)S(1)}, f32[6,8,16,128]{3,2,1,0:T(8,128)S(1)}, bf16[6,8,16,1024]{3,2...) custom-call(s32[5]{0:T(128)S(1)} %stack.23.place, bf16[384,2048]{1,0:T(8,128)(2,1)S(1)} %copy-done.8, ...), custom_call_target="tpu_custom_call" | custom-call | flops 3422552064 | bytes 16000000 | tf_op jit(solution)/shard_map/project/pallas_call | solution.py:167
  28.9 7.5 %project.3 = (bf16[6,8,16,1024]{3,2,1,0:T(8,128)(2,1)S(1)}, f32[6,8,16,1024]{3,2,1,0:T(8,128)S(1)}, f32[6,8,16,128]{3,2,1,0:T(8,128)S(1)}, bf16[6,8,16,1024]{3,2...) custom-call(s32[5]{0:T(128)S(1)} %stack.23.place, ...), custom_call_target="tpu_custom_call", output_to_operand_aliasing={{0}: (8, {}), {1}: (9, {}), {2}: (10, {}), {3}: (11, {}), {... | custom-call | flops 3422552064 | bytes 16000000 | tf_op jit(solution)/shard_map/project/pallas_call | solution.py:167
  36.5 8.8 %attention.2 = (bf16[512,768]{1,0:T(8,128)(2,1)S(1)}, bf16[3,6,8,16,512]{4,3,2,1,0:T(8,128)(2,1)S(1)}) custom-call(bf16[6,8,16,3072]{3,2,1,0:T(8,128)(2,1)S(1)} %get-tuple-element.43.q_ref.k_ref.v_ref, bf16[6,8,16,3072]{3,2,1,0:T(8,128)(2,1)S(1)} %get-tuple-element.43.q_ref.k_ref.v_ref, bf16[6,8,16,3072]{3,2,1,0:T(8,128)(2,1)S(1)} %get-tuple-element.43.q_ref.k_ref.v_ref, ...), custom_call_target="tpu_custom_call" | custom-call | flops 2415919104 | bytes 6400000 | tf_op jit(solution)/shard_map/attention/pallas_call | solution.py:232
  45.3 5.4 %grad_rows.4 = (bf16[512,768]{1,0:T(8,128)(2,1)S(1)}, bf16[512,768]{1,0:T(8,128)(2,1)S(1)}, bf16[512,768]{1,0:T(8,128)(2,1)S(1)}, bf16[512,768]{1,0:T(8,128)(2,1)S(1)}) custom-call(s32[5]{0:T(128)S(1)} %stack.23.place, bf16[6,8,16,1024]{3,2,1,0:T(8,128)(2,1)S(1)} %get-tuple-element.45.refs_0_, bf16[3,6,8,16,512]{4,3,2,1,0:T(8,128)(2,1)S(1)} %get-tuple-element.44.refs_1_.refs_0_), custom_call_target="tpu_custom_call" | custom-call | flops 2415919104 | bytes 7145728 | tf_op jit(solution)/shard_map/grad_rows/pallas_call | solution.py:366
  50.7 8.9 %attention.3 = (bf16[512,768]{1,0:T(8,128)(2,1)S(1)}, bf16[3,6,8,16,512]{4,3,2,1,0:T(8,128)(2,1)S(1)}) custom-call(bf16[6,8,16,3072]{3,2,1,0:T(8,128)(2,1)S(1)} %get-tuple-element.43.q_ref.k_ref.v_ref, bf16[6,8,16,3072]{3,2,1,0:T(8,128)(2,1)S(1)} %get-tuple-element.43.q_ref.k_ref.v_ref, bf16[6,8,16,3072]{3,2,1,0:T(8,128)(2,1)S(1)} %get-tuple-element.43.q_ref.k_ref.v_ref, ...), custom_call_target="tpu_custom_call" | custom-call | flops 2415919104 | bytes 6400000 | tf_op jit(solution)/shard_map/attention/pallas_call | solution.py:232
  59.6 15.1 %input_grad.1 = (bf16[6,8,16,1024]{3,2,1,0:T(8,128)(2,1)S(1)}, f32[8,1024]{1,0:T(8,128)S(1)}) custom-call(bf16[3,6,8,16,512]{4,3,2,1,0:T(8,128)(2,1)S(1)} %get-tuple-element.44.refs_1_.refs_0_, bf16[3,6,8,16,512]{4,3,2,1,0:T(8,128)(2,1)S(1)} %get-tuple-element.47.refs_1_, bf16[1024,3072]{1,0:T(8,128)(2,1)S(1)} %bitcast.28, bf16[1024,3072]{1,0:T(8,128)(2,1)S(1)} %bitcast.28, ...), custom_call_target="tpu_custom_call" | custom-call | flops 4831838208 | bytes 20000000 | tf_op jit(solution)/shard_map/input_grad/pallas_call | solution.py:445
  74.8 6.3 %grad_rows.5 = (bf16[512,768]{1,0:T(8,128)(2,1)S(1)}, bf16[512,768]{1,0:T(8,128)(2,1)S(1)}, bf16[512,768]{1,0:T(8,128)(2,1)S(1)}, bf16[512,768]{1,0:T(8,128)(2,1)S(1)}) custom-call(s32[5]{0:T(128)S(1)} %stack.23.place, bf16[6,8,16,1024]{3,2,1,0:T(8,128)(2,1)S(1)} %get-tuple-element.51.refs_0_, ...), custom_call_target="tpu_custom_call" | custom-call | flops 2415919104 | bytes 7145728 | tf_op jit(solution)/shard_map/grad_rows/pallas_call | solution.py:366
  81.1 2.5 %back.1 = (bf16[96,2048]{1,0:T(8,128)(2,1)S(1)}, bf16[96,2048]{1,0:T(8,128)(2,1)S(1)}, bf16[96,2048]{1,0:T(8,128)(2,1)S(1)}, bf16[96,2048]{1,0:T(8,128)(2,1)S(1)}) custom-call(s32[5]{0:T(128)S(1)} %stack.23.place, bf16[6,8,16,1024]{3,2,1,0:T(8,128)(2,1)S(1)} %get-tuple-element.50.refs_1_.d_x_ref, bf16[1024,1024]{1,0:T(8,128)(2,1)S(1)} %copy-done.7, ...), custom_call_target="tpu_custom_call" | custom-call | flops 1610612736 | bytes 6000000 | tf_op jit(solution)/shard_map/back/pallas_call | solution.py:488
  83.8 5.2 %grad_rows.6 = (bf16[512,1536]{1,0:T(8,128)(2,1)S(1)}, bf16[512,1536]{1,0:T(8,128)(2,1)S(1)}) custom-call(s32[5]{0:T(128)S(1)} %stack.23.place, bf16[6,8,16,1024]{3,2,1,0:T(8,128)(2,1)S(1)} %get-tuple-element.45.refs_0_, bf16[3,6,8,16,512]{4,3,2,1,0:T(8,128)(2,1)S(1)} %get-tuple-element.47.refs_1_), custom_call_target="tpu_custom_call" | custom-call | flops 2415919104 | bytes 7145728 | tf_op jit(solution)/shard_map/grad_rows/pallas_call | solution.py:366
  91.9 3.6 %grad_rows.7 = (bf16[512,1024]{1,0:T(8,128)(2,1)S(1)}, bf16[512,1024]{1,0:T(8,128)(2,1)S(1)}) custom-call(s32[5]{0:T(128)S(1)} %stack.23.place, bf16[512,768]{1,0:T(8,128)(2,1)S(1)} %get-tuple-element.66.refs_0_, bf16[512,768]{1,0:T(8,128)(2,1)S(1)} %get-tuple-element.67.refs_1_, bf16[6,8,16,1024]{3,2,1,0:T(8,128)(2,1)S(1)} %bitcast.30, ...), custom_call_target="tpu_custom_call" | custom-call | flops 1610612736 | bytes 6097152 | tf_op jit(solution)/shard_map/grad_rows/pallas_call | solution.py:366
  95.6 6.3 %collective-permute-done.4 = bf16[96,2048]{1,0:T(8,128)(2,1)S(1)} collective-permute-done((bf16[96,2048]{1,0:T(8,128)(2,1)S(1)}, bf16[96,2048]{1,0:T(8,128)(2,1)S(1)}, u32[]{:S(2)}, u32[]{:S(2)}) %collective-permute-start.4) | collective-permute-done | bytes 393248 | tf_op jit(solution)/shard_map/ppermute | solution.py:55
  101.9 7.0 %collective-permute-done.5 = bf16[96,2048]{1,0:T(8,128)(2,1)S(1)} collective-permute-done((bf16[96,2048]{1,0:T(8,128)(2,1)S(1)}, bf16[96,2048]{1,0:T(8,128)(2,1)S(1)}, u32[]{:S(2)}, u32[]{:S(2)}) %collective-permute-start.5) | collective-permute-done | bytes 393248 | tf_op jit(solution)/shard_map/ppermute | solution.py:55
  116.8 5.1 %collective-permute-done.15 = bf16[256,768]{1,0:T(8,128)(2,1)S(1)} collective-permute-done((bf16[256,768]{1,0:T(8,128)(2,1)S(1)}, bf16[256,768]{1,0:T(8,128)(2,1)S(1)}, u32[]{:S(2)}, u32[]{:S(2)}) %collective-permute-start.15) | collective-permute-done | bytes 393248 | tf_op jit(solution)/shard_map/ppermute | solution.py:55
  125.5 4.3 %collective-permute-done.7 = bf16[256,768]{1,0:T(8,128)(2,1)S(1)} collective-permute-done((bf16[256,768]{1,0:T(8,128)(2,1)S(1)}, bf16[256,768]{1,0:T(8,128)(2,1)S(1)}, u32[]{:S(2)}, u32[]{:S(2)}) %collective-permute-start.7) | collective-permute-done | bytes 393248 | tf_op jit(solution)/shard_map/ppermute | solution.py:55
  133.9 13.8 %collective-permute-done.16 = bf16[128,768]{1,0:T(8,128)(2,1)S(1)} collective-permute-done((bf16[128,768]{1,0:T(8,128)(2,1)S(1)}, bf16[128,768]{1,0:T(8,128)(2,1)S(1)}, u32[]{:S(2)}, u32[]{:S(2)}) %collective-permute-start.16) | collective-permute-done | bytes 196640 | tf_op jit(solution)/shard_map/ppermute | solution.py:55
  157.9 2.6 %collective-permute-start.21 = (bf16[32,1536]{1,0:T(8,128)(2,1)S(1)}, bf16[32,1536]{1,0:T(8,128)(2,1)S(1)}, u32[]{:S(2)}, u32[]{:S(2)}) collective-permute-start(bf16[32,1536]{1,0:T(8,128)(2,1)S(1)} %add_convert_fusion.30), channel_id=1, source_target_pairs={{0,16},{1,17},{2,18},{3,19},{4,20},{5,21},{6,22},{7,23},{8,24},{9,... | collective-permute-start | bytes 294920 | tf_op jit(solution)/shard_map/ppermute | solution.py:55
  162.9 15.0 %collective-permute-done.23 = bf16[256,1536]{1,0:T(8,128)(2,1)S(1)} collective-permute-done((bf16[256,1536]{1,0:T(8,128)(2,1)S(1)}, bf16[256,1536]{1,0:T(8,128)(2,1)S(1)}, u32[]{:S(2)}, u32[]{:S(2)}) %collective-permute-start.23) | collective-permute-done | bytes 786464 | tf_op jit(solution)/shard_map/ppermute | solution.py:55
  179.9 6.1 %collective-permute-done.24 = bf16[128,1536]{1,0:T(8,128)(2,1)S(1)} collective-permute-done((bf16[128,1536]{1,0:T(8,128)(2,1)S(1)}, bf16[128,1536]{1,0:T(8,128)(2,1)S(1)}, u32[]{:S(2)}, u32[]{:S(2)}) %collective-permute-start.24) | collective-permute-done | bytes 393248 | tf_op jit(solution)/shard_map/ppermute | solution.py:55
  186.7 8.3 %collective-permute-done.28 = bf16[64,2560]{1,0:T(8,128)(2,1)S(1)} collective-permute-done((bf16[64,2560]{1,0:T(8,128)(2,1)S(1)}, bf16[64,2560]{1,0:T(8,128)(2,1)S(1)}, u32[]{:S(2)}, u32[]{:S(2)}) %collective-permute-start.28) | collective-permute-done | bytes 327712 | tf_op jit(solution)/shard_map/ppermute | solution.py:55
  198.9 3.7 %collective-permute-done.29 = bf16[32,2560]{1,0:T(8,128)(2,1)S(1)} collective-permute-done((bf16[32,2560]{1,0:T(8,128)(2,1)S(1)}, bf16[32,2560]{1,0:T(8,128)(2,1)S(1)}, u32[]{:S(2)}, u32[]{:S(2)}) %collective-permute-start.29) | collective-permute-done | bytes 163872 | tf_op jit(solution)/shard_map/ppermute | solution.py:55
  (131 shorter events, 45.8 us)
Async XLA Ops:
  3.1 12.0 %collective-permute-start.2 = (bf16[96,2048]{1,0:T(8,128)(2,1)}, bf16[96,2048]{1,0:T(8,128)(2,1)}, u32[]{:S(2)}, u32[]{:S(2)}) collective-permute-start(bf16[96,2048]{1,0:T(8,128)(2,1)} %get-tuple-element.84), channel_id=1, source_target_pairs={{0,1},{1,0},{2,3},{3,2},{4,5},{5,4},{6,7},{7,6},{8,9},{9,8},{10,11... | collective-permute-start | bytes 1179656 | tf_op jit(solution)/shard_map/ppermute | solution.py:55
  3.6 25.3 %collective-permute-start = (bf16[96,2048]{1,0:T(8,128)(2,1)}, bf16[96,2048]{1,0:T(8,128)(2,1)}, u32[]{:S(2)}, u32[]{:S(2)}) collective-permute-start(bf16[96,2048]{1,0:T(8,128)(2,1)} %get-tuple-element.86), channel_id=1, source_target_pairs={{0,2},{1,3},{2,0},{3,1},{4,6},{5,7},{6,4},{7,5},{8,10},{9,11},{10,... | collective-permute-start | bytes 1179656 | tf_op jit(solution)/shard_map/ppermute | solution.py:55
  6.1 22.8 %collective-permute-start.1 = (bf16[96,2048]{1,0:T(8,128)(2,1)}, bf16[96,2048]{1,0:T(8,128)(2,1)}, u32[]{:S(2)}, u32[]{:S(2)}) collective-permute-start(bf16[96,2048]{1,0:T(8,128)(2,1)} %get-tuple-element.85), channel_id=1, source_target_pairs={{0,3},{1,2},{2,1},{3,0},{4,7},{5,6},{6,5},{7,4},{8,11},{9,10},{10,... | collective-permute-start | bytes 1179656 | tf_op jit(solution)/shard_map/ppermute | solution.py:55
  83.6 11.9 %collective-permute-start.3 = (bf16[96,2048]{1,0:T(8,128)(2,1)S(1)}, bf16[96,2048]{1,0:T(8,128)(2,1)S(1)}, u32[]{:S(2)}, u32[]{:S(2)}) collective-permute-start(bf16[96,2048]{1,0:T(8,128)(2,1)S(1)} %get-tuple-element.55), channel_id=1, source_target_pairs={{0,1},{1,0},{2,3},{3,2},{4,5},{5,4},{6,7},{7,6},{8,9},{9,8},{10,11... | collective-permute-start | bytes 1179656 | tf_op jit(solution)/shard_map/ppermute | solution.py:55
  88.9 67.0 %collective-permute-start.22 = (bf16[512,1536]{1,0:T(8,128)(2,1)S(1)}, bf16[512,1536]{1,0:T(8,128)(2,1)S(1)}, u32[]{:S(2)}, u32[]{:S(2)}) collective-permute-start(bf16[512,1536]{1,0:T(8,128)(2,1)S(1)} %get-tuple-element.65), channel_id=1, source_target_pairs={{0,1},{1,0},{2,3},{3,2},{4,5},{5,4},{6,7},{7,6},{8,9},{9,8},{10,11... | collective-permute-start | bytes 4718600 | tf_op jit(solution)/shard_map/ppermute | solution.py:55
  89.4 20.1 %collective-permute-start.14 = (bf16[512,768]{1,0:T(8,128)(2,1)S(1)}, bf16[512,768]{1,0:T(8,128)(2,1)S(1)}, u32[]{:S(2)}, u32[]{:S(2)}) collective-permute-start(bf16[512,768]{1,0:T(8,128)(2,1)S(1)} %get-tuple-element.61), channel_id=1, source_target_pairs={{0,1},{1,0},{2,3},{3,2},{4,5},{5,4},{6,7},{7,6},{8,9},{9,8},{10,11... | collective-permute-start | bytes 2359304 | tf_op jit(solution)/shard_map/ppermute | solution.py:55
  89.5 20.3 %collective-permute-start.17 = (bf16[512,768]{1,0:T(8,128)(2,1)S(1)}, bf16[512,768]{1,0:T(8,128)(2,1)S(1)}, u32[]{:S(2)}, u32[]{:S(2)}) collective-permute-start(bf16[512,768]{1,0:T(8,128)(2,1)S(1)} %get-tuple-element.63), channel_id=1, source_target_pairs={{0,1},{1,0},{2,3},{3,2},{4,5},{5,4},{6,7},{7,6},{8,9},{9,8},{10,11... | collective-permute-start | bytes 2359304 | tf_op jit(solution)/shard_map/ppermute | solution.py:55
  89.9 12.0 %collective-permute-start.4 = (bf16[96,2048]{1,0:T(8,128)(2,1)S(1)}, bf16[96,2048]{1,0:T(8,128)(2,1)S(1)}, u32[]{:S(2)}, u32[]{:S(2)}) collective-permute-start(bf16[96,2048]{1,0:T(8,128)(2,1)S(1)} %get-tuple-element.56), channel_id=1, source_target_pairs={{0,2},{1,3},{2,0},{3,1},{4,6},{5,7},{6,4},{7,5},{8,10},{9,11},{10,... | collective-permute-start | bytes 1179656 | tf_op jit(solution)/shard_map/ppermute | solution.py:55
  95.4 13.5 %collective-permute-start.5 = (bf16[96,2048]{1,0:T(8,128)(2,1)S(1)}, bf16[96,2048]{1,0:T(8,128)(2,1)S(1)}, u32[]{:S(2)}, u32[]{:S(2)}) collective-permute-start(bf16[96,2048]{1,0:T(8,128)(2,1)S(1)} %get-tuple-element.57), channel_id=1, source_target_pairs={{0,3},{1,2},{2,1},{3,0},{4,7},{5,6},{6,5},{7,4},{8,11},{9,10},{10,... | collective-permute-start | bytes 1179656 | tf_op jit(solution)/shard_map/ppermute | solution.py:55
  101.9 9.9 %collective-permute-start.6 = (bf16[512,768]{1,0:T(8,128)(2,1)S(1)}, bf16[512,768]{1,0:T(8,128)(2,1)S(1)}, u32[]{:S(2)}, u32[]{:S(2)}) collective-permute-start(bf16[512,768]{1,0:T(8,128)(2,1)S(1)} %get-tuple-element.58), channel_id=1, source_target_pairs={{0,1},{1,0},{2,3},{3,2},{4,5},{5,4},{6,7},{7,6},{8,9},{9,8},{10,11... | collective-permute-start | bytes 2359304 | tf_op jit(solution)/shard_map/ppermute | solution.py:55
  109.8 12.1 %collective-permute-start.15 = (bf16[256,768]{1,0:T(8,128)(2,1)S(1)}, bf16[256,768]{1,0:T(8,128)(2,1)S(1)}, u32[]{:S(2)}, u32[]{:S(2)}) collective-permute-start(bf16[256,768]{1,0:T(8,128)(2,1)S(1)} %get-tuple-element.77), channel_id=1, source_target_pairs={{0,2},{1,3},{2,0},{3,1},{4,6},{5,7},{6,4},{7,5},{8,10},{9,11},{10,... | collective-permute-start | bytes 1179656 | tf_op jit(solution)/shard_map/ppermute | solution.py:55
  111.8 12.1 %collective-permute-start.18 = (bf16[256,768]{1,0:T(8,128)(2,1)S(1)}, bf16[256,768]{1,0:T(8,128)(2,1)S(1)}, u32[]{:S(2)}, u32[]{:S(2)}) collective-permute-start(bf16[256,768]{1,0:T(8,128)(2,1)S(1)} %get-tuple-element.79), channel_id=1, source_target_pairs={{0,4},{1,5},{2,6},{3,7},{4,0},{5,1},{6,2},{7,3},{8,12},{9,13},{10,... | collective-permute-start | bytes 1179656 | tf_op jit(solution)/shard_map/ppermute | solution.py:55
  113.6 16.2 %collective-permute-start.7 = (bf16[256,768]{1,0:T(8,128)(2,1)S(1)}, bf16[256,768]{1,0:T(8,128)(2,1)S(1)}, u32[]{:S(2)}, u32[]{:S(2)}) collective-permute-start(bf16[256,768]{1,0:T(8,128)(2,1)S(1)} %get-tuple-element.81), channel_id=1, source_target_pairs={{0,2},{1,3},{2,0},{3,1},{4,6},{5,7},{6,4},{7,5},{8,10},{9,11},{10,... | collective-permute-start | bytes 1179656 | tf_op jit(solution)/shard_map/ppermute | solution.py:55
  114.8 17.5 %collective-permute-start.10 = (bf16[256,768]{1,0:T(8,128)(2,1)S(1)}, bf16[256,768]{1,0:T(8,128)(2,1)S(1)}, u32[]{:S(2)}, u32[]{:S(2)}) collective-permute-start(bf16[256,768]{1,0:T(8,128)(2,1)S(1)} %get-tuple-element.83), channel_id=1, source_target_pairs={{0,4},{1,5},{2,6},{3,7},{4,0},{5,1},{6,2},{7,3},{8,12},{9,13},{10,... | collective-permute-start | bytes 1179656 | tf_op jit(solution)/shard_map/ppermute | solution.py:55
  121.9 33.3 %collective-permute-start.26 = (bf16[256,1024]{1,0:T(8,128)(2,1)S(1)}, bf16[256,1024]{1,0:T(8,128)(2,1)S(1)}, u32[]{:S(2)}, u32[]{:S(2)}) collective-permute-start(bf16[256,1024]{1,0:T(8,128)(2,1)S(1)} %get-tuple-element.73), channel_id=1, source_target_pairs={{0,4},{1,5},{2,6},{3,7},{4,0},{5,1},{6,2},{7,3},{8,12},{9,13},{10,... | collective-permute-start | bytes 1572872 | tf_op jit(solution)/shard_map/ppermute | solution.py:55
  123.9 23.9 %collective-permute-start.16 = (bf16[128,768]{1,0:T(8,128)(2,1)S(1)}, bf16[128,768]{1,0:T(8,128)(2,1)S(1)}, u32[]{:S(2)}, u32[]{:S(2)}) collective-permute-start(bf16[128,768]{1,0:T(8,128)(2,1)S(1)} %get-tuple-element.92), channel_id=1, source_target_pairs={{0,4},{1,5},{2,6},{3,7},{4,0},{5,1},{6,2},{7,3},{8,12},{9,13},{10,... | collective-permute-start | bytes 589832 | tf_op jit(solution)/shard_map/ppermute | solution.py:55
  129.8 18.5 %collective-permute-start.19 = (bf16[128,768]{1,0:T(8,128)(2,1)S(1)}, bf16[128,768]{1,0:T(8,128)(2,1)S(1)}, u32[]{:S(2)}, u32[]{:S(2)}) collective-permute-start(bf16[128,768]{1,0:T(8,128)(2,1)S(1)} %get-tuple-element.94), channel_id=1, source_target_pairs={{0,2},{1,3},{2,0},{3,1},{4,6},{5,7},{6,4},{7,5},{8,10},{9,11},{10,... | collective-permute-start | bytes 589832 | tf_op jit(solution)/shard_map/ppermute | solution.py:55
  132.3 18.9 %collective-permute-start.8 = (bf16[128,768]{1,0:T(8,128)(2,1)S(1)}, bf16[128,768]{1,0:T(8,128)(2,1)S(1)}, u32[]{:S(2)}, u32[]{:S(2)}) collective-permute-start(bf16[128,768]{1,0:T(8,128)(2,1)S(1)} %get-tuple-element.96), channel_id=1, source_target_pairs={{0,4},{1,5},{2,6},{3,7},{4,0},{5,1},{6,2},{7,3},{8,12},{9,13},{10,... | collective-permute-start | bytes 589832 | tf_op jit(solution)/shard_map/ppermute | solution.py:55
  148.4 9.5 %collective-permute-start.20 = (bf16[64,1536]{1,0:T(8,128)(2,1)S(1)}, bf16[64,1536]{1,0:T(8,128)(2,1)S(1)}, u32[]{:S(2)}, u32[]{:S(2)}) collective-permute-start(bf16[64,1536]{1,0:T(8,128)(2,1)S(1)} %pad_maximum_fusion.2), channel_id=1, source_target_pairs={{0,8},{1,9},{2,10},{3,11},{4,12},{5,13},{6,14},{7,15},{8,0},{9,1},... | collective-permute-start | bytes 589832 | tf_op jit(solution)/shard_map/ppermute | solution.py:55
  155.3 24.5 %collective-permute-start.27 = (bf16[128,1024]{1,0:T(8,128)(2,1)S(1)}, bf16[128,1024]{1,0:T(8,128)(2,1)S(1)}, u32[]{:S(2)}, u32[]{:S(2)}) collective-permute-start(bf16[128,1024]{1,0:T(8,128)(2,1)S(1)} %get-tuple-element.88), channel_id=1, source_target_pairs={{0,2},{1,3},{2,0},{3,1},{4,6},{5,7},{6,4},{7,5},{8,10},{9,11},{10,... | collective-permute-start | bytes 786440 | tf_op jit(solution)/shard_map/ppermute | solution.py:55
  156.3 21.6 %collective-permute-start.23 = (bf16[256,1536]{1,0:T(8,128)(2,1)S(1)}, bf16[256,1536]{1,0:T(8,128)(2,1)S(1)}, u32[]{:S(2)}, u32[]{:S(2)}) collective-permute-start(bf16[256,1536]{1,0:T(8,128)(2,1)S(1)} %get-tuple-element.71), channel_id=1, source_target_pairs={{0,2},{1,3},{2,0},{3,1},{4,6},{5,7},{6,4},{7,5},{8,10},{9,11},{10,... | collective-permute-start | bytes 2359304 | tf_op jit(solution)/shard_map/ppermute | solution.py:55
  157.9 21.8 %collective-permute-start.21 = (bf16[32,1536]{1,0:T(8,128)(2,1)S(1)}, bf16[32,1536]{1,0:T(8,128)(2,1)S(1)}, u32[]{:S(2)}, u32[]{:S(2)}) collective-permute-start(bf16[32,1536]{1,0:T(8,128)(2,1)S(1)} %add_convert_fusion.30), channel_id=1, source_target_pairs={{0,16},{1,17},{2,18},{3,19},{4,20},{5,21},{6,22},{7,23},{8,24},{9,... | collective-permute-start | bytes 294920 | tf_op jit(solution)/shard_map/ppermute | solution.py:55
  160.6 26.0 %collective-permute-start.13 = (bf16[32,1536]{1,0:T(8,128)(2,1)S(1)}, bf16[32,1536]{1,0:T(8,128)(2,1)S(1)}, u32[]{:S(2)}, u32[]{:S(2)}) collective-permute-start(bf16[32,1536]{1,0:T(8,128)(2,1)S(1)} %add_convert_fusion.36), channel_id=1, source_target_pairs={{0,16},{1,17},{2,18},{3,19},{4,20},{5,21},{6,22},{7,23},{8,24},{9,... | collective-permute-start | bytes 294920 | tf_op jit(solution)/shard_map/ppermute | solution.py:55
  186.2 8.9 %collective-permute-start.28 = (bf16[64,2560]{1,0:T(8,128)(2,1)S(1)}, bf16[64,2560]{1,0:T(8,128)(2,1)S(1)}, u32[]{:S(2)}, u32[]{:S(2)}) collective-permute-start(bf16[64,2560]{1,0:T(8,128)(2,1)S(1)} %pad_maximum_fusion), channel_id=1, source_target_pairs={{0,8},{1,9},{2,10},{3,11},{4,12},{5,13},{6,14},{7,15},{8,0},{9,1},... | collective-permute-start | bytes 983048 | tf_op jit(solution)/shard_map/ppermute | solution.py:55
  (22 other events, 140.1 us)

commit v3 on v1

--- a/solution.py
+++ b/solution.py
@@ -108,15 +108,20 @@
             x_ref[:, n : n + 256] = dot(onehot, embed_ref[:, n : n + 256]) + dot(
                 slices, w_proj_ref[:, n : n + 256]
             )
+        tiles = [slice(c, c + 128) for c in range(0, width, 128)]
         for g in range(groups):
             for p in range(four):
-                at = g * tile + p * GROUP
-                x = x_ref[at : at + GROUP, :]
-                inv = lax.rsqrt(jnp.mean(x * x, axis=1, keepdims=True) + 1e-05)
-                normed = x * inv
-                normed_ref[g, p] = normed
-                inv_ref[g, p] = jnp.broadcast_to(inv, (GROUP, 128))
-                act_ref[g, p] = (normed * gain_ref[...]).astype(BF16)
+                at = slice(g * tile + p * GROUP, g * tile + (p + 1) * GROUP)
+                square = jnp.zeros((GROUP, 128), F32)
+                for c in tiles:
+                    square = square + x_ref[at, c] * x_ref[at, c]
+                mean = jnp.sum(square, axis=1, keepdims=True) * (1.0 / width)
+                inv = jnp.broadcast_to(lax.rsqrt(mean + 1e-05), (GROUP, 128))
+                inv_ref[g, p] = inv
+                for c in tiles:
+                    normed = x_ref[at, c] * inv
+                    normed_ref[g, p, :, c] = normed
+                    act_ref[g, p, :, c] = (normed * gain_ref[:, c]).astype(BF16)
 
     act = act_ref[...].reshape(rows, width)
     qkv_ref[...] = dot(act, w_qkv_ref[...]).astype(BF16).reshape(qkv_ref.shape)
@@ -138,20 +143,25 @@
     ]
     block = 512
     flip = 0 if earlier is None else 1
+    once = pl.Buffered(1)
     part = lambda cols: pl.BlockSpec(
-        (groups, four, GROUP, cols), lambda n, s: (0, s[0] ^ flip, 0, 0)
-    )
-    first_spec = pl.BlockSpec((half, 2 * width), lambda n, s: (0 if flip else s[2], 0))
+        (groups, four, GROUP, cols), lambda n, s: (0, s[0] ^ flip, 0, 0), pipeline_mode=once
+    )
+    first_spec = pl.BlockSpec(
+        (half, 2 * width), lambda n, s: (0 if flip else s[2], 0), pipeline_mode=once
+    )
     in_specs = [
         first_spec,
-        pl.BlockSpec((half, 2 * width), lambda n, s: (0, 0)),
+        pl.BlockSpec((half, 2 * width), lambda n, s: (0, 0), pipeline_mode=once),
         part(vocab),
-        pl.BlockSpec((vocab, width), lambda n, s: (0, 0)),
-        pl.BlockSpec((width, width), lambda n, s: (0, 0)),
-        pl.BlockSpec((1, width), lambda n, s: (0, 0)),
+        pl.BlockSpec((vocab, width), lambda n, s: (0, 0), pipeline_mode=once),
+        pl.BlockSpec((width, width), lambda n, s: (0, 0), pipeline_mode=once),
+        pl.BlockSpec((1, width), lambda n, s: (0, 0), pipeline_mode=once),
         pl.BlockSpec((width, block), lambda n, s: (0, n)),
     ]
-    args = [place, first, second, onehot, embed, w_proj, gain, w_qkv]
+    keep = lambda a: pltpu.with_memory_space_constraint(a, pltpu.HBM)
+    first = first if flip else keep(first)
+    args = [place, first, second, onehot, embed, keep(w_proj), gain, keep(w_qkv)]
     aliases = {}
     if earlier is not None:
         in_specs += [pl.BlockSpec(memory_space=pl.ANY)] * 5
@@ -176,48 +186,58 @@
         out_shape=outs,
         input_output_aliases=aliases,
         cost_estimate=cost(2 * four * half * width * (4 * width + vocab), 16e6),
+        compiler_params=pltpu.CompilerParams(vmem_limit_bytes=16 << 20),
         name="project",
     )(*args)
 
 
 def attention_kernel(q_ref, k_ref, v_ref, d_ref, *rest):
-    context_ref, d_qkv_ref, mask_ref = rest[-3:]
+    context_ref, d_qkv_ref, bias_ref, own_ref, s_ref, dp_ref, p_ref, ds_ref = rest[-8:]
     rows = PATCH * GROUP
-    scale = HEAD ** (-0.5)
+    groups = q_ref.shape[0]
+    scale = jnp.asarray(HEAD ** (-0.5), BF16)
 
     @pl.when(pl.program_id(0) == 0)
     def _():
-        key = lax.broadcasted_iota(jnp.int32, (rows, 2 * rows), 0)
-        query = lax.broadcasted_iota(jnp.int32, (rows, 2 * rows), 1) % rows
-        seen = (key % GROUP == query % GROUP) & (key // GROUP <= query // GROUP)
-        mask_ref[...] = seen.astype(F32)
+        key = lax.broadcasted_iota(jnp.int32, (rows, rows), 0)
+        query = lax.broadcasted_iota(jnp.int32, (rows, rows), 1)
+        same = key % GROUP == query % GROUP
+        bias_ref[...] = jnp.where(same & (key // GROUP <= query // GROUP), 0.0, -1e30)
+        own_ref[...] = same[:GROUP].astype(F32)
 
     low = lax.broadcasted_iota(jnp.int32, (rows, PAIR), 1) < HEAD
-    own = mask_ref[:GROUP, :] > 0.5
 
     def stack(value):
         zero = jnp.zeros_like(value)
         return jnp.concatenate([jnp.where(low, value, zero), jnp.where(low, zero, value)], axis=0)
 
-    split = lambda value: value.reshape(PATCH, GROUP, 2 * rows)
-    join = lambda value: value.astype(BF16).reshape(rows, 2 * rows)
-    for g in range(q_ref.shape[0]):
-        q, k, v, d = (ref[g].reshape(rows, PAIR) for ref in (q_ref, k_ref, v_ref, d_ref))
-        q2, d2 = stack(q * jnp.asarray(scale, BF16)), stack(d)
-        scores = split(jnp.where(mask_ref[...] > 0.5, dot(k, q2, NT), -1e30))
-        expo = jnp.exp(scores - jnp.max(scores, axis=0, keepdims=True))
-        total = jnp.sum(expo, axis=0, keepdims=True)
-        probs = expo * jnp.where(own, 1.0 / total, 0.0)
-        d_probs = split(dot(v, d2, NT))
-        d_scores = probs * (d_probs - jnp.sum(probs * d_probs, axis=0, keepdims=True))
-        probs, d_scores = join(probs), join(d_scores)
-        context = dot(v.T, probs).astype(BF16)
+    block = lambda ref, g: ref[g].reshape(rows, PAIR)
+    for g in range(groups):
+        s_ref[g] = dot(block(k_ref, g), stack(block(q_ref, g) * scale), NT)
+        dp_ref[g] = dot(block(v_ref, g), stack(block(d_ref, g)), NT)
+    for g in range(groups):
+        for h in range(2):
+            at = slice(h * rows, (h + 1) * rows)
+            scores = (s_ref[g, :, at] + bias_ref[...]).reshape(PATCH, GROUP, rows)
+            expo = jnp.exp(scores - jnp.max(scores, axis=0, keepdims=True))
+            total = jnp.sum(expo, axis=0, keepdims=True)
+            probs = expo * (own_ref[...] / total)
+            d_probs = dp_ref[g, :, at].reshape(PATCH, GROUP, rows)
+            d_scores = probs * (d_probs - jnp.sum(probs * d_probs, axis=0, keepdims=True))
+            p_ref[g, :, at] = probs.astype(BF16).reshape(rows, rows)
+            ds_ref[g, :, at] = d_scores.astype(BF16).reshape(rows, rows)
+    for g in range(groups):
+        k = block(k_ref, g)
+        probs, d_scores = p_ref[g], ds_ref[g]
+        context = dot(block(v_ref, g).T, probs).astype(BF16)
         at = slice(g * rows, (g + 1) * rows)
         context_ref[:HEAD, at] = context[:HEAD, :rows]
         context_ref[HEAD:, at] = context[HEAD:, rows:]
-        d_query = dot(d_scores, k * jnp.asarray(scale, BF16), TN)
+        d_query = dot(d_scores, k * scale, TN)
         d_query = jnp.where(low, d_query[:rows], d_query[rows:])
-        for n, grad in enumerate((d_query, dot(d_scores, q2), dot(probs, d2))):
+        d_key = dot(d_scores, stack(block(q_ref, g) * scale))
+        d_value = dot(probs, stack(block(d_ref, g)))
+        for n, grad in enumerate((d_query, d_key, d_value)):
             d_qkv_ref[n, g] = grad.astype(BF16).reshape(PATCH, GROUP, PAIR)
 
 
@@ -241,8 +261,16 @@
             jax.ShapeDtypeStruct((count * PAIR, tokens), BF16),
             jax.ShapeDtypeStruct((3, groups, PATCH, GROUP, count * PAIR), BF16),
         ],
-        scratch_shapes=[pltpu.VMEM((PATCH * GROUP, 2 * PATCH * GROUP), F32)],
+        scratch_shapes=[
+            pltpu.VMEM((PATCH * GROUP, PATCH * GROUP), F32),
+            pltpu.VMEM((GROUP, PATCH * GROUP), F32),
+            pltpu.VMEM((groups, PATCH * GROUP, 2 * PATCH * GROUP), F32),
+            pltpu.VMEM((groups, PATCH * GROUP, 2 * PATCH * GROUP), F32),
+            pltpu.VMEM((groups, PATCH * GROUP, 2 * PATCH * GROUP), BF16),
+            pltpu.VMEM((groups, PATCH * GROUP, 2 * PATCH * GROUP), BF16),
+        ],
         cost_estimate=cost(count * groups * 6 * 2 * 256 * 256 * 128, count * 1.6e6),
+        compiler_params=pltpu.CompilerParams(vmem_limit_bytes=11 << 20),
         name="attention",
     )(qkv, qkv, qkv, d_context, *after)
 
@@ -340,7 +368,9 @@
     per = cols // block
     height = rows // devices
     steps = planes * per + (2 if extra else 0)
-    whole = lambda a: pl.BlockSpec(a.shape, lambda n, s: (0,) * a.ndim)
+    whole = lambda a: pl.BlockSpec(
+        a.shape, lambda n, s: (0,) * a.ndim, pipeline_mode=pl.Buffered(1)
+    )
     if stacked:
         rhs_spec = pl.BlockSpec(
             (1,) + rhs.shape[1:4] + (block,), lambda n, s: (n // per, 0, 0, 0, n % per)
@@ -381,6 +411,7 @@
         ),
         out_shape=[out] * (2 * len(kinds)),
         cost_estimate=cost(2 * tokens * rows * steps * block, 2 * rows * steps * block + 4e6),
+        compiler_params=pltpu.CompilerParams(vmem_limit_bytes=13 << 20),
         name="grad_rows",
     )(place, *lhs, rhs, *extra, *after)
     return [(got[n], got[n + 1]) for n in range(0, len(got), 2)]
@@ -410,20 +441,27 @@
     @pl.when(step == pl.num_programs(0) - 1)
     def _():
         grad_gain_ref[...] = jnp.zeros_like(grad_gain_ref)
+        tiles = [slice(c, c + 128) for c in range(0, width, 128)]
 
         @pl.loop(0, groups)
         def _(g):
-          for p in range(PATCH):
-            n = g * PATCH + p
-            d_act = acc_ref[pl.ds(pl.multiple_of(n * GROUP, GROUP), GROUP), :]
-            normed = normed_ref[g, p]
-            inv = inv_ref[g, p][:, :1]
-            part = d_act * normed
-            grad_gain_ref[...] += part[:8] + part[8:]
-            d_normed = d_act * gain_ref[...]
-            mean = jnp.mean(part * gain_ref[...], axis=1, keepdims=True)
-            d_x = out_grad_ref[g, p].astype(F32) + inv * (d_normed - normed * mean)
-            d_x_ref[g, p] = d_x.astype(BF16)
+            at = [pl.multiple_of((g * PATCH + p) * GROUP, GROUP) for p in range(PATCH)]
+            sums = [jnp.zeros((GROUP, 128), F32) for _ in range(PATCH)]
+            for tile in tiles:
+                total = jnp.zeros((GROUP, 128), F32)
+                for p in range(PATCH):
+                    part = acc_ref[pl.ds(at[p], GROUP), tile] * normed_ref[g, p, :, tile]
+                    total = total + part
+                    sums[p] = sums[p] + part * gain_ref[:, tile]
+                grad_gain_ref[:, tile] += total[:8] + total[8:]
+            for p in range(PATCH):
+                mean = jnp.sum(sums[p], axis=1, keepdims=True) * (1.0 / width)
+                inv = inv_ref[g, p]
+                for tile in tiles:
+                    d_normed = acc_ref[pl.ds(at[p], GROUP), tile] * gain_ref[:, tile]
+                    d_x = inv * (d_normed - normed_ref[g, p, :, tile] * mean)
+                    d_x = out_grad_ref[g, p, :, tile].astype(F32) + d_x
+                    d_x_ref[g, p, :, tile] = d_x.astype(BF16)
 
 
 def input_grad(d_qkvs, w_qkv, normed, inv, gain, out_grad, after=()):
@@ -438,7 +476,9 @@
             pl.BlockSpec((width, c), lambda n, c=c, at=at: (0, n * (width // c) + at // c))
         )
         at += c
-    whole = lambda a: pl.BlockSpec(a.shape, lambda n: (0,) * a.ndim)
+    whole = lambda a: pl.BlockSpec(
+        a.shape, lambda n: (0,) * a.ndim, pipeline_mode=pl.Buffered(1)
+    )
     return pl.pallas_call(
         functools.partial(input_grad_kernel, chunks=chunks),
         grid=(3,),
@@ -456,6 +496,7 @@
         ],
         scratch_shapes=[pltpu.VMEM((tokens, width), F32)],
         cost_estimate=cost(2 * tokens * width * 3 * width, 20e6),
+        compiler_params=pltpu.CompilerParams(vmem_limit_bytes=20 << 20),
         name="input_grad",
     )(*d_qkvs, *([w_qkv] * chunks), normed, inv, gain, out_grad, *after)
 
@@ -479,7 +520,9 @@
 def back(place, d_x, w_proj, tp, after=()):
     groups, _, _, width = d_x.shape
     half = groups * GROUP
-    whole = lambda a: pl.BlockSpec(a.shape, lambda n, s: (0,) * a.ndim)
+    whole = lambda a: pl.BlockSpec(
+        a.shape, lambda n, s: (0,) * a.ndim, pipeline_mode=pl.Buffered(1)
+    )
     out = jax.ShapeDtypeStruct((half, 2 * width), BF16)
     return pl.pallas_call(
         functools.partial(back_kernel, count=tp),
@@ -493,6 +536,7 @@
         ),
         out_shape=[out] * tp,
         cost_estimate=cost(2 * PATCH * half * width * width, 6e6),
+        compiler_params=pltpu.CompilerParams(vmem_limit_bytes=11 << 20),
         name="back",
     )(place, d_x, w_proj, *after)
 
@@ -524,10 +568,9 @@
     core, wide = tp_bits[:1], tp_bits[1:]
     xy = [core, wide] + [[bit] for bit in seq_bits]
     yx = [core, seq_bits[:1], wide] + [[bit] for bit in seq_bits[1:]]
-    place = jnp.stack(
-        [t >> 1, t & 1, t, spot_of(me, xy, devices), spot_of(me, yx, devices)]
-    )
-    XY, YX = (3, xy), (4, yx)
+    yzx = [core] + [[bit] for bit in seq_bits] + [wide]
+    place = jnp.stack([t >> 1, t & 1, t] + [spot_of(me, o, devices) for o in (xy, yx, yzx)])
+    XY, YX, YZX = (3, xy), (4, yx), (5, yzx)
 
     arrived = {}
     for k in (2, 3, 1)[: tp - 1]:
@@ -579,11 +622,11 @@
     two = hop(two, second)
 
     height = vocab // devices
-    spot = spot_of((ids // height) ^ me, yx, devices) * height + ids % height
+    spot = spot_of((ids // height) ^ me, yzx, devices) * height + ids % height
     marks = (spot[..., None] == jnp.arange(vocab, dtype=jnp.int32)).astype(BF16)
     fits = height % 8 == 0 and width == 4 * vocab
     extra = (marks, grad_gain) if fits else ()
-    three = grad_rows(place, (XY, YX), [slices], d_x, devices, (), extra)
+    three = grad_rows(place, (XY, YZX), [slices], d_x, devices, (), extra)
 
     rows = back(place, d_x, w_proj, tp, flat(three)[:1])
     glob_grad = jnp.zeros((tp * half, 2 * width), BF16)
@@ -595,25 +638,28 @@
 
     two = hop(two, second[::-1], "merge")
     three = hop(three, (first, first))
-    three = hop(three, second)
-    three = hop(three, second[::-1], "merge")
-    one, two, three = finish(one), finish(two), finish(three)
+    paths = list(zip([b[0] for b in xy[1:]], [b[0] for b in yzx[1:]]))
+    for n, masks in enumerate(paths):
+        last = n + 1 == len(paths)
+        three = hop(three, masks, "last" if last else "split")
+    one, two = finish(one), finish(two)
 
     each = width // devices
     if fits:
-        grad_proj = three[:, :width]
-        marked = three[:, width : width + 256].reshape(4, height, 256)
+        cut = width - three[0].shape[1]
+        grad_proj = jnp.concatenate([three[0], three[1][:, :cut]], axis=1)
+        marked = three[1][:, cut : cut + 256].reshape(4, height, 256)
         grad_embed = marked.transpose(1, 0, 2).reshape(height, width)
-        grad_gain = three[:, width + 256]
+        grad_gain = three[1][:, cut + 256]
     else:
-        grad_proj = three
+        grad_proj = jnp.concatenate(three, axis=1)
         grad_embed = lax.dot_general(
             marks, d_x, (((0, 1, 2), (0, 1, 2)), ((), ())), preferred_element_type=F32
         ).astype(BF16)
-        flips = [first, second[1], second[0]] + rest
+        flips = [b[0] for b in yzx]
         grad_embed = split_scatter(grad_embed, flips, devices)
         blocks = jnp.sum(grad_gain, axis=0).reshape(devices, each)
-        blocks = blocks[jnp.array(scatter_order(yx), dtype=jnp.int32) ^ me]
+        blocks = blocks[jnp.array(scatter_order(yzx), dtype=jnp.int32) ^ me]
         grad_gain = split_scatter(blocks, flips, devices).reshape(-1)
 
     span = count * PAIR

time: 229 us -> 201 us (0.88)
  Pallas kernels: 101 us -> 68.5 us
  waiting for transfers between devices: 70.4 us -> 82.5 us
  local copies, waits for them, and re-layouts: 12.7 us -> 7.97 us
  other arithmetic: 7.4 us -> 4.1 us
    pallas_call x4, Pallas kernels: 32.6 us -> 20.4 us  [grad_rows(): pl.pallas_call(functools.partial(grad_kernel, sources=len(lhs), orders=[(...]
    ppermute x30 -> x32, waiting for transfers between devices: 70.4 us -> 82.5 us  [exchange(): return lax.ppermute(block, AXES, [(d, d ^ mask) for d in range(devices)])]
    pallas_call x2, Pallas kernels: 19.6 us -> 11.4 us  [attention(): pl.pallas_call(attention_kernel, grid=(count,), in_specs=[spec(0), spec(1...]
    pallas_call x1, Pallas kernels: 19.6 us -> 15 us  [input_grad(): pl.pallas_call(functools.partial(input_grad_kernel, chunks=chunks), grid=...]
    pallas_call x2, Pallas kernels: 23.7 us -> 19.2 us  [project(): pl.pallas_call(functools.partial(project_kernel, alias=earlier is not Non...]
    pallas_call x1, Pallas kernels: 5.73 us -> 2.5 us  [back(): pl.pallas_call(functools.partial(back_kernel, count=tp), grid_spec=pltpu....]
    convert_element_type x21 -> x22, other arithmetic: 5.33 us -> 2.87 us  [combine(): (k[part].astype(F32) + g[part].astype(F32)).astype(BF16)]
    ppermute x30 -> x32, starting transfers between devices: 31.2 us -> 31.9 us  [exchange(): return lax.ppermute(block, AXES, [(d, d ^ mask) for d in range(devices)])]
  transfers between devices with their start and end apart: 30 -> 32, of which waited for: 11 -> 17; matrix products, arithmetic and copies ran while one was open for 9% -> 6% of each run, Pallas kernels for 12% -> 9%
where the time goes in v3:
time: 201 us
  waiting for transfers between devices  82.5 us (41%)
  Pallas kernels  68.5 us (34%)
  starting transfers between devices  31.9 us (16%)
  local copies, waits for them, and re-layouts  7.97 us (4%)
  matrix products  4.61 us (2%)
  other arithmetic  4.1 us (2%)
    ppermute x32, waiting for transfers between devices, exchange(): return lax.ppermute(block, AXES, [(d, d ^ mask) for d in range(devices)])  82.5 us
    ppermute x32, starting transfers between devices, exchange(): return lax.ppermute(block, AXES, [(d, d ^ mask) for d in range(devices)])  31.9 us
    pallas_call x4, Pallas kernels, grad_rows(): pl.pallas_call(functools.partial(grad_kernel, sources=len(lhs), orders=[(...  20.4 us
    pallas_call x2, Pallas kernels, project(): pl.pallas_call(functools.partial(project_kernel, alias=earlier is not Non...  19.2 us
    pallas_call x1, Pallas kernels, input_grad(): pl.pallas_call(functools.partial(input_grad_kernel, chunks=chunks), grid=...  15 us
    pallas_call x2, Pallas kernels, attention(): pl.pallas_call(attention_kernel, grid=(count,), in_specs=[spec(0), spec(1...  11.4 us
    dot_general x1, matrix products, on_device(): lax.dot_general(grads, w_out, (((3,), (1,)), ((), ())), preferred_element...  4.61 us
  transfers between devices with their start and end apart: 32, of which 17 were waited for; matrix products, arithmetic and copies ran while one was open for 6% of the time, Pallas kernels for 9%

profile of v3, /device:TPU:0, one launch (start us, length us, event | category | flops | bytes accessed | tf_op | source)
XLA Modules:
  0.0 200.9 jit_solution(9447615460295835538)
XLA Ops:
  3.6 2.5 %collective-permute-start = (bf16[96,2048]{1,0:T(8,128)(2,1)}, bf16[96,2048]{1,0:T(8,128)(2,1)S(1)}, u32[]{:S(2)}, u32[]{:S(2)}) collective-permute-start(bf16[96,2048]{1,0:T(8,128)(2,1)} %get-tuple-element.86), channel_id=1, source_target_pairs={{0,2},{1,3},{2,0},{3,1},{4,6},{5,7},{6,4},{7,5},{8,10},{9,11},{10,... | collective-permute-start | bytes 1179656 | tf_op jit(solution)/shard_map/ppermute | solution.py:55
  6.3 4.6 %fusion.2.d_ref = bf16[6,8,16,1024]{3,2,1,0:T(8,128)(2,1)} fusion(bf16[1024,1024]{1,0:T(8,128)(2,1)S(1)} %copy-done, bf16[6,16,8,1024]{3,2,1,0:T(8,128)(2,1)} %bitcast.35), kind=kOutput, calls=%fused_computation.2 | convolution fusion | flops 1611399168 | bytes 5242880 | tf_op jit(solution)/shard_map/dot_general | solution.py:583
  13.8 9.8 %project.2 = (bf16[6,8,16,1024]{3,2,1,0:T(8,128)(2,1)S(1)}, f32[6,8,16,1024]{3,2,1,0:T(8,128)S(1)}, f32[6,8,16,128]{3,2,1,0:T(8,128)S(1)}, bf16[6,8,16,1024]{3,2...) custom-call(s32[6]{0:T(128)S(1)} %stack.27.place, bf16[384,2048]{1,0:T(8,128)(2,1)} %a_ref.1, ...), custom_call_target="tpu_custom_call" | custom-call | flops 3422552064 | bytes 16000000 | tf_op jit(solution)/shard_map/project/pallas_call | solution.py:177
  24.4 9.4 %project.3 = (bf16[6,8,16,1024]{3,2,1,0:T(8,128)(2,1)S(1)}, f32[6,8,16,1024]{3,2,1,0:T(8,128)S(1)}, f32[6,8,16,128]{3,2,1,0:T(8,128)S(1)}, bf16[6,8,16,1024]{3,2...) custom-call(s32[6]{0:T(128)S(1)} %stack.27.place, ...), custom_call_target="tpu_custom_call", output_to_operand_aliasing={{0}: (8, {}), {1}: (9, {}), {2}: (10, {}), {3}: (11, {}), {... | custom-call | flops 3422552064 | bytes 16000000 | tf_op jit(solution)/shard_map/project/pallas_call | solution.py:177
  33.9 5.7 %attention.2 = (bf16[512,768]{1,0:T(8,128)(2,1)S(1)}, bf16[3,6,8,16,512]{4,3,2,1,0:T(8,128)(2,1)S(1)}) custom-call(bf16[6,8,16,3072]{3,2,1,0:T(8,128)(2,1)S(1)} %get-tuple-element.43.q_ref.k_ref.v_ref, bf16[6,8,16,3072]{3,2,1,0:T(8,128)(2,1)S(1)} %get-tuple-element.43.q_ref.k_ref.v_ref, bf16[6,8,16,3072]{3,2,1,0:T(8,128)(2,1)S(1)} %get-tuple-element.43.q_ref.k_ref.v_ref, ...), custom_call_target="tpu_custom_call" | custom-call | flops 2415919104 | bytes 6400000 | tf_op jit(solution)/shard_map/attention/pallas_call | solution.py:251
  39.6 5.4 %grad_rows.4 = (bf16[512,768]{1,0:T(8,128)(2,1)S(1)}, bf16[512,768]{1,0:T(8,128)(2,1)S(1)}, bf16[512,768]{1,0:T(8,128)(2,1)S(1)}, bf16[512,768]{1,0:T(8,128)(2,1)S(1)}) custom-call(s32[6]{0:T(128)S(1)} %stack.27.place, bf16[6,8,16,1024]{3,2,1,0:T(8,128)(2,1)S(1)} %get-tuple-element.45.refs_0_, bf16[3,6,8,16,512]{4,3,2,1,0:T(8,128)(2,1)S(1)} %get-tuple-element.44.refs_1_.refs_0_), custom_call_target="tpu_custom_call" | custom-call | flops 2415919104 | bytes 7145728 | tf_op jit(solution)/shard_map/grad_rows/pallas_call | solution.py:394
  45.0 5.7 %attention.3 = (bf16[512,768]{1,0:T(8,128)(2,1)S(1)}, bf16[3,6,8,16,512]{4,3,2,1,0:T(8,128)(2,1)S(1)}) custom-call(bf16[6,8,16,3072]{3,2,1,0:T(8,128)(2,1)S(1)} %get-tuple-element.43.q_ref.k_ref.v_ref, bf16[6,8,16,3072]{3,2,1,0:T(8,128)(2,1)S(1)} %get-tuple-element.43.q_ref.k_ref.v_ref, bf16[6,8,16,3072]{3,2,1,0:T(8,128)(2,1)S(1)} %get-tuple-element.43.q_ref.k_ref.v_ref, ...), custom_call_target="tpu_custom_call" | custom-call | flops 2415919104 | bytes 6400000 | tf_op jit(solution)/shard_map/attention/pallas_call | solution.py:251
  50.8 15.0 %input_grad.1 = (bf16[6,8,16,1024]{3,2,1,0:T(8,128)(2,1)S(1)}, f32[8,1024]{1,0:T(8,128)S(1)}) custom-call(bf16[3,6,8,16,512]{4,3,2,1,0:T(8,128)(2,1)S(1)} %get-tuple-element.44.refs_1_.refs_0_, bf16[3,6,8,16,512]{4,3,2,1,0:T(8,128)(2,1)S(1)} %get-tuple-element.47.refs_1_, bf16[1024,3072]{1,0:T(8,128)(2,1)S(1)} %bitcast.29, bf16[1024,3072]{1,0:T(8,128)(2,1)S(1)} %bitcast.29, ...), custom_call_target="tpu_custom_call" | custom-call | flops 4831838208 | bytes 20000000 | tf_op jit(solution)/shard_map/input_grad/pallas_call | solution.py:482
  65.8 6.3 %grad_rows.5 = (bf16[512,768]{1,0:T(8,128)(2,1)S(1)}, bf16[512,768]{1,0:T(8,128)(2,1)S(1)}, bf16[512,768]{1,0:T(8,128)(2,1)S(1)}, bf16[512,768]{1,0:T(8,128)(2,1)S(1)}) custom-call(s32[6]{0:T(128)S(1)} %stack.27.place, bf16[6,8,16,1024]{3,2,1,0:T(8,128)(2,1)S(1)} %get-tuple-element.51.refs_0_, ...), custom_call_target="tpu_custom_call" | custom-call | flops 2415919104 | bytes 7145728 | tf_op jit(solution)/shard_map/grad_rows/pallas_call | solution.py:394
  72.1 2.5 %back.1 = (bf16[96,2048]{1,0:T(8,128)(2,1)S(1)}, bf16[96,2048]{1,0:T(8,128)(2,1)S(1)}, bf16[96,2048]{1,0:T(8,128)(2,1)S(1)}, bf16[96,2048]{1,0:T(8,128)(2,1)S(1)}) custom-call(s32[6]{0:T(128)S(1)} %stack.27.place, bf16[6,8,16,1024]{3,2,1,0:T(8,128)(2,1)S(1)} %get-tuple-element.50.refs_1_.d_x_ref, bf16[1024,1024]{1,0:T(8,128)(2,1)S(1)} %copy-done.3, ...), custom_call_target="tpu_custom_call" | custom-call | flops 1610612736 | bytes 6000000 | tf_op jit(solution)/shard_map/back/pallas_call | solution.py:527
  74.8 5.2 %grad_rows.6 = (bf16[512,1536]{1,0:T(8,128)(2,1)S(1)}, bf16[512,1536]{1,0:T(8,128)(2,1)S(1)}) custom-call(s32[6]{0:T(128)S(1)} %stack.27.place, bf16[6,8,16,1024]{3,2,1,0:T(8,128)(2,1)S(1)} %get-tuple-element.45.refs_0_, bf16[3,6,8,16,512]{4,3,2,1,0:T(8,128)(2,1)S(1)} %get-tuple-element.47.refs_1_), custom_call_target="tpu_custom_call" | custom-call | flops 2415919104 | bytes 7145728 | tf_op jit(solution)/shard_map/grad_rows/pallas_call | solution.py:394
  82.6 3.6 %grad_rows.7 = (bf16[512,1024]{1,0:T(8,128)(2,1)S(1)}, bf16[512,1024]{1,0:T(8,128)(2,1)S(1)}) custom-call(s32[6]{0:T(128)S(1)} %stack.27.place, bf16[512,768]{1,0:T(8,128)(2,1)S(1)} %get-tuple-element.66.refs_0_, bf16[512,768]{1,0:T(8,128)(2,1)S(1)} %get-tuple-element.67.refs_1_, bf16[6,8,16,1024]{3,2,1,0:T(8,128)(2,1)S(1)} %bitcast.31, ...), custom_call_target="tpu_custom_call" | custom-call | flops 1610612736 | bytes 6097152 | tf_op jit(solution)/shard_map/grad_rows/pallas_call | solution.py:394
  86.3 6.6 %collective-permute-done.4 = bf16[96,2048]{1,0:T(8,128)(2,1)S(1)} collective-permute-done((bf16[96,2048]{1,0:T(8,128)(2,1)S(1)}, bf16[96,2048]{1,0:T(8,128)(2,1)S(1)}, u32[]{:S(2)}, u32[]{:S(2)}) %collective-permute-start.4) | collective-permute-done | bytes 393248 | tf_op jit(solution)/shard_map/ppermute | solution.py:55
  92.9 6.7 %collective-permute-done.5 = bf16[96,2048]{1,0:T(8,128)(2,1)S(1)} collective-permute-done((bf16[96,2048]{1,0:T(8,128)(2,1)S(1)}, bf16[96,2048]{1,0:T(8,128)(2,1)S(1)}, u32[]{:S(2)}, u32[]{:S(2)}) %collective-permute-start.5) | collective-permute-done | bytes 393248 | tf_op jit(solution)/shard_map/ppermute | solution.py:55
  107.5 5.2 %collective-permute-done.17 = bf16[256,768]{1,0:T(8,128)(2,1)S(1)} collective-permute-done((bf16[256,768]{1,0:T(8,128)(2,1)S(1)}, bf16[256,768]{1,0:T(8,128)(2,1)S(1)}, u32[]{:S(2)}, u32[]{:S(2)}) %collective-permute-start.17) | collective-permute-done | bytes 393248 | tf_op jit(solution)/shard_map/ppermute | solution.py:55
  116.2 4.4 %collective-permute-done.12 = bf16[256,768]{1,0:T(8,128)(2,1)S(1)} collective-permute-done((bf16[256,768]{1,0:T(8,128)(2,1)S(1)}, bf16[256,768]{1,0:T(8,128)(2,1)S(1)}, u32[]{:S(2)}, u32[]{:S(2)}) %collective-permute-start.12) | collective-permute-done | bytes 393248 | tf_op jit(solution)/shard_map/ppermute | solution.py:55
  124.7 13.8 %collective-permute-done.18 = bf16[128,768]{1,0:T(8,128)(2,1)S(1)} collective-permute-done((bf16[128,768]{1,0:T(8,128)(2,1)S(1)}, bf16[128,768]{1,0:T(8,128)(2,1)S(1)}, u32[]{:S(2)}, u32[]{:S(2)}) %collective-permute-start.18) | collective-permute-done | bytes 196640 | tf_op jit(solution)/shard_map/ppermute | solution.py:55
  140.7 6.3 %collective-permute-done.8 = bf16[128,768]{1,0:T(8,128)(2,1)S(1)} collective-permute-done((bf16[128,768]{1,0:T(8,128)(2,1)S(1)}, bf16[128,768]{1,0:T(8,128)(2,1)S(1)}, u32[]{:S(2)}, u32[]{:S(2)}) %collective-permute-start.8) | collective-permute-done | bytes 196640 | tf_op jit(solution)/shard_map/ppermute | solution.py:55
  151.4 2.6 %collective-permute-done.9 = bf16[64,768]{1,0:T(8,128)(2,1)S(1)} collective-permute-done((bf16[64,768]{1,0:T(8,128)(2,1)S(1)}, bf16[64,768]{1,0:T(8,128)(2,1)S(1)}, u32[]{:S(2)}, u32[]{:S(2)}) %collective-permute-start.9) | collective-permute-done | bytes 98336 | tf_op jit(solution)/shard_map/ppermute | solution.py:55
  155.2 3.5 %collective-permute-done.10 = bf16[32,768]{1,0:T(8,128)(2,1)S(1)} collective-permute-done((bf16[32,768]{1,0:T(8,128)(2,1)S(1)}, bf16[32,768]{1,0:T(8,128)(2,1)S(1)}, u32[]{:S(2)}, u32[]{:S(2)}) %collective-permute-start.10) | collective-permute-done | bytes 49184 | tf_op jit(solution)/shard_map/ppermute | solution.py:55
  163.4 12.3 %collective-permute-done.25 = bf16[256,1536]{1,0:T(8,128)(2,1)S(1)} collective-permute-done((bf16[256,1536]{1,0:T(8,128)(2,1)S(1)}, bf16[256,1536]{1,0:T(8,128)(2,1)S(1)}, u32[]{:S(2)}, u32[]{:S(2)}) %collective-permute-start.25) | collective-permute-done | bytes 786464 | tf_op jit(solution)/shard_map/ppermute | solution.py:55
  178.6 5.2 %collective-permute-done.26 = bf16[128,1536]{1,0:T(8,128)(2,1)S(1)} collective-permute-done((bf16[128,1536]{1,0:T(8,128)(2,1)S(1)}, bf16[128,1536]{1,0:T(8,128)(2,1)S(1)}, u32[]{:S(2)}, u32[]{:S(2)}) %collective-permute-start.26) | collective-permute-done | bytes 393248 | tf_op jit(solution)/shard_map/ppermute | solution.py:55
  185.2 6.1 %collective-permute-done.30 = bf16[64,2560]{1,0:T(8,128)(2,1)S(1)} collective-permute-done((bf16[64,2560]{1,0:T(8,128)(2,1)S(1)}, bf16[64,2560]{1,0:T(8,128)(2,1)S(1)}, u32[]{:S(2)}, u32[]{:S(2)}) %collective-permute-start.30) | collective-permute-done | bytes 327712 | tf_op jit(solution)/shard_map/ppermute | solution.py:55
  192.0 7.4 %collective-permute-done.31 = bf16[32,2560]{1,0:T(8,128)(2,1)S(1)} collective-permute-done((bf16[32,2560]{1,0:T(8,128)(2,1)S(1)}, bf16[32,2560]{1,0:T(8,128)(2,1)S(1)}, u32[]{:S(2)}, u32[]{:S(2)}) %collective-permute-start.31) | collective-permute-done | bytes 163872 | tf_op jit(solution)/shard_map/ppermute | solution.py:55
  (126 shorter events, 43.9 us)
Async XLA Ops:
  3.1 10.7 %collective-permute-start.2 = (bf16[96,2048]{1,0:T(8,128)(2,1)}, bf16[96,2048]{1,0:T(8,128)(2,1)}, u32[]{:S(2)}, u32[]{:S(2)}) collective-permute-start(bf16[96,2048]{1,0:T(8,128)(2,1)} %get-tuple-element.84), channel_id=1, source_target_pairs={{0,1},{1,0},{2,3},{3,2},{4,5},{5,4},{6,7},{7,6},{8,9},{9,8},{10,11... | collective-permute-start | bytes 1179656 | tf_op jit(solution)/shard_map/ppermute | solution.py:55
  3.6 20.0 %collective-permute-start = (bf16[96,2048]{1,0:T(8,128)(2,1)}, bf16[96,2048]{1,0:T(8,128)(2,1)S(1)}, u32[]{:S(2)}, u32[]{:S(2)}) collective-permute-start(bf16[96,2048]{1,0:T(8,128)(2,1)} %get-tuple-element.86), channel_id=1, source_target_pairs={{0,2},{1,3},{2,0},{3,1},{4,6},{5,7},{6,4},{7,5},{8,10},{9,11},{10,... | collective-permute-start | bytes 1179656 | tf_op jit(solution)/shard_map/ppermute | solution.py:55
  6.1 18.3 %collective-permute-start.1 = (bf16[96,2048]{1,0:T(8,128)(2,1)}, bf16[96,2048]{1,0:T(8,128)(2,1)}, u32[]{:S(2)}, u32[]{:S(2)}) collective-permute-start(bf16[96,2048]{1,0:T(8,128)(2,1)} %get-tuple-element.85), channel_id=1, source_target_pairs={{0,3},{1,2},{2,1},{3,0},{4,7},{5,6},{6,5},{7,4},{8,11},{9,10},{10,... | collective-permute-start | bytes 1179656 | tf_op jit(solution)/shard_map/ppermute | solution.py:55
  74.6 11.6 %collective-permute-start.3 = (bf16[96,2048]{1,0:T(8,128)(2,1)S(1)}, bf16[96,2048]{1,0:T(8,128)(2,1)S(1)}, u32[]{:S(2)}, u32[]{:S(2)}) collective-permute-start(bf16[96,2048]{1,0:T(8,128)(2,1)S(1)} %get-tuple-element.55), channel_id=1, source_target_pairs={{0,1},{1,0},{2,3},{3,2},{4,5},{5,4},{6,7},{7,6},{8,9},{9,8},{10,11... | collective-permute-start | bytes 1179656 | tf_op jit(solution)/shard_map/ppermute | solution.py:55
  79.9 78.8 %collective-permute-start.24 = (bf16[512,1536]{1,0:T(8,128)(2,1)S(1)}, bf16[512,1536]{1,0:T(8,128)(2,1)S(1)}, u32[]{:S(2)}, u32[]{:S(2)}) collective-permute-start(bf16[512,1536]{1,0:T(8,128)(2,1)S(1)} %get-tuple-element.65), channel_id=1, source_target_pairs={{0,1},{1,0},{2,3},{3,2},{4,5},{5,4},{6,7},{7,6},{8,9},{9,8},{10,11... | collective-permute-start | bytes 4718600 | tf_op jit(solution)/shard_map/ppermute | solution.py:55
  80.4 19.9 %collective-permute-start.16 = (bf16[512,768]{1,0:T(8,128)(2,1)S(1)}, bf16[512,768]{1,0:T(8,128)(2,1)S(1)}, u32[]{:S(2)}, u32[]{:S(2)}) collective-permute-start(bf16[512,768]{1,0:T(8,128)(2,1)S(1)} %get-tuple-element.61), channel_id=1, source_target_pairs={{0,1},{1,0},{2,3},{3,2},{4,5},{5,4},{6,7},{7,6},{8,9},{9,8},{10,11... | collective-permute-start | bytes 2359304 | tf_op jit(solution)/shard_map/ppermute | solution.py:55
  80.5 20.1 %collective-permute-start.19 = (bf16[512,768]{1,0:T(8,128)(2,1)S(1)}, bf16[512,768]{1,0:T(8,128)(2,1)S(1)}, u32[]{:S(2)}, u32[]{:S(2)}) collective-permute-start(bf16[512,768]{1,0:T(8,128)(2,1)S(1)} %get-tuple-element.63), channel_id=1, source_target_pairs={{0,1},{1,0},{2,3},{3,2},{4,5},{5,4},{6,7},{7,6},{8,9},{9,8},{10,11... | collective-permute-start | bytes 2359304 | tf_op jit(solution)/shard_map/ppermute | solution.py:55
  80.9 12.0 %collective-permute-start.4 = (bf16[96,2048]{1,0:T(8,128)(2,1)S(1)}, bf16[96,2048]{1,0:T(8,128)(2,1)S(1)}, u32[]{:S(2)}, u32[]{:S(2)}) collective-permute-start(bf16[96,2048]{1,0:T(8,128)(2,1)S(1)} %get-tuple-element.56), channel_id=1, source_target_pairs={{0,2},{1,3},{2,0},{3,1},{4,6},{5,7},{6,4},{7,5},{8,10},{9,11},{10,... | collective-permute-start | bytes 1179656 | tf_op jit(solution)/shard_map/ppermute | solution.py:55
  86.2 13.5 %collective-permute-start.5 = (bf16[96,2048]{1,0:T(8,128)(2,1)S(1)}, bf16[96,2048]{1,0:T(8,128)(2,1)S(1)}, u32[]{:S(2)}, u32[]{:S(2)}) collective-permute-start(bf16[96,2048]{1,0:T(8,128)(2,1)S(1)} %get-tuple-element.57), channel_id=1, source_target_pairs={{0,3},{1,2},{2,1},{3,0},{4,7},{5,6},{6,5},{7,4},{8,11},{9,10},{10,... | collective-permute-start | bytes 1179656 | tf_op jit(solution)/shard_map/ppermute | solution.py:55
  92.9 9.7 %collective-permute-start.11 = (bf16[512,768]{1,0:T(8,128)(2,1)S(1)}, bf16[512,768]{1,0:T(8,128)(2,1)S(1)}, u32[]{:S(2)}, u32[]{:S(2)}) collective-permute-start(bf16[512,768]{1,0:T(8,128)(2,1)S(1)} %get-tuple-element.60), channel_id=1, source_target_pairs={{0,1},{1,0},{2,3},{3,2},{4,5},{5,4},{6,7},{7,6},{8,9},{9,8},{10,11... | collective-permute-start | bytes 2359304 | tf_op jit(solution)/shard_map/ppermute | solution.py:55
  100.7 12.1 %collective-permute-start.17 = (bf16[256,768]{1,0:T(8,128)(2,1)S(1)}, bf16[256,768]{1,0:T(8,128)(2,1)S(1)}, u32[]{:S(2)}, u32[]{:S(2)}) collective-permute-start(bf16[256,768]{1,0:T(8,128)(2,1)S(1)} %get-tuple-element.77), channel_id=1, source_target_pairs={{0,2},{1,3},{2,0},{3,1},{4,6},{5,7},{6,4},{7,5},{8,10},{9,11},{10,... | collective-permute-start | bytes 1179656 | tf_op jit(solution)/shard_map/ppermute | solution.py:55
  102.6 12.1 %collective-permute-start.20 = (bf16[256,768]{1,0:T(8,128)(2,1)S(1)}, bf16[256,768]{1,0:T(8,128)(2,1)S(1)}, u32[]{:S(2)}, u32[]{:S(2)}) collective-permute-start(bf16[256,768]{1,0:T(8,128)(2,1)S(1)} %get-tuple-element.79), channel_id=1, source_target_pairs={{0,4},{1,5},{2,6},{3,7},{4,0},{5,1},{6,2},{7,3},{8,12},{9,13},{10,... | collective-permute-start | bytes 1179656 | tf_op jit(solution)/shard_map/ppermute | solution.py:55
  104.4 16.3 %collective-permute-start.12 = (bf16[256,768]{1,0:T(8,128)(2,1)S(1)}, bf16[256,768]{1,0:T(8,128)(2,1)S(1)}, u32[]{:S(2)}, u32[]{:S(2)}) collective-permute-start(bf16[256,768]{1,0:T(8,128)(2,1)S(1)} %get-tuple-element.81), channel_id=1, source_target_pairs={{0,2},{1,3},{2,0},{3,1},{4,6},{5,7},{6,4},{7,5},{8,10},{9,11},{10,... | collective-permute-start | bytes 1179656 | tf_op jit(solution)/shard_map/ppermute | solution.py:55
  105.5 17.5 %collective-permute-start.7 = (bf16[256,768]{1,0:T(8,128)(2,1)S(1)}, bf16[256,768]{1,0:T(8,128)(2,1)S(1)}, u32[]{:S(2)}, u32[]{:S(2)}) collective-permute-start(bf16[256,768]{1,0:T(8,128)(2,1)S(1)} %get-tuple-element.83), channel_id=1, source_target_pairs={{0,4},{1,5},{2,6},{3,7},{4,0},{5,1},{6,2},{7,3},{8,12},{9,13},{10,... | collective-permute-start | bytes 1179656 | tf_op jit(solution)/shard_map/ppermute | solution.py:55
  112.7 48.7 %collective-permute-start.28 = (bf16[256,1024]{1,0:T(8,128)(2,1)S(1)}, bf16[256,1024]{1,0:T(8,128)(2,1)S(1)}, u32[]{:S(2)}, u32[]{:S(2)}) collective-permute-start(bf16[256,1024]{1,0:T(8,128)(2,1)S(1)} %get-tuple-element.73), channel_id=1, source_target_pairs={{0,4},{1,5},{2,6},{3,7},{4,0},{5,1},{6,2},{7,3},{8,12},{9,13},{10,... | collective-permute-start | bytes 1572872 | tf_op jit(solution)/shard_map/ppermute | solution.py:55
  114.6 23.9 %collective-permute-start.18 = (bf16[128,768]{1,0:T(8,128)(2,1)S(1)}, bf16[128,768]{1,0:T(8,128)(2,1)S(1)}, u32[]{:S(2)}, u32[]{:S(2)}) collective-permute-start(bf16[128,768]{1,0:T(8,128)(2,1)S(1)} %get-tuple-element.92), channel_id=1, source_target_pairs={{0,4},{1,5},{2,6},{3,7},{4,0},{5,1},{6,2},{7,3},{8,12},{9,13},{10,... | collective-permute-start | bytes 589832 | tf_op jit(solution)/shard_map/ppermute | solution.py:55
  120.7 19.5 %collective-permute-start.21 = (bf16[128,768]{1,0:T(8,128)(2,1)S(1)}, bf16[128,768]{1,0:T(8,128)(2,1)S(1)}, u32[]{:S(2)}, u32[]{:S(2)}) collective-permute-start(bf16[128,768]{1,0:T(8,128)(2,1)S(1)} %get-tuple-element.94), channel_id=1, source_target_pairs={{0,2},{1,3},{2,0},{3,1},{4,6},{5,7},{6,4},{7,5},{8,10},{9,11},{10,... | collective-permute-start | bytes 589832 | tf_op jit(solution)/shard_map/ppermute | solution.py:55
  123.1 25.9 %collective-permute-start.13 = (bf16[128,768]{1,0:T(8,128)(2,1)S(1)}, bf16[128,768]{1,0:T(8,128)(2,1)S(1)}, u32[]{:S(2)}, u32[]{:S(2)}) collective-permute-start(bf16[128,768]{1,0:T(8,128)(2,1)S(1)} %get-tuple-element.96), channel_id=1, source_target_pairs={{0,4},{1,5},{2,6},{3,7},{4,0},{5,1},{6,2},{7,3},{8,12},{9,13},{10,... | collective-permute-start | bytes 589832 | tf_op jit(solution)/shard_map/ppermute | solution.py:55
  138.5 8.6 %collective-permute-start.8 = (bf16[128,768]{1,0:T(8,128)(2,1)S(1)}, bf16[128,768]{1,0:T(8,128)(2,1)S(1)}, u32[]{:S(2)}, u32[]{:S(2)}) collective-permute-start(bf16[128,768]{1,0:T(8,128)(2,1)S(1)} %get-tuple-element.98), channel_id=1, source_target_pairs={{0,8},{1,9},{2,10},{3,11},{4,12},{5,13},{6,14},{7,15},{8,0},{9,1},... | collective-permute-start | bytes 589832 | tf_op jit(solution)/shard_map/ppermute | solution.py:55
  140.2 37.4 %collective-permute-start.22 = (bf16[64,1536]{1,0:T(8,128)(2,1)S(1)}, bf16[64,1536]{1,0:T(8,128)(2,1)S(1)}, u32[]{:S(2)}, u32[]{:S(2)}) collective-permute-start(bf16[64,1536]{1,0:T(8,128)(2,1)S(1)} %pad_maximum_fusion.1), channel_id=1, source_target_pairs={{0,8},{1,9},{2,10},{3,11},{4,12},{5,13},{6,14},{7,15},{8,0},{9,1},... | collective-permute-start | bytes 589832 | tf_op jit(solution)/shard_map/ppermute | solution.py:55
  159.1 16.6 %collective-permute-start.25 = (bf16[256,1536]{1,0:T(8,128)(2,1)S(1)}, bf16[256,1536]{1,0:T(8,128)(2,1)S(1)}, u32[]{:S(2)}, u32[]{:S(2)}) collective-permute-start(bf16[256,1536]{1,0:T(8,128)(2,1)S(1)} %get-tuple-element.71), channel_id=1, source_target_pairs={{0,2},{1,3},{2,0},{3,1},{4,6},{5,7},{6,4},{7,5},{8,10},{9,11},{10,... | collective-permute-start | bytes 2359304 | tf_op jit(solution)/shard_map/ppermute | solution.py:55
  161.6 17.0 %collective-permute-start.29 = (bf16[128,1024]{1,0:T(8,128)(2,1)S(1)}, bf16[128,1024]{1,0:T(8,128)(2,1)S(1)}, u32[]{:S(2)}, u32[]{:S(2)}) collective-permute-start(bf16[128,1024]{1,0:T(8,128)(2,1)S(1)} %get-tuple-element.88), channel_id=1, source_target_pairs={{0,2},{1,3},{2,0},{3,1},{4,6},{5,7},{6,4},{7,5},{8,10},{9,11},{10,... | collective-permute-start | bytes 786440 | tf_op jit(solution)/shard_map/ppermute | solution.py:55
  176.0 7.8 %collective-permute-start.26 = (bf16[128,1536]{1,0:T(8,128)(2,1)S(1)}, bf16[128,1536]{1,0:T(8,128)(2,1)S(1)}, u32[]{:S(2)}, u32[]{:S(2)}) collective-permute-start(bf16[128,1536]{1,0:T(8,128)(2,1)S(1)} %get-tuple-element.75), channel_id=1, source_target_pairs={{0,4},{1,5},{2,6},{3,7},{4,0},{5,1},{6,2},{7,3},{8,12},{9,13},{10,... | collective-permute-start | bytes 1179656 | tf_op jit(solution)/shard_map/ppermute | solution.py:55
  191.3 8.0 %collective-permute-start.31 = (bf16[32,2560]{1,0:T(8,128)(2,1)S(1)}, bf16[32,2560]{1,0:T(8,128)(2,1)S(1)}, u32[]{:S(2)}, u32[]{:S(2)}) collective-permute-start(bf16[32,2560]{1,0:T(8,128)(2,1)S(1)} %add_convert_fusion.26), channel_id=1, source_target_pairs={{0,16},{1,17},{2,18},{3,19},{4,20},{5,21},{6,22},{7,23},{8,24},{9,... | collective-permute-start | bytes 491528 | tf_op jit(solution)/shard_map/ppermute | solution.py:55
  (19 other events, 111.3 us)

commit v4 on v3

--- a/solution.py
+++ b/solution.py
@@ -28,6 +28,10 @@
     return pl.CostEstimate(
         flops=int(flops), bytes_accessed=int(nbytes), transcendentals=int(transcendentals)
     )
+
+
+def in_hbm(value):
+    return pltpu.with_memory_space_constraint(value, pltpu.HBM)
 
 
 def bit_masks(mesh):
@@ -159,9 +163,8 @@
         pl.BlockSpec((1, width), lambda n, s: (0, 0), pipeline_mode=once),
         pl.BlockSpec((width, block), lambda n, s: (0, n)),
     ]
-    keep = lambda a: pltpu.with_memory_space_constraint(a, pltpu.HBM)
-    first = first if flip else keep(first)
-    args = [place, first, second, onehot, embed, keep(w_proj), gain, keep(w_qkv)]
+    first = first if flip else in_hbm(first)
+    args = [place, first, second, onehot, embed, in_hbm(w_proj), gain, in_hbm(w_qkv)]
     aliases = {}
     if earlier is not None:
         in_specs += [pl.BlockSpec(memory_space=pl.ANY)] * 5
@@ -418,28 +421,30 @@
 
 
 def input_grad_kernel(*refs, chunks):
-    d_refs, w_refs = refs[:chunks], refs[chunks : 2 * chunks]
-    normed_ref, inv_ref, gain_ref, out_grad_ref = refs[2 * chunks : 2 * chunks + 4]
-    d_x_ref, grad_gain_ref, acc_ref = refs[-3:]
+    d_refs, w_ref = refs[:chunks], refs[chunks]
+    far, gain_ref = refs[chunks + 1 : chunks + 4], refs[chunks + 4]
+    d_x_ref, grad_gain_ref, acc_ref, normed_ref, inv_ref, out_grad_ref, sems = refs[-7:]
     step = pl.program_id(0)
+    near = (normed_ref, inv_ref, out_grad_ref)
+    copies = [pltpu.make_async_copy(a, b, sems.at[n]) for n, (a, b) in enumerate(zip(far, near))]
     groups, _, _, width = normed_ref.shape
     rows = groups * PATCH * GROUP
+
+    @pl.when(step == 0)
+    def _():
+        for copy in copies:
+            copy.start()
+        acc_ref[...] = jnp.zeros_like(acc_ref)
+
+    d_qkv = [d_ref[...].reshape(rows, d_ref.shape[-1]) for d_ref in d_refs]
+    d_qkv = jnp.concatenate(d_qkv, axis=1)
     for n in range(0, width, 256):
-        total = None
-        for d_ref, w_ref in zip(d_refs, w_refs):
-            term = dot(d_ref[...].reshape(rows, d_ref.shape[-1]), w_ref[n : n + 256, :], NT)
-            total = term if total is None else total + term
-
-        @pl.when(step == 0)
-        def _():
-            acc_ref[:, n : n + 256] = total
-
-        @pl.when(step > 0)
-        def _():
-            acc_ref[:, n : n + 256] += total
+        acc_ref[:, n : n + 256] += dot(d_qkv, w_ref[n : n + 256, :], NT)
 
     @pl.when(step == pl.num_programs(0) - 1)
     def _():
+        for copy in copies:
+            copy.wait()
         grad_gain_ref[...] = jnp.zeros_like(grad_gain_ref)
         tiles = [slice(c, c + 128) for c in range(0, width, 128)]
 
@@ -468,14 +473,11 @@
     groups, _, _, width = normed.shape
     tokens = groups * PATCH * GROUP
     chunks = len(d_qkvs)
-    cols = [d.shape[-1] for d in d_qkvs]
-    d_specs, w_specs, at = [], [], 0
-    for c in cols:
-        d_specs.append(pl.BlockSpec((1, groups, PATCH, GROUP, c), lambda n: (n, 0, 0, 0, 0)))
-        w_specs.append(
-            pl.BlockSpec((width, c), lambda n, c=c, at=at: (0, n * (width // c) + at // c))
-        )
-        at += c
+    d_specs = [
+        pl.BlockSpec((1, groups, PATCH, GROUP, d.shape[-1]), lambda n: (n, 0, 0, 0, 0))
+        for d in d_qkvs
+    ]
+    w_spec = pl.BlockSpec((width, width), lambda n: (0, n))
     whole = lambda a: pl.BlockSpec(
         a.shape, lambda n: (0,) * a.ndim, pipeline_mode=pl.Buffered(1)
     )
@@ -483,8 +485,9 @@
         functools.partial(input_grad_kernel, chunks=chunks),
         grid=(3,),
         in_specs=d_specs
-        + w_specs
-        + [whole(normed), whole(inv), whole(gain), whole(out_grad)]
+        + [w_spec]
+        + [pl.BlockSpec(memory_space=pl.ANY)] * 3
+        + [whole(gain)]
         + [pl.BlockSpec(memory_space=pl.ANY)] * len(after),
         out_specs=[
             pl.BlockSpec(normed.shape, lambda n: (0, 0, 0, 0)),
@@ -494,11 +497,17 @@
             jax.ShapeDtypeStruct(normed.shape, BF16),
             jax.ShapeDtypeStruct((8, width), F32),
         ],
-        scratch_shapes=[pltpu.VMEM((tokens, width), F32)],
+        scratch_shapes=[
+            pltpu.VMEM((tokens, width), F32),
+            pltpu.VMEM(normed.shape, F32),
+            pltpu.VMEM(inv.shape, F32),
+            pltpu.VMEM(out_grad.shape, BF16),
+            pltpu.SemaphoreType.DMA((3,)),
+        ],
         cost_estimate=cost(2 * tokens * width * 3 * width, 20e6),
         compiler_params=pltpu.CompilerParams(vmem_limit_bytes=20 << 20),
         name="input_grad",
-    )(*d_qkvs, *([w_qkv] * chunks), normed, inv, gain, out_grad, *after)
+    )(*map(in_hbm, d_qkvs), w_qkv, normed, inv, out_grad, gain, *after)
 
 
 def back_kernel(place, d_x_ref, w_ref, *refs, count):

time: 201 us -> 197 us (0.980)
  Pallas kernels: 68.5 us -> 62.6 us
    pallas_call x1, Pallas kernels: 15 us -> 9.07 us  [input_grad(): pl.pallas_call(functools.partial(input_grad_kernel, chunks=chunks), grid=...]
where the time goes in v4:
time: 197 us; the launch traced here: 196 us
  waiting for transfers between devices  82.5 us (42%)
  Pallas kernels  62.6 us (32%)
  starting transfers between devices  31.9 us (16%)
  local copies, waits for them, and re-layouts  9.41 us (5%)
  matrix products  4.61 us (2%)
  other arithmetic  4.06 us (2%)
    ppermute x32, waiting for transfers between devices, exchange(): return lax.ppermute(block, AXES, [(d, d ^ mask) for d in range(devices)])  82.5 us
    ppermute x32, starting transfers between devices, exchange(): return lax.ppermute(block, AXES, [(d, d ^ mask) for d in range(devices)])  31.9 us
    pallas_call x4, Pallas kernels, grad_rows(): pl.pallas_call(functools.partial(grad_kernel, sources=len(lhs), orders=[(...  20.4 us
    pallas_call x2, Pallas kernels, project(): pl.pallas_call(functools.partial(project_kernel, alias=earlier is not Non...  19.2 us
    pallas_call x2, Pallas kernels, attention(): pl.pallas_call(attention_kernel, grid=(count,), in_specs=[spec(0), spec(1...  11.4 us
    pallas_call x1, Pallas kernels, input_grad(): pl.pallas_call(functools.partial(input_grad_kernel, chunks=chunks), grid=...  9.07 us
    dot_general x1, matrix products, on_device(): lax.dot_general(grads, w_out, (((3,), (1,)), ((), ())), preferred_element...  4.61 us
  transfers between devices with their start and end apart: 32, of which 17 were waited for; matrix products, arithmetic and copies ran while one was open for 6% of the time, Pallas kernels for 9%

profile of v4, /device:TPU:0, one launch (start us, length us, event | category | flops | bytes accessed | tf_op | source)
XLA Modules:
  0.0 196.3 jit_solution(17112825079279306634)
XLA Ops:
  3.6 2.5 %collective-permute-start = (bf16[96,2048]{1,0:T(8,128)(2,1)}, bf16[96,2048]{1,0:T(8,128)(2,1)S(1)}, u32[]{:S(2)}, u32[]{:S(2)}) collective-permute-start(bf16[96,2048]{1,0:T(8,128)(2,1)} %get-tuple-element.86), channel_id=1, source_target_pairs={{0,2},{1,3},{2,0},{3,1},{4,6},{5,7},{6,4},{7,5},{8,10},{9,11},{10,... | collective-permute-start | bytes 1179656 | tf_op jit(solution)/shard_map/ppermute | solution.py:59
  6.4 4.6 %fusion.2.d_ref = bf16[6,8,16,1024]{3,2,1,0:T(8,128)(2,1)} fusion(bf16[1024,1024]{1,0:T(8,128)(2,1)S(1)} %copy-done, bf16[6,16,8,1024]{3,2,1,0:T(8,128)(2,1)} %bitcast.35), kind=kOutput, calls=%fused_computation.2 | convolution fusion | flops 1611399168 | bytes 5242880 | tf_op jit(solution)/shard_map/dot_general | solution.py:592
  13.8 9.8 %project.2 = (bf16[6,8,16,1024]{3,2,1,0:T(8,128)(2,1)S(1)}, f32[6,8,16,1024]{3,2,1,0:T(8,128)S(1)}, f32[6,8,16,128]{3,2,1,0:T(8,128)S(1)}, bf16[6,8,16,1024]{3,2...) custom-call(s32[6]{0:T(128)S(1)} %stack.27.place, bf16[384,2048]{1,0:T(8,128)(2,1)} %a_ref.1, ...), custom_call_target="tpu_custom_call" | custom-call | flops 3422552064 | bytes 16000000 | tf_op jit(solution)/shard_map/project/pallas_call | solution.py:180
  24.4 9.4 %project.3 = (bf16[6,8,16,1024]{3,2,1,0:T(8,128)(2,1)S(1)}, f32[6,8,16,1024]{3,2,1,0:T(8,128)S(1)}, f32[6,8,16,128]{3,2,1,0:T(8,128)S(1)}, bf16[6,8,16,1024]{3,2...) custom-call(s32[6]{0:T(128)S(1)} %stack.27.place, ...), custom_call_target="tpu_custom_call", output_to_operand_aliasing={{0}: (8, {}), {1}: (9, {}), {2}: (10, {}), {3}: (11, {}), {... | custom-call | flops 3422552064 | bytes 16000000 | tf_op jit(solution)/shard_map/project/pallas_call | solution.py:180
  33.9 5.7 %attention.2 = (bf16[512,768]{1,0:T(8,128)(2,1)S(1)}, bf16[3,6,8,16,512]{4,3,2,1,0:T(8,128)(2,1)S(1)}) custom-call(bf16[6,8,16,3072]{3,2,1,0:T(8,128)(2,1)S(1)} %get-tuple-element.43.q_ref.k_ref.v_ref, bf16[6,8,16,3072]{3,2,1,0:T(8,128)(2,1)S(1)} %get-tuple-element.43.q_ref.k_ref.v_ref, bf16[6,8,16,3072]{3,2,1,0:T(8,128)(2,1)S(1)} %get-tuple-element.43.q_ref.k_ref.v_ref, ...), custom_call_target="tpu_custom_call" | custom-call | flops 2415919104 | bytes 6400000 | tf_op jit(solution)/shard_map/attention/pallas_call | solution.py:254
  39.6 5.4 %grad_rows.4 = (bf16[512,768]{1,0:T(8,128)(2,1)S(1)}, bf16[512,768]{1,0:T(8,128)(2,1)S(1)}, bf16[512,768]{1,0:T(8,128)(2,1)S(1)}, bf16[512,768]{1,0:T(8,128)(2,1)S(1)}) custom-call(s32[6]{0:T(128)S(1)} %stack.27.place, bf16[6,8,16,1024]{3,2,1,0:T(8,128)(2,1)S(1)} %get-tuple-element.45.refs_0_, bf16[3,6,8,16,512]{4,3,2,1,0:T(8,128)(2,1)S(1)} %get-tuple-element.44.refs_1_.refs_0_), custom_call_target="tpu_custom_call" | custom-call | flops 2415919104 | bytes 7145728 | tf_op jit(solution)/shard_map/grad_rows/pallas_call | solution.py:397
  45.0 5.7 %attention.3 = (bf16[512,768]{1,0:T(8,128)(2,1)S(1)}, bf16[3,6,8,16,512]{4,3,2,1,0:T(8,128)(2,1)S(1)}) custom-call(bf16[6,8,16,3072]{3,2,1,0:T(8,128)(2,1)S(1)} %get-tuple-element.43.q_ref.k_ref.v_ref, bf16[6,8,16,3072]{3,2,1,0:T(8,128)(2,1)S(1)} %get-tuple-element.43.q_ref.k_ref.v_ref, bf16[6,8,16,3072]{3,2,1,0:T(8,128)(2,1)S(1)} %get-tuple-element.43.q_ref.k_ref.v_ref, ...), custom_call_target="tpu_custom_call" | custom-call | flops 2415919104 | bytes 6400000 | tf_op jit(solution)/shard_map/attention/pallas_call | solution.py:254
  52.2 9.1 %input_grad.1 = (bf16[6,8,16,1024]{3,2,1,0:T(8,128)(2,1)S(1)}, f32[8,1024]{1,0:T(8,128)S(1)}) custom-call(bf16[3,6,8,16,512]{4,3,2,1,0:T(8,128)(2,1)} %copy-done.8, bf16[3,6,8,16,512]{4,3,2,1,0:T(8,128)(2,1)} %copy-done.6, bf16[1024,3072]{1,0:T(8,128)(2,1)S(1)} %bitcast.29, f32[6,8,16,1024]{3,2,1,0:T(8,128)S(1)} %get-tuple-element.48.refs_3_, ...), custom_call_target="tpu_custom_call" | custom-call | flops 4831838208 | bytes 20000000 | tf_op jit(solution)/shard_map/input_grad/pallas_call | solution.py:484
  61.3 6.3 %grad_rows.5 = (bf16[512,768]{1,0:T(8,128)(2,1)S(1)}, bf16[512,768]{1,0:T(8,128)(2,1)S(1)}, bf16[512,768]{1,0:T(8,128)(2,1)S(1)}, bf16[512,768]{1,0:T(8,128)(2,1)S(1)}) custom-call(s32[6]{0:T(128)S(1)} %stack.27.place, bf16[6,8,16,1024]{3,2,1,0:T(8,128)(2,1)S(1)} %get-tuple-element.51.refs_0_, ...), custom_call_target="tpu_custom_call" | custom-call | flops 2415919104 | bytes 7145728 | tf_op jit(solution)/shard_map/grad_rows/pallas_call | solution.py:397
  67.6 2.5 %back.1 = (bf16[96,2048]{1,0:T(8,128)(2,1)S(1)}, bf16[96,2048]{1,0:T(8,128)(2,1)S(1)}, bf16[96,2048]{1,0:T(8,128)(2,1)S(1)}, bf16[96,2048]{1,0:T(8,128)(2,1)S(1)}) custom-call(s32[6]{0:T(128)S(1)} %stack.27.place, bf16[6,8,16,1024]{3,2,1,0:T(8,128)(2,1)S(1)} %get-tuple-element.50.refs_1_.d_x_ref, bf16[1024,1024]{1,0:T(8,128)(2,1)S(1)} %copy-done.3, ...), custom_call_target="tpu_custom_call" | custom-call | flops 1610612736 | bytes 6000000 | tf_op jit(solution)/shard_map/back/pallas_call | solution.py:536
  70.3 5.2 %grad_rows.6 = (bf16[512,1536]{1,0:T(8,128)(2,1)S(1)}, bf16[512,1536]{1,0:T(8,128)(2,1)S(1)}) custom-call(s32[6]{0:T(128)S(1)} %stack.27.place, bf16[6,8,16,1024]{3,2,1,0:T(8,128)(2,1)S(1)} %get-tuple-element.45.refs_0_, bf16[3,6,8,16,512]{4,3,2,1,0:T(8,128)(2,1)S(1)} %copy-done.7), custom_call_target="tpu_custom_call" | custom-call | flops 2415919104 | bytes 7145728 | tf_op jit(solution)/shard_map/grad_rows/pallas_call | solution.py:397
  78.1 3.6 %grad_rows.7 = (bf16[512,1024]{1,0:T(8,128)(2,1)S(1)}, bf16[512,1024]{1,0:T(8,128)(2,1)S(1)}) custom-call(s32[6]{0:T(128)S(1)} %stack.27.place, bf16[512,768]{1,0:T(8,128)(2,1)S(1)} %get-tuple-element.66.refs_0_, bf16[512,768]{1,0:T(8,128)(2,1)S(1)} %get-tuple-element.67.refs_1_, bf16[6,8,16,1024]{3,2,1,0:T(8,128)(2,1)S(1)} %bitcast.31, ...), custom_call_target="tpu_custom_call" | custom-call | flops 1610612736 | bytes 6097152 | tf_op jit(solution)/shard_map/grad_rows/pallas_call | solution.py:397
  81.8 6.6 %collective-permute-done.4 = bf16[96,2048]{1,0:T(8,128)(2,1)S(1)} collective-permute-done((bf16[96,2048]{1,0:T(8,128)(2,1)S(1)}, bf16[96,2048]{1,0:T(8,128)(2,1)S(1)}, u32[]{:S(2)}, u32[]{:S(2)}) %collective-permute-start.4) | collective-permute-done | bytes 393248 | tf_op jit(solution)/shard_map/ppermute | solution.py:59
  88.4 6.7 %collective-permute-done.5 = bf16[96,2048]{1,0:T(8,128)(2,1)S(1)} collective-permute-done((bf16[96,2048]{1,0:T(8,128)(2,1)S(1)}, bf16[96,2048]{1,0:T(8,128)(2,1)S(1)}, u32[]{:S(2)}, u32[]{:S(2)}) %collective-permute-start.5) | collective-permute-done | bytes 393248 | tf_op jit(solution)/shard_map/ppermute | solution.py:59
  103.0 5.1 %collective-permute-done.17 = bf16[256,768]{1,0:T(8,128)(2,1)S(1)} collective-permute-done((bf16[256,768]{1,0:T(8,128)(2,1)S(1)}, bf16[256,768]{1,0:T(8,128)(2,1)S(1)}, u32[]{:S(2)}, u32[]{:S(2)}) %collective-permute-start.17) | collective-permute-done | bytes 393248 | tf_op jit(solution)/shard_map/ppermute | solution.py:59
  111.7 4.4 %collective-permute-done.12 = bf16[256,768]{1,0:T(8,128)(2,1)S(1)} collective-permute-done((bf16[256,768]{1,0:T(8,128)(2,1)S(1)}, bf16[256,768]{1,0:T(8,128)(2,1)S(1)}, u32[]{:S(2)}, u32[]{:S(2)}) %collective-permute-start.12) | collective-permute-done | bytes 393248 | tf_op jit(solution)/shard_map/ppermute | solution.py:59
  120.1 13.8 %collective-permute-done.18 = bf16[128,768]{1,0:T(8,128)(2,1)S(1)} collective-permute-done((bf16[128,768]{1,0:T(8,128)(2,1)S(1)}, bf16[128,768]{1,0:T(8,128)(2,1)S(1)}, u32[]{:S(2)}, u32[]{:S(2)}) %collective-permute-start.18) | collective-permute-done | bytes 196640 | tf_op jit(solution)/shard_map/ppermute | solution.py:59
  136.2 6.3 %collective-permute-done.8 = bf16[128,768]{1,0:T(8,128)(2,1)S(1)} collective-permute-done((bf16[128,768]{1,0:T(8,128)(2,1)S(1)}, bf16[128,768]{1,0:T(8,128)(2,1)S(1)}, u32[]{:S(2)}, u32[]{:S(2)}) %collective-permute-start.8) | collective-permute-done | bytes 196640 | tf_op jit(solution)/shard_map/ppermute | solution.py:59
  146.9 2.6 %collective-permute-done.9 = bf16[64,768]{1,0:T(8,128)(2,1)S(1)} collective-permute-done((bf16[64,768]{1,0:T(8,128)(2,1)S(1)}, bf16[64,768]{1,0:T(8,128)(2,1)S(1)}, u32[]{:S(2)}, u32[]{:S(2)}) %collective-permute-start.9) | collective-permute-done | bytes 98336 | tf_op jit(solution)/shard_map/ppermute | solution.py:59
  150.7 3.5 %collective-permute-done.10 = bf16[32,768]{1,0:T(8,128)(2,1)S(1)} collective-permute-done((bf16[32,768]{1,0:T(8,128)(2,1)S(1)}, bf16[32,768]{1,0:T(8,128)(2,1)S(1)}, u32[]{:S(2)}, u32[]{:S(2)}) %collective-permute-start.10) | collective-permute-done | bytes 49184 | tf_op jit(solution)/shard_map/ppermute | solution.py:59
  158.9 12.3 %collective-permute-done.25 = bf16[256,1536]{1,0:T(8,128)(2,1)S(1)} collective-permute-done((bf16[256,1536]{1,0:T(8,128)(2,1)S(1)}, bf16[256,1536]{1,0:T(8,128)(2,1)S(1)}, u32[]{:S(2)}, u32[]{:S(2)}) %collective-permute-start.25) | collective-permute-done | bytes 786464 | tf_op jit(solution)/shard_map/ppermute | solution.py:59
  174.1 5.2 %collective-permute-done.26 = bf16[128,1536]{1,0:T(8,128)(2,1)S(1)} collective-permute-done((bf16[128,1536]{1,0:T(8,128)(2,1)S(1)}, bf16[128,1536]{1,0:T(8,128)(2,1)S(1)}, u32[]{:S(2)}, u32[]{:S(2)}) %collective-permute-start.26) | collective-permute-done | bytes 393248 | tf_op jit(solution)/shard_map/ppermute | solution.py:59
  180.7 6.1 %collective-permute-done.30 = bf16[64,2560]{1,0:T(8,128)(2,1)S(1)} collective-permute-done((bf16[64,2560]{1,0:T(8,128)(2,1)S(1)}, bf16[64,2560]{1,0:T(8,128)(2,1)S(1)}, u32[]{:S(2)}, u32[]{:S(2)}) %collective-permute-start.30) | collective-permute-done | bytes 327712 | tf_op jit(solution)/shard_map/ppermute | solution.py:59
  187.4 7.4 %collective-permute-done.31 = bf16[32,2560]{1,0:T(8,128)(2,1)S(1)} collective-permute-done((bf16[32,2560]{1,0:T(8,128)(2,1)S(1)}, bf16[32,2560]{1,0:T(8,128)(2,1)S(1)}, u32[]{:S(2)}, u32[]{:S(2)}) %collective-permute-start.31) | collective-permute-done | bytes 163872 | tf_op jit(solution)/shard_map/ppermute | solution.py:59
  (132 shorter events, 45.3 us)
Async XLA Ops:
  3.1 10.7 %collective-permute-start.2 = (bf16[96,2048]{1,0:T(8,128)(2,1)}, bf16[96,2048]{1,0:T(8,128)(2,1)}, u32[]{:S(2)}, u32[]{:S(2)}) collective-permute-start(bf16[96,2048]{1,0:T(8,128)(2,1)} %get-tuple-element.84), channel_id=1, source_target_pairs={{0,1},{1,0},{2,3},{3,2},{4,5},{5,4},{6,7},{7,6},{8,9},{9,8},{10,11... | collective-permute-start | bytes 1179656 | tf_op jit(solution)/shard_map/ppermute | solution.py:59
  3.6 20.0 %collective-permute-start = (bf16[96,2048]{1,0:T(8,128)(2,1)}, bf16[96,2048]{1,0:T(8,128)(2,1)S(1)}, u32[]{:S(2)}, u32[]{:S(2)}) collective-permute-start(bf16[96,2048]{1,0:T(8,128)(2,1)} %get-tuple-element.86), channel_id=1, source_target_pairs={{0,2},{1,3},{2,0},{3,1},{4,6},{5,7},{6,4},{7,5},{8,10},{9,11},{10,... | collective-permute-start | bytes 1179656 | tf_op jit(solution)/shard_map/ppermute | solution.py:59
  6.1 18.3 %collective-permute-start.1 = (bf16[96,2048]{1,0:T(8,128)(2,1)}, bf16[96,2048]{1,0:T(8,128)(2,1)}, u32[]{:S(2)}, u32[]{:S(2)}) collective-permute-start(bf16[96,2048]{1,0:T(8,128)(2,1)} %get-tuple-element.85), channel_id=1, source_target_pairs={{0,3},{1,2},{2,1},{3,0},{4,7},{5,6},{6,5},{7,4},{8,11},{9,10},{10,... | collective-permute-start | bytes 1179656 | tf_op jit(solution)/shard_map/ppermute | solution.py:59
  70.1 11.6 %collective-permute-start.3 = (bf16[96,2048]{1,0:T(8,128)(2,1)S(1)}, bf16[96,2048]{1,0:T(8,128)(2,1)S(1)}, u32[]{:S(2)}, u32[]{:S(2)}) collective-permute-start(bf16[96,2048]{1,0:T(8,128)(2,1)S(1)} %get-tuple-element.55), channel_id=1, source_target_pairs={{0,1},{1,0},{2,3},{3,2},{4,5},{5,4},{6,7},{7,6},{8,9},{9,8},{10,11... | collective-permute-start | bytes 1179656 | tf_op jit(solution)/shard_map/ppermute | solution.py:59
  75.4 78.8 %collective-permute-start.24 = (bf16[512,1536]{1,0:T(8,128)(2,1)S(1)}, bf16[512,1536]{1,0:T(8,128)(2,1)S(1)}, u32[]{:S(2)}, u32[]{:S(2)}) collective-permute-start(bf16[512,1536]{1,0:T(8,128)(2,1)S(1)} %get-tuple-element.65), channel_id=1, source_target_pairs={{0,1},{1,0},{2,3},{3,2},{4,5},{5,4},{6,7},{7,6},{8,9},{9,8},{10,11... | collective-permute-start | bytes 4718600 | tf_op jit(solution)/shard_map/ppermute | solution.py:59
  75.9 19.9 %collective-permute-start.16 = (bf16[512,768]{1,0:T(8,128)(2,1)S(1)}, bf16[512,768]{1,0:T(8,128)(2,1)S(1)}, u32[]{:S(2)}, u32[]{:S(2)}) collective-permute-start(bf16[512,768]{1,0:T(8,128)(2,1)S(1)} %get-tuple-element.61), channel_id=1, source_target_pairs={{0,1},{1,0},{2,3},{3,2},{4,5},{5,4},{6,7},{7,6},{8,9},{9,8},{10,11... | collective-permute-start | bytes 2359304 | tf_op jit(solution)/shard_map/ppermute | solution.py:59
  76.0 20.1 %collective-permute-start.19 = (bf16[512,768]{1,0:T(8,128)(2,1)S(1)}, bf16[512,768]{1,0:T(8,128)(2,1)S(1)}, u32[]{:S(2)}, u32[]{:S(2)}) collective-permute-start(bf16[512,768]{1,0:T(8,128)(2,1)S(1)} %get-tuple-element.63), channel_id=1, source_target_pairs={{0,1},{1,0},{2,3},{3,2},{4,5},{5,4},{6,7},{7,6},{8,9},{9,8},{10,11... | collective-permute-start | bytes 2359304 | tf_op jit(solution)/shard_map/ppermute | solution.py:59
  76.4 12.0 %collective-permute-start.4 = (bf16[96,2048]{1,0:T(8,128)(2,1)S(1)}, bf16[96,2048]{1,0:T(8,128)(2,1)S(1)}, u32[]{:S(2)}, u32[]{:S(2)}) collective-permute-start(bf16[96,2048]{1,0:T(8,128)(2,1)S(1)} %get-tuple-element.56), channel_id=1, source_target_pairs={{0,2},{1,3},{2,0},{3,1},{4,6},{5,7},{6,4},{7,5},{8,10},{9,11},{10,... | collective-permute-start | bytes 1179656 | tf_op jit(solution)/shard_map/ppermute | solution.py:59
  81.7 13.4 %collective-permute-start.5 = (bf16[96,2048]{1,0:T(8,128)(2,1)S(1)}, bf16[96,2048]{1,0:T(8,128)(2,1)S(1)}, u32[]{:S(2)}, u32[]{:S(2)}) collective-permute-start(bf16[96,2048]{1,0:T(8,128)(2,1)S(1)} %get-tuple-element.57), channel_id=1, source_target_pairs={{0,3},{1,2},{2,1},{3,0},{4,7},{5,6},{6,5},{7,4},{8,11},{9,10},{10,... | collective-permute-start | bytes 1179656 | tf_op jit(solution)/shard_map/ppermute | solution.py:59
  88.4 9.7 %collective-permute-start.11 = (bf16[512,768]{1,0:T(8,128)(2,1)S(1)}, bf16[512,768]{1,0:T(8,128)(2,1)S(1)}, u32[]{:S(2)}, u32[]{:S(2)}) collective-permute-start(bf16[512,768]{1,0:T(8,128)(2,1)S(1)} %get-tuple-element.60), channel_id=1, source_target_pairs={{0,1},{1,0},{2,3},{3,2},{4,5},{5,4},{6,7},{7,6},{8,9},{9,8},{10,11... | collective-permute-start | bytes 2359304 | tf_op jit(solution)/shard_map/ppermute | solution.py:59
  96.1 12.1 %collective-permute-start.17 = (bf16[256,768]{1,0:T(8,128)(2,1)S(1)}, bf16[256,768]{1,0:T(8,128)(2,1)S(1)}, u32[]{:S(2)}, u32[]{:S(2)}) collective-permute-start(bf16[256,768]{1,0:T(8,128)(2,1)S(1)} %get-tuple-element.77), channel_id=1, source_target_pairs={{0,2},{1,3},{2,0},{3,1},{4,6},{5,7},{6,4},{7,5},{8,10},{9,11},{10,... | collective-permute-start | bytes 1179656 | tf_op jit(solution)/shard_map/ppermute | solution.py:59
  98.1 12.1 %collective-permute-start.20 = (bf16[256,768]{1,0:T(8,128)(2,1)S(1)}, bf16[256,768]{1,0:T(8,128)(2,1)S(1)}, u32[]{:S(2)}, u32[]{:S(2)}) collective-permute-start(bf16[256,768]{1,0:T(8,128)(2,1)S(1)} %get-tuple-element.79), channel_id=1, source_target_pairs={{0,4},{1,5},{2,6},{3,7},{4,0},{5,1},{6,2},{7,3},{8,12},{9,13},{10,... | collective-permute-start | bytes 1179656 | tf_op jit(solution)/shard_map/ppermute | solution.py:59
  99.9 16.3 %collective-permute-start.12 = (bf16[256,768]{1,0:T(8,128)(2,1)S(1)}, bf16[256,768]{1,0:T(8,128)(2,1)S(1)}, u32[]{:S(2)}, u32[]{:S(2)}) collective-permute-start(bf16[256,768]{1,0:T(8,128)(2,1)S(1)} %get-tuple-element.81), channel_id=1, source_target_pairs={{0,2},{1,3},{2,0},{3,1},{4,6},{5,7},{6,4},{7,5},{8,10},{9,11},{10,... | collective-permute-start | bytes 1179656 | tf_op jit(solution)/shard_map/ppermute | solution.py:59
  101.1 17.5 %collective-permute-start.7 = (bf16[256,768]{1,0:T(8,128)(2,1)S(1)}, bf16[256,768]{1,0:T(8,128)(2,1)S(1)}, u32[]{:S(2)}, u32[]{:S(2)}) collective-permute-start(bf16[256,768]{1,0:T(8,128)(2,1)S(1)} %get-tuple-element.83), channel_id=1, source_target_pairs={{0,4},{1,5},{2,6},{3,7},{4,0},{5,1},{6,2},{7,3},{8,12},{9,13},{10,... | collective-permute-start | bytes 1179656 | tf_op jit(solution)/shard_map/ppermute | solution.py:59
  108.2 48.7 %collective-permute-start.28 = (bf16[256,1024]{1,0:T(8,128)(2,1)S(1)}, bf16[256,1024]{1,0:T(8,128)(2,1)S(1)}, u32[]{:S(2)}, u32[]{:S(2)}) collective-permute-start(bf16[256,1024]{1,0:T(8,128)(2,1)S(1)} %get-tuple-element.73), channel_id=1, source_target_pairs={{0,4},{1,5},{2,6},{3,7},{4,0},{5,1},{6,2},{7,3},{8,12},{9,13},{10,... | collective-permute-start | bytes 1572872 | tf_op jit(solution)/shard_map/ppermute | solution.py:59
  110.1 23.9 %collective-permute-start.18 = (bf16[128,768]{1,0:T(8,128)(2,1)S(1)}, bf16[128,768]{1,0:T(8,128)(2,1)S(1)}, u32[]{:S(2)}, u32[]{:S(2)}) collective-permute-start(bf16[128,768]{1,0:T(8,128)(2,1)S(1)} %get-tuple-element.92), channel_id=1, source_target_pairs={{0,4},{1,5},{2,6},{3,7},{4,0},{5,1},{6,2},{7,3},{8,12},{9,13},{10,... | collective-permute-start | bytes 589832 | tf_op jit(solution)/shard_map/ppermute | solution.py:59
  116.1 19.5 %collective-permute-start.21 = (bf16[128,768]{1,0:T(8,128)(2,1)S(1)}, bf16[128,768]{1,0:T(8,128)(2,1)S(1)}, u32[]{:S(2)}, u32[]{:S(2)}) collective-permute-start(bf16[128,768]{1,0:T(8,128)(2,1)S(1)} %get-tuple-element.94), channel_id=1, source_target_pairs={{0,2},{1,3},{2,0},{3,1},{4,6},{5,7},{6,4},{7,5},{8,10},{9,11},{10,... | collective-permute-start | bytes 589832 | tf_op jit(solution)/shard_map/ppermute | solution.py:59
  118.5 25.9 %collective-permute-start.13 = (bf16[128,768]{1,0:T(8,128)(2,1)S(1)}, bf16[128,768]{1,0:T(8,128)(2,1)S(1)}, u32[]{:S(2)}, u32[]{:S(2)}) collective-permute-start(bf16[128,768]{1,0:T(8,128)(2,1)S(1)} %get-tuple-element.96), channel_id=1, source_target_pairs={{0,4},{1,5},{2,6},{3,7},{4,0},{5,1},{6,2},{7,3},{8,12},{9,13},{10,... | collective-permute-start | bytes 589832 | tf_op jit(solution)/shard_map/ppermute | solution.py:59
  134.0 8.6 %collective-permute-start.8 = (bf16[128,768]{1,0:T(8,128)(2,1)S(1)}, bf16[128,768]{1,0:T(8,128)(2,1)S(1)}, u32[]{:S(2)}, u32[]{:S(2)}) collective-permute-start(bf16[128,768]{1,0:T(8,128)(2,1)S(1)} %get-tuple-element.98), channel_id=1, source_target_pairs={{0,8},{1,9},{2,10},{3,11},{4,12},{5,13},{6,14},{7,15},{8,0},{9,1},... | collective-permute-start | bytes 589832 | tf_op jit(solution)/shard_map/ppermute | solution.py:59
  135.7 37.3 %collective-permute-start.22 = (bf16[64,1536]{1,0:T(8,128)(2,1)S(1)}, bf16[64,1536]{1,0:T(8,128)(2,1)S(1)}, u32[]{:S(2)}, u32[]{:S(2)}) collective-permute-start(bf16[64,1536]{1,0:T(8,128)(2,1)S(1)} %pad_maximum_fusion.1), channel_id=1, source_target_pairs={{0,8},{1,9},{2,10},{3,11},{4,12},{5,13},{6,14},{7,15},{8,0},{9,1},... | collective-permute-start | bytes 589832 | tf_op jit(solution)/shard_map/ppermute | solution.py:59
  154.6 16.6 %collective-permute-start.25 = (bf16[256,1536]{1,0:T(8,128)(2,1)S(1)}, bf16[256,1536]{1,0:T(8,128)(2,1)S(1)}, u32[]{:S(2)}, u32[]{:S(2)}) collective-permute-start(bf16[256,1536]{1,0:T(8,128)(2,1)S(1)} %get-tuple-element.71), channel_id=1, source_target_pairs={{0,2},{1,3},{2,0},{3,1},{4,6},{5,7},{6,4},{7,5},{8,10},{9,11},{10,... | collective-permute-start | bytes 2359304 | tf_op jit(solution)/shard_map/ppermute | solution.py:59
  157.1 17.0 %collective-permute-start.29 = (bf16[128,1024]{1,0:T(8,128)(2,1)S(1)}, bf16[128,1024]{1,0:T(8,128)(2,1)S(1)}, u32[]{:S(2)}, u32[]{:S(2)}) collective-permute-start(bf16[128,1024]{1,0:T(8,128)(2,1)S(1)} %get-tuple-element.88), channel_id=1, source_target_pairs={{0,2},{1,3},{2,0},{3,1},{4,6},{5,7},{6,4},{7,5},{8,10},{9,11},{10,... | collective-permute-start | bytes 786440 | tf_op jit(solution)/shard_map/ppermute | solution.py:59
  171.5 7.8 %collective-permute-start.26 = (bf16[128,1536]{1,0:T(8,128)(2,1)S(1)}, bf16[128,1536]{1,0:T(8,128)(2,1)S(1)}, u32[]{:S(2)}, u32[]{:S(2)}) collective-permute-start(bf16[128,1536]{1,0:T(8,128)(2,1)S(1)} %get-tuple-element.75), channel_id=1, source_target_pairs={{0,4},{1,5},{2,6},{3,7},{4,0},{5,1},{6,2},{7,3},{8,12},{9,13},{10,... | collective-permute-start | bytes 1179656 | tf_op jit(solution)/shard_map/ppermute | solution.py:59
  186.8 8.0 %collective-permute-start.31 = (bf16[32,2560]{1,0:T(8,128)(2,1)S(1)}, bf16[32,2560]{1,0:T(8,128)(2,1)S(1)}, u32[]{:S(2)}, u32[]{:S(2)}) collective-permute-start(bf16[32,2560]{1,0:T(8,128)(2,1)S(1)} %add_convert_fusion.26), channel_id=1, source_target_pairs={{0,16},{1,17},{2,18},{3,19},{4,20},{5,21},{6,22},{7,23},{8,24},{9,... | collective-permute-start | bytes 491528 | tf_op jit(solution)/shard_map/ppermute | solution.py:59
  (22 other events, 129.2 us)
